TPU v7x, 256 devices: a whole 4x4x8 slice. The times are simulated.
256 devices in a mesh: inst: 8 (over y_hi, x), space: 32 (over z, y_lo, core).
Axes of the slice: x: 4, y: 4 (y_hi: 2, y_lo: 2; y = y_hi * 2 + y_lo), z: 8, core: 2. Of those that a mesh axis runs over, the one named last changes fastest.
Arguments:
- psi_start: float32 [5, 8, 256, 1024], P(None, 'inst', 'space'), may hold values from -6 to 6
- density: float32 [8, 256, 1024], P('inst', 'space'), may hold values from 0.8 to 1.25
- velocity: float32 [3, 8, 256, 1024], P(None, 'inst', 'space'), may hold values from -0.6 to 0.6
- pressure: float32 [8, 256, 1024], P('inst', 'space'), may hold values from 0.5 to 1
- obs_pos: float32 [3, 512], P(None, 'space'), may hold values from -16 to 16, as said below
- obs_weight: float32 [2, 512], P(None, 'space'), may hold values from -0.6 to 0.6
- obs_harmonic: int32 [512], P('space'), may hold values from 1 to 3
- panel_pos: float32 [3, 65536], replicated, may hold values from -1 to 1
- panel_normal: float32 [3, 65536], P(None, 'space'), may hold values from -5 to 5
- panel_cell: int32 [65536], P('space'), may hold values from 0 to 8191
- plane_nbr: int32 [4, 1024], replicated, may hold values from 0 to 1023
Outputs:
- adjoint: float32 [5, 8, 256, 1024], P(None, 'inst', 'space')
Inputs may be any that keep to these rules, and one draw needn't show every extreme that they name: `obs_pos`: observers lie between 8 and 16 from the anchor, outside the panels' cube. panel_cell[q] is an index into the 8 x 1024 cells of the slot's owner, layer panel_cell[q] // 1024.
All inputs are finite; a program needn't handle non-finite values.
Results may differ from a plain program's by a relative error of at most 0.0001.
Values sent between devices are 32-bit elements; how exact they have to be, the bound alone decides.
A program may use at most 64 MiB of HBM per device.

v0:
```python
import functools
import math

import jax
import jax.numpy as jnp
from jax import lax
from jax.sharding import PartitionSpec as P
from jax.experimental import pallas as pl
from jax.experimental.pallas import tpu as pltpu

ITERS = 3


GAMMA = 1.4
KWAVE = 0.7
RADIUS = 10.0
TAU = 0.05
DISSIP = 0.25
OMEGA = 1.5
VISCO = 0.5


def padded_2(cells, sides, width):
    for axis, dim in sides:
        count = lax.axis_size(axis)
        head = lax.slice_in_dim(cells, 0, width, axis=dim)
        tail = lax.slice_in_dim(cells, cells.shape[dim] - width, cells.shape[dim], axis=dim)
        cells = jnp.concatenate(
            [
                lax.ppermute(tail, axis, [(i, (i + 1) % count) for i in range(count)]),
                cells,
                lax.ppermute(head, axis, [((i + 1) % count, i) for i in range(count)]),
            ],
            axis=dim,
        )
    return cells


def panel_block(observers, panels, time_now):
    delta = panels[:, None, :] - observers[:3, :, None]
    dist2 = jnp.sum(delta * delta, axis=0)
    dist = jnp.sqrt(dist2)
    harm = observers[5][:, None]
    phase = harm * (time_now - KWAVE * dist)
    amp = (
        (observers[3][:, None] * jnp.cos(phase) + observers[4][:, None] * jnp.sin(phase))
        * (RADIUS * RADIUS)
        / (dist2 * dist)
    )
    return jnp.sum(amp[None] * delta, axis=1)


def sensitivity(observers, panels, time_now):
    count = panels.shape[1]
    obs_count = observers.shape[1]
    block = math.gcd(count, max(128, 262144 // obs_count))
    split = panels.reshape(3, count // block, block).transpose(1, 0, 2)
    out = lax.map(lambda piece: panel_block(observers, piece, time_now), split)
    return out.transpose(1, 0, 2).reshape(3, count)


def conserved(density, velocity, pressure):
    moment = density[None] * velocity
    energy = pressure / (GAMMA - 1.0) + 0.5 * density * jnp.sum(velocity * velocity, axis=0)
    return jnp.concatenate([density[None], moment, energy[None]], axis=0)


def fluxes(state):
    dens = state[0]
    moment = state[1:4]
    energy = state[4]
    vel = moment / dens
    press = (GAMMA - 1.0) * (energy - 0.5 * jnp.sum(moment * vel, axis=0))
    result = []
    for axis_d in range(3):
        comps = [moment[axis_d]]
        for axis_e in range(3):
            term = moment[axis_e] * vel[axis_d]
            if axis_e == axis_d:
                term = term + press
            comps.append(term)
        comps.append((energy + press) * vel[axis_d])
        result.append(jnp.stack(comps))
    return tuple(result)


def spectral_coeff(offset, count):
    safe = jnp.where(offset == 0, 1.0, offset)
    angle = math.pi * safe / count
    even_odd_flag = 1.0 - 2.0 * jnp.mod(safe, 2.0)
    other = (
        -(OMEGA / 2.0) * even_odd_flag * jnp.cos(angle) / jnp.sin(angle)
        + VISCO * (OMEGA * OMEGA / 2.0) * even_odd_flag / jnp.sin(angle) ** 2
    )
    return jnp.where(offset == 0, VISCO * OMEGA * OMEGA * (count * count + 2.0) / 12.0, other)


def split_three(values):
    high = lax.reduce_precision(values, exponent_bits=8, mantissa_bits=7)
    rest = values - high
    middle = lax.reduce_precision(rest, exponent_bits=8, mantissa_bits=7)
    low = rest - middle
    return jnp.stack([high, middle, low]).astype(jnp.bfloat16)


def plane_gather(psi, onehot):
    comps, layers, plane = psi.shape
    parts = split_three(psi.reshape(comps * layers, plane))
    picked = jnp.einsum("pra,kba->kprb", parts, onehot,
                        preferred_element_type=jnp.float32)
    picked = (picked[:, 0] + picked[:, 1]) + picked[:, 2]
    return picked.reshape(onehot.shape[0], comps, layers, plane)


def cell_sum(weight, cell, layers, plane):
    by_layer = (cell // plane)[None, :] == jnp.arange(layers, dtype=jnp.int32)[:, None]
    spread = jnp.where(by_layer, weight[None, :], 0.0)
    picks = ((cell % plane)[:, None] == jnp.arange(plane, dtype=jnp.int32)[None, :]).astype(
        jnp.bfloat16
    )
    parts = split_three(spread)
    summed = jnp.einsum("plq,qb->plb", parts, picks, preferred_element_type=jnp.float32)
    return (summed[0] + summed[1]) + summed[2]


def instance_peers(count, inner, me, sign):
    outer = count // inner
    me_hi, me_lo = me // inner, me % inner
    peers = []
    for slot in range(1, count):
        hi, lo = slot // inner, slot % inner
        peers.append(((me_hi + sign * hi) % outer) * inner + (me_lo + sign * lo) % inner)
    return peers


def coupling_kernel(count, inner, psi_ref, coef_ref, out_ref, held, send_sem, recv_sem):
    me = lax.axis_index("inst")
    targets = instance_peers(count, inner, me, 1)
    barrier = pltpu.get_barrier_semaphore()
    for peer in targets:
        pl.semaphore_signal(barrier, inc=1, device_id={"inst": peer},
                            device_id_type=pl.DeviceIdType.MESH)
    pl.semaphore_wait(barrier, count - 1)
    copies = []
    for slot, peer in enumerate(targets):
        copy = pltpu.make_async_remote_copy(
            src_ref=psi_ref,
            dst_ref=held.at[slot],
            send_sem=send_sem.at[slot],
            recv_sem=recv_sem.at[slot],
            device_id={"inst": peer},
            device_id_type=pl.DeviceIdType.MESH,
        )
        copy.start()
        copies.append(copy)
    total = coef_ref[0] * psi_ref[...]
    for slot, copy in enumerate(copies):
        copy.wait()
        total = total + coef_ref[slot + 1] * held[slot]
    out_ref[...] = total


def instance_coupling(psi, row_entry, step):
    count = lax.axis_size("inst")
    me = lax.axis_index("inst")
    inner = 4 if count % 4 == 0 else count
    sources = instance_peers(count, inner, me, -1)
    coef = jnp.stack([row_entry[0]] + [row_entry[(me - s) % count] for s in sources])
    return pl.pallas_call(
        functools.partial(coupling_kernel, count, inner),
        out_shape=jax.ShapeDtypeStruct(psi.shape, psi.dtype),
        in_specs=[
            pl.BlockSpec(memory_space=pltpu.VMEM),
            pl.BlockSpec(memory_space=pltpu.SMEM),
        ],
        out_specs=pl.BlockSpec(memory_space=pltpu.VMEM),
        scratch_shapes=[
            pltpu.VMEM((count - 1, *psi.shape), psi.dtype),
            pltpu.SemaphoreType.DMA((count - 1,)),
            pltpu.SemaphoreType.DMA((count - 1,)),
        ],
        compiler_params=pltpu.CompilerParams(collective_id=step, has_side_effects=True),
        name=f"instance_coupling_{step}",
    )(psi, coef)


def shards(
    psi_start,
    density,
    velocity,
    pressure,
    obs_pos,
    obs_weight,
    obs_harmonic,
    panel_pos,
    panel_normal,
    panel_cell,
    plane_nbr,
):
    inst_count = lax.axis_size("inst")
    inst_id = lax.axis_index("inst")
    space_id = lax.axis_index("space")
    times = jnp.array([2.0 * math.pi * i / inst_count for i in range(inst_count)], jnp.float32)
    time_now = times[inst_id]
    local_obs = jnp.concatenate(
        [obs_pos, obs_weight, obs_harmonic[None].astype(jnp.float32)], axis=0
    )
    observers = lax.all_gather(local_obs, "space", axis=1, tiled=True)
    owned_count = panel_normal.shape[1]
    mine = lax.dynamic_slice_in_dim(panel_pos, space_id * owned_count, owned_count, 1)
    delta = mine[:, None, :] - observers[:3, :, None]
    dist2 = jnp.sum(delta * delta, axis=0)
    dist = jnp.sqrt(dist2)
    phase = observers[5][:, None] * (time_now - KWAVE * dist)
    amp = (
        (observers[3][:, None] * jnp.cos(phase) + observers[4][:, None] * jnp.sin(phase))
        * (RADIUS * RADIUS)
        / (dist2 * dist)
    )
    along = jnp.sum(delta * panel_normal[:, None, :], axis=0)
    weight = jnp.sum(amp * along, axis=0)
    layers = psi_start.shape[2]
    plane = psi_start.shape[3]
    wall = cell_sum(weight, panel_cell, layers, plane)
    dens = density[0]
    vel = velocity[:, 0]
    state = conserved(dens, vel, pressure[0])
    slope = jnp.concatenate(
        [0.5 * jnp.sum(vel * vel, axis=0)[None], -vel, jnp.ones_like(dens)[None]], axis=0
    ) * (GAMMA - 1.0)
    source = slope * wall[None]
    _, pull = jax.vjp(fluxes, state)
    onehot = (plane_nbr[:, :, None] == jnp.arange(plane, dtype=jnp.int32)[None, None, :]).astype(
        jnp.bfloat16
    )
    row_entry = spectral_coeff(
        jnp.arange(inst_count, dtype=jnp.int32).astype(jnp.float32), float(inst_count)
    )
    psi = psi_start[:, 0]
    for step in range(ITERS):
        padded = padded_2(psi, (("space", 1),), 1)
        minus_a = padded[:, :-2]
        plus_a = padded[:, 2:]
        plus_y, minus_y, plus_z, minus_z = plane_gather(psi, onehot)
        middle_point = pull(
            (0.5 * (minus_a - plus_a), 0.5 * (minus_y - plus_y), 0.5 * (minus_z - plus_z))
        )[0]
        spread = 6.0 * psi - (minus_a + plus_a + plus_y + minus_y + plus_z + minus_z)
        spectral_operator = instance_coupling(psi, row_entry, step)
        psi = psi - TAU * (middle_point + DISSIP * spread + spectral_operator + source)
    return psi[:, None]


def solution(mesh):
    placed = (
        P(None, "inst", "space", None),
        P("inst", "space", None),
        P(None, "inst", "space", None),
        P("inst", "space", None),
        P(None, "space"),
        P(None, "space"),
        P("space"),
        P(),
        P(None, "space"),
        P("space"),
        P(),
    )
    return jax.shard_map(
        shards,
        mesh=mesh,
        in_specs=placed,
        out_specs=P(None, "inst", "space", None),
        check_vma=False,
    )
```

profile of v0, /device:TPU:24, one launch (start us, length us, event | category | flops | bytes accessed | tf_op | source)
XLA Modules:
  0.0 178.5 jit_solution(1492395044522254339)
XLA Ops:
  0.0 1.1 fusion.77
  1.1 0.3 collective-permute-start.1
  1.4 0.3 collective-permute-start
  1.7 0.7 convert_bitcast_fusion
  2.4 0.7 maximum_bitcast_fusion.6
  3.1 37.1 %all-gather = f32[32,16,6]{1,2,0:T(8,128)S(1)} all-gather(f32[1,16,6]{1,2,0:T(8,128)S(1)} %maximum_bitcast_fusion.6), channel_id=1, replica_groups=mesh['inst'=8,'space'=32] {'space'}, dimensions={0}, use_global_device_ids=true | all-gather | bytes 12672 | tf_op jit(solution)/shard_map/all_gather | solution.py:208
  40.3 1.0 reduce-precision_convert_fusion.5
  41.6 0.7 add_select_fusion.1
  42.3 1.2 dynamic_slice.48
  43.5 8.2 %fusion.7 = (f32[512,2048]{1,0:T(8,128)S(1)}, f32[512,2048]{1,0:T(8,128)S(1)}) fusion(f32[3,512]{1,0:T(4,128)S(1)} %slice.213, f32[3,2048]{1,0:T(4,128)S(1)} %constant_dynamic-slice_fusion, f32[3,2048]{1,0:T(4,128)} %param.20), kind=kLoop, calls=%fused_computation.7 | loop fusion | flops 13631488 | bytes 8443904 | tf_op jit(solution)/shard_map/reduce_sum | solution.py:212
  51.8 19.3 %fusion.20 = f32[2048]{0:T(1024)S(1)} fusion(f32[512,2048]{1,0:T(8,128)S(1)} %get-tuple-element.6, f32[512,2048]{1,0:T(8,128)S(1)} %get-tuple-element.5, f32[512]{0:T(512)S(1)} %bitcast.201, f32[]{:T(128)} %bitcast.23, f32[512]{0:T(512)S(1)} %bitcast.202, f32[512]{0:T(512)S(1)} %bitcast.200), kind=kLoop, calls=%fused_computation.22 | loop fusion | flops 11532288 | bytes 8402948 | tf_op jit(solution)/shard_map/reduce_sum | solution.py:221
  71.1 1.6 fusion.13
  72.8 3.5 %fusion.21 = f32[4,3,40,1024]{3,2,1,0:T(8,128)S(1)} fusion(s32[4,1024]{1,0:T(4,128)S(1)} %copy-done.10, bf16[1,40,1024]{2,1,0:T(8,128)(2,1)S(1)} %get-tuple-element.123, bf16[1,40,1024]{2,1,0:T(8,128)(2,1)S(1)} %get-tuple-element.124, bf16[1,40,1024]{2,1,0:T(8,128)(2,1)S(1)} %get-tuple-element.122), kind=kOutput, calls=%fused_computation.23 | convolution fusion | flops 1011564544 | bytes 2228224 | tf_op jit(solution)/shard_map/pra,kba->kprb/dot_general | solution.py:109
  76.4 0.1 slice_add_fusion.4
  76.7 0.4 copy-done.8
  77.1 0.7 fusion.79
  77.8 5.7 %stack.15.coef_ref = f32[8]{0:T(128)} concatenate(f32[1]{0:T(128)} %get-tuple-element.162, f32[1]{0:T(128)} %get-tuple-element.161, f32[1]{0:T(128)} %get-tuple-element.160, f32[1]{0:T(128)} %get-tuple-element.159, f32[1]{0:T(128)} %get-tuple-element.158, f32[1]{0:T(128)} %get-tuple-element.157, f32[1]{0:T(128)} %get-tuple-element.156, f32[1]{0:T(128)} %get-tuple-element.155), dimensions={0} | concatenate | bytes 64 | tf_op jit(solution)/shard_map/stack | solution.py:168
  83.6 26.8 %instance_coupling_0.1 = f32[5,8,1024]{2,1,0:T(8,128)} custom-call(f32[5,8,1024]{2,1,0:T(8,128)} %bitcast.190, f32[8]{0:T(128)} %stack.15.coef_ref), custom_call_target="tpu_custom_call" | custom-call | tf_op jit(solution)/shard_map/instance_coupling_0/pallas_call | solution.py:169
  110.6 0.1 fusion.53
  110.8 1.1 reduce-precision_convert_fusion.3
  111.9 3.5 %fusion.24 = f32[4,3,40,1024]{3,2,1,0:T(8,128)S(1)} fusion(s32[4,1024]{1,0:T(4,128)S(1)} %copy-done.10, bf16[1,40,1024]{2,1,0:T(8,128)(2,1)S(1)} %get-tuple-element.109, bf16[1,40,1024]{2,1,0:T(8,128)(2,1)S(1)} %get-tuple-element.108, bf16[1,40,1024]{2,1,0:T(8,128)(2,1)S(1)} %get-tuple-element.17), kind=kOutput, calls=%fused_computation.24 | convolution fusion | flops 1011564544 | bytes 2228224 | tf_op jit(solution)/shard_map/pra,kba->kprb/dot_general | solution.py:109
  115.5 0.1 slice_add_fusion.2
  115.7 0.5 collective-permute-start.2
  116.3 26.6 %instance_coupling_1.1 = f32[5,8,1024]{2,1,0:T(8,128)} custom-call(f32[5,8,1024]{2,1,0:T(8,128)} %copy-done.3, f32[8]{0:T(128)} %stack.15.coef_ref), custom_call_target="tpu_custom_call" | custom-call | tf_op jit(solution)/shard_map/instance_coupling_1/pallas_call | solution.py:169
  143.0 1.1 subtract_multiply_fusion.5
  144.3 1.1 reduce-precision_convert_fusion.1
  145.5 1.7 collective-permute-start.5
  147.3 3.5 %fusion.27 = f32[4,3,40,1024]{3,2,1,0:T(8,128)S(1)} fusion(s32[4,1024]{1,0:T(4,128)S(1)} %copy-done.10, bf16[1,40,1024]{2,1,0:T(8,128)(2,1)S(1)} %get-tuple-element.94, bf16[1,40,1024]{2,1,0:T(8,128)(2,1)S(1)} %get-tuple-element.93, bf16[1,40,1024]{2,1,0:T(8,128)(2,1)S(1)} %get-tuple-element.11), kind=kOutput, calls=%fused_computation.25 | convolution fusion | flops 1011564544 | bytes 2228224 | tf_op jit(solution)/shard_map/pra,kba->kprb/dot_general | solution.py:109
  150.8 0.1 slice_add_fusion
  151.1 24.4 %instance_coupling_2.1 = f32[5,8,1024]{2,1,0:T(8,128)} custom-call(f32[5,8,1024]{2,1,0:T(8,128)} %copy-done.1, f32[8]{0:T(128)} %stack.15.coef_ref), custom_call_target="tpu_custom_call" | custom-call | tf_op jit(solution)/shard_map/instance_coupling_2/pallas_call | solution.py:169
  175.5 1.1 subtract_multiply_fusion.2
  176.8 1.7 subtract_bitcast_fusion
  (68 shorter events, 1.4 us)
Async XLA Ops:
  0.0 42.3 %copy-start = (f32[3,65536]{1,0:T(4,128)S(1)}, f32[3,65536]{1,0:T(4,128)}, u32[]{:S(2)}) copy-start(f32[3,65536]{1,0:T(4,128)} %param.19) | copy-start | bytes 2359300
  1.1 109.3 %collective-permute-start.1 = (f32[5,1,1024]{2,1,0:T(1,128)S(1)}, f32[5,1,1024]{2,1,0:T(1,128)S(1)}, u32[]{:S(2)}, u32[]{:S(2)}) collective-permute-start(f32[5,1,1024]{2,1,0:T(1,128)S(1)} %get-tuple-element.121), channel_id=1, source_target_pairs={{1,0},{2,1},{3,2},{4,3},{5,4},{6,5},{7,6},{8,7},{9,8},{10,9},{11,1... | collective-permute-start | bytes 61448 | tf_op jit(solution)/shard_map/ppermute | solution.py:32
  1.4 109.0 %collective-permute-start = (f32[5,1,1024]{2,1,0:T(1,128)S(1)}, f32[5,1,1024]{2,1,0:T(1,128)S(1)}, u32[]{:S(2)}, u32[]{:S(2)}) collective-permute-start(f32[5,1,1024]{2,1,0:T(1,128)S(1)} %get-tuple-element.120), channel_id=1, source_target_pairs={{0,1},{1,2},{2,3},{3,4},{4,5},{5,6},{6,7},{7,8},{8,9},{9,10},{10,1... | collective-permute-start | bytes 61448 | tf_op jit(solution)/shard_map/ppermute | solution.py:30
  51.8 20.9 %copy-start.10 = (s32[4,1024]{1,0:T(4,128)S(1)}, s32[4,1024]{1,0:T(4,128)}, u32[]{:S(2)}) copy-start(s32[4,1024]{1,0:T(4,128)} %param.22) | copy-start | bytes 49156
  72.7 3.8 %copy-start.6 = (f32[1,8,1024]{2,1,0:T(8,128)S(1)}, f32[1,8,1024]{2,1,0:T(8,128)}, u32[]{:S(2)}) copy-start(f32[1,8,1024]{2,1,0:T(8,128)} %param.13) | copy-start | bytes 98308
  72.8 3.8 %copy-start.7 = (f32[3,1,8,1024]{3,2,1,0:T(8,128)S(1)}, f32[3,1,8,1024]{3,2,1,0:T(8,128)}, u32[]{:S(2)}) copy-start(f32[3,1,8,1024]{3,2,1,0:T(8,128)} %param.14) | copy-start | bytes 294916
  76.3 0.8 copy-start.8
  76.3 34.1 %copy-start.5 = (f32[5,1,8,1024]{3,2,1,0:T(8,128)S(1)}, f32[5,1,8,1024]{3,2,1,0:T(8,128)}, u32[]{:S(2)}) copy-start(f32[5,1,8,1024]{3,2,1,0:T(8,128)} %param.12) | copy-start | bytes 491524
  76.3 34.3 %copy-start.9 = (pred[3]{0:T(512)(128)(4,1)S(1)}, pred[3]{0:T(512)(128)(4,1)}, u32[]{:S(2)}) copy-start(pred[3]{0:T(512)(128)(4,1)} %constant.260.clone.1) | copy-start | bytes 13
  111.8 3.6 %copy-start.3 = (f32[5,8,1024]{2,1,0:T(8,128)}, f32[5,8,1024]{2,1,0:T(8,128)S(1)}, u32[]{:S(2)}) copy-start(f32[5,8,1024]{2,1,0:T(8,128)S(1)} %get-tuple-element.18.psi_ref) | copy-start | bytes 491524
  115.6 28.6 %copy-start.4 = (f32[5,8,1024]{2,1,0:T(8,128)S(1)}, f32[5,8,1024]{2,1,0:T(8,128)}, u32[]{:S(2)}) copy-start(f32[5,8,1024]{2,1,0:T(8,128)} %copy-done.3) | copy-start | bytes 491524
  115.6 27.3 %collective-permute-start.3 = (f32[5,1,1024]{2,1,0:T(1,128)S(1)}, f32[5,1,1024]{2,1,0:T(1,128)S(1)}, u32[]{:S(2)}, u32[]{:S(2)}) collective-permute-start(f32[5,1,1024]{2,1,0:T(1,128)S(1)} %get-tuple-element.107), channel_id=1, source_target_pairs={{1,0},{2,1},{3,2},{4,3},{5,4},{6,5},{7,6},{8,7},{9,8},{10,9},{11,1... | collective-permute-start | bytes 61448 | tf_op jit(solution)/shard_map/ppermute | solution.py:32
  115.7 27.2 %collective-permute-start.2 = (f32[5,1,1024]{2,1,0:T(1,128)S(1)}, f32[5,1,1024]{2,1,0:T(1,128)S(1)}, u32[]{:S(2)}, u32[]{:S(2)}) collective-permute-start(f32[5,1,1024]{2,1,0:T(1,128)S(1)} %get-tuple-element.106), channel_id=1, source_target_pairs={{0,1},{1,2},{2,3},{3,4},{4,5},{5,6},{6,7},{7,8},{8,9},{9,10},{10,1... | collective-permute-start | bytes 61448 | tf_op jit(solution)/shard_map/ppermute | solution.py:30
  145.4 5.5 %copy-start.1 = (f32[5,8,1024]{2,1,0:T(8,128)}, f32[5,8,1024]{2,1,0:T(8,128)S(1)}, u32[]{:S(2)}) copy-start(f32[5,8,1024]{2,1,0:T(8,128)S(1)} %get-tuple-element.12.psi_ref) | copy-start | bytes 491524
  145.4 30.0 %collective-permute-start.4 = (f32[5,1,1024]{2,1,0:T(1,128)S(1)}, f32[5,1,1024]{2,1,0:T(1,128)S(1)}, u32[]{:S(2)}, u32[]{:S(2)}) collective-permute-start(f32[5,1,1024]{2,1,0:T(1,128)S(1)} %get-tuple-element.96), channel_id=1, source_target_pairs={{0,1},{1,2},{2,3},{3,4},{4,5},{5,6},{6,7},{7,8},{8,9},{9,10},{10,1... | collective-permute-start | bytes 61448 | tf_op jit(solution)/shard_map/ppermute | solution.py:30
  145.5 29.9 %collective-permute-start.5 = (f32[5,1,1024]{2,1,0:T(1,128)S(1)}, f32[5,1,1024]{2,1,0:T(1,128)S(1)}, u32[]{:S(2)}, u32[]{:S(2)}) collective-permute-start(f32[5,1,1024]{2,1,0:T(1,128)S(1)} %get-tuple-element.95), channel_id=1, source_target_pairs={{1,0},{2,1},{3,2},{4,3},{5,4},{6,5},{7,6},{8,7},{9,8},{10,9},{11,1... | collective-permute-start | bytes 61448 | tf_op jit(solution)/shard_map/ppermute | solution.py:32
  151.0 25.8 %copy-start.2 = (f32[5,8,1024]{2,1,0:T(8,128)S(1)}, f32[5,8,1024]{2,1,0:T(8,128)}, u32[]{:S(2)}) copy-start(f32[5,8,1024]{2,1,0:T(8,128)} %copy-done.1) | copy-start | bytes 491524
where the time goes:
time: 179 us
  Pallas kernels  77.9 us (44%)
  other arithmetic  38 us (21%)
  blocking collectives  37.1 us (21%)
  matrix products  12.2 us (7%)
  local copies, waits for them, and re-layouts  9.49 us (5%)
  starting transfers between devices  2.98 us (2%)
    pallas_call x3, Pallas kernels, instance_coupling(): pl.pallas_call(functools.partial(coupling_kernel, count, inner), out_shap...  77.9 us
    all_gather x1, blocking collectives, shards(): observers = lax.all_gather(local_obs, 'space', axis=1, tiled=True)  37.1 us
    reduce_sum x1, other arithmetic, shards(): weight = jnp.sum(amp * along, axis=0)  19.3 us
    dot_general x3, matrix products, plane_gather(): jnp.einsum('pra,kba->kprb', parts, onehot, preferred_element_type=jnp.flo...  10.6 us
    reduce_sum x1, other arithmetic, shards(): dist2 = jnp.sum(delta * delta, axis=0)  8.23 us
    another operation x1, local copies, waits for them, and re-layouts, instance_coupling(): jnp.stack([row_entry[0]] + [row_entry[(me - s) % count] for s in sources])  5.73 us
  transfers between devices with their start and end apart: 6, of which 0 were waited for; matrix products, arithmetic and copies ran while one was open for 27% of the time, Pallas kernels for 44%

commit v1 on v0

--- a/solution.py
+++ b/solution.py
@@ -123,49 +123,62 @@
     return (summed[0] + summed[1]) + summed[2]
 
 
-def instance_peers(count, inner, me, sign):
+def greet(axis, peers):
+    barrier = pltpu.get_barrier_semaphore()
+    for peer in peers:
+        pl.semaphore_signal(barrier, inc=1, device_id={axis: peer},
+                            device_id_type=pl.DeviceIdType.MESH)
+    pl.semaphore_wait(barrier, len(peers))
+
+
+def coupling_kernel(count, inner, psi_ref, table_ref, out_ref, held, outbox, inbox,
+                    ring_send, ring_recv, cross_send, cross_recv):
     outer = count // inner
+    me = lax.axis_index("inst")
     me_hi, me_lo = me // inner, me % inner
-    peers = []
-    for slot in range(1, count):
-        hi, lo = slot // inner, slot % inner
-        peers.append(((me_hi + sign * hi) % outer) * inner + (me_lo + sign * lo) % inner)
-    return peers
-
-
-def coupling_kernel(count, inner, psi_ref, coef_ref, out_ref, held, send_sem, recv_sem):
-    me = lax.axis_index("inst")
-    targets = instance_peers(count, inner, me, 1)
-    barrier = pltpu.get_barrier_semaphore()
-    for peer in targets:
-        pl.semaphore_signal(barrier, inc=1, device_id={"inst": peer},
-                            device_id_type=pl.DeviceIdType.MESH)
-    pl.semaphore_wait(barrier, count - 1)
+    ring = [me_hi * inner + (me_lo + d) % inner for d in range(1, inner)]
+    ring_from = [me_hi * inner + (me_lo - d) % inner for d in range(1, inner)]
+    partners = [((me_hi + h) % outer) * inner + me_lo for h in range(1, outer)]
+    greet("inst", ring + partners)
+
+    def coef(row, col):
+        return table_ref[(row - col) % count]
+
     copies = []
-    for slot, peer in enumerate(targets):
+    for slot, peer in enumerate(ring):
         copy = pltpu.make_async_remote_copy(
-            src_ref=psi_ref,
-            dst_ref=held.at[slot],
-            send_sem=send_sem.at[slot],
-            recv_sem=recv_sem.at[slot],
-            device_id={"inst": peer},
-            device_id_type=pl.DeviceIdType.MESH,
-        )
+            src_ref=psi_ref, dst_ref=held.at[slot], send_sem=ring_send.at[slot],
+            recv_sem=ring_recv.at[slot], device_id={"inst": peer},
+            device_id_type=pl.DeviceIdType.MESH)
         copy.start()
         copies.append(copy)
-    total = coef_ref[0] * psi_ref[...]
-    for slot, copy in enumerate(copies):
+    for copy in copies:
         copy.wait()
-        total = total + coef_ref[slot + 1] * held[slot]
+    cross = []
+    for slot, partner in enumerate(partners):
+        part = coef(partner, me) * psi_ref[...]
+        for d, source in enumerate(ring_from):
+            part = part + coef(partner, source) * held[d]
+        outbox[slot] = part
+        copy = pltpu.make_async_remote_copy(
+            src_ref=outbox.at[slot], dst_ref=inbox.at[slot], send_sem=cross_send.at[slot],
+            recv_sem=cross_recv.at[slot], device_id={"inst": partner},
+            device_id_type=pl.DeviceIdType.MESH)
+        copy.start()
+        cross.append(copy)
+    total = coef(me, me) * psi_ref[...]
+    for d, source in enumerate(ring_from):
+        total = total + coef(me, source) * held[d]
+    for slot, copy in enumerate(cross):
+        copy.wait()
+        total = total + inbox[slot]
     out_ref[...] = total
 
 
-def instance_coupling(psi, row_entry, step):
+def instance_coupling(psi, table, step):
     count = lax.axis_size("inst")
-    me = lax.axis_index("inst")
     inner = 4 if count % 4 == 0 else count
-    sources = instance_peers(count, inner, me, -1)
-    coef = jnp.stack([row_entry[0]] + [row_entry[(me - s) % count] for s in sources])
+    outer = count // inner
     return pl.pallas_call(
         functools.partial(coupling_kernel, count, inner),
         out_shape=jax.ShapeDtypeStruct(psi.shape, psi.dtype),
@@ -175,13 +188,52 @@
         ],
         out_specs=pl.BlockSpec(memory_space=pltpu.VMEM),
         scratch_shapes=[
-            pltpu.VMEM((count - 1, *psi.shape), psi.dtype),
+            pltpu.VMEM((inner - 1, *psi.shape), psi.dtype),
+            pltpu.VMEM((max(outer - 1, 1), *psi.shape), psi.dtype),
+            pltpu.VMEM((max(outer - 1, 1), *psi.shape), psi.dtype),
+            pltpu.SemaphoreType.DMA((inner - 1,)),
+            pltpu.SemaphoreType.DMA((inner - 1,)),
+            pltpu.SemaphoreType.DMA((max(outer - 1, 1),)),
+            pltpu.SemaphoreType.DMA((max(outer - 1, 1),)),
+        ],
+        compiler_params=pltpu.CompilerParams(collective_id=step, has_side_effects=True),
+        name=f"instance_coupling_{step}",
+    )(psi, table)
+
+
+def gather_kernel(count, block_ref, out_ref, held, send_sem, recv_sem):
+    me = lax.axis_index("space")
+    peers = [(me + d) % count for d in range(1, count)]
+    greet("space", peers)
+    copies = []
+    for slot, peer in enumerate(peers):
+        copy = pltpu.make_async_remote_copy(
+            src_ref=block_ref, dst_ref=held.at[me], send_sem=send_sem.at[slot],
+            recv_sem=recv_sem.at[slot], device_id={"space": peer},
+            device_id_type=pl.DeviceIdType.MESH)
+        copy.start()
+        copies.append(copy)
+    for copy in copies:
+        copy.wait()
+    held[me] = block_ref[...]
+    out_ref[...] = held[...]
+
+
+def space_gather(block, collective):
+    count = lax.axis_size("space")
+    return pl.pallas_call(
+        functools.partial(gather_kernel, count),
+        out_shape=jax.ShapeDtypeStruct((count, *block.shape), block.dtype),
+        in_specs=[pl.BlockSpec(memory_space=pltpu.VMEM)],
+        out_specs=pl.BlockSpec(memory_space=pltpu.VMEM),
+        scratch_shapes=[
+            pltpu.VMEM((count, *block.shape), block.dtype),
             pltpu.SemaphoreType.DMA((count - 1,)),
             pltpu.SemaphoreType.DMA((count - 1,)),
         ],
-        compiler_params=pltpu.CompilerParams(collective_id=step, has_side_effects=True),
-        name=f"instance_coupling_{step}",
-    )(psi, coef)
+        compiler_params=pltpu.CompilerParams(collective_id=collective, has_side_effects=True),
+        name="space_gather",
+    )(block)
 
 
 def shards(
@@ -205,7 +257,11 @@
     local_obs = jnp.concatenate(
         [obs_pos, obs_weight, obs_harmonic[None].astype(jnp.float32)], axis=0
     )
-    observers = lax.all_gather(local_obs, "space", axis=1, tiled=True)
+    rows, per = local_obs.shape
+    assert rows <= 8 and per <= 128
+    packed = jnp.zeros((8, 128), jnp.float32).at[:rows, :per].set(local_obs)
+    stacked = space_gather(packed, ITERS)
+    observers = stacked[:, :rows, :per].transpose(1, 0, 2).reshape(rows, -1)
     owned_count = panel_normal.shape[1]
     mine = lax.dynamic_slice_in_dim(panel_pos, space_id * owned_count, owned_count, 1)
     delta = mine[:, None, :] - observers[:3, :, None]

time: 179 us -> 136 us (0.76)
  the two profiles are of different devices: /device:TPU:24 before, /device:TPU:8 now
where the time goes in v1:
time: 136 us
  Pallas kernels  76.1 us (56%)
  other arithmetic  39.2 us (29%)
  matrix products  12.3 us (9%)
  local copies, waits for them, and re-layouts  4.36 us (3%)
  starting transfers between devices  3.2 us (2%)
    pallas_call x3, Pallas kernels, instance_coupling(): pl.pallas_call(functools.partial(coupling_kernel, count, inner), out_shap...  58.5 us
    reduce_sum x1, other arithmetic, shards(): weight = jnp.sum(amp * along, axis=0)  19.3 us
    pallas_call x1, Pallas kernels, space_gather(): pl.pallas_call(functools.partial(gather_kernel, count), out_shape=jax.Sha...  17.6 us
    dot_general x3, matrix products, plane_gather(): jnp.einsum('pra,kba->kprb', parts, onehot, preferred_element_type=jnp.flo...  10.7 us
    reduce_sum x1, other arithmetic, shards(): dist2 = jnp.sum(delta * delta, axis=0)  8.23 us
    another operation x6, other arithmetic  3.18 us
  transfers between devices with their start and end apart: 6, of which 0 were waited for; matrix products, arithmetic and copies ran while one was open for 32% of the time, Pallas kernels for 56%

profile of v1, /device:TPU:8, one launch (start us, length us, event | category | flops | bytes accessed | tf_op | source)
XLA Modules:
  0.0 135.7 jit_solution(14541395508004131236)
XLA Ops:
  0.0 1.1 fusion.77
  1.2 0.5 collective-permute-start
  1.7 0.7 convert_bitcast_fusion
  2.4 1.3 select_maximum_fusion.block_ref
  3.7 17.6 %space_gather.1 = f32[32,8,128]{2,1,0:T(8,128)} custom-call(f32[8,128]{1,0:T(8,128)} %select_maximum_fusion.block_ref), custom_call_target="tpu_custom_call" | custom-call | tf_op jit(solution)/shard_map/space_gather/pallas_call | solution.py:224
  21.2 0.9 slice_bitcast_fusion.12
  22.2 0.1 slice_reduce_fusion.2
  22.3 1.0 reduce-precision_convert_fusion.5
  23.3 0.7 add_select_fusion.1
  24.4 1.2 dynamic_slice.6
  25.6 8.2 %fusion.7 = (f32[512,2048]{1,0:T(8,128)S(1)}, f32[512,2048]{1,0:T(8,128)S(1)}) fusion(f32[3,512]{1,0:T(4,128)S(1)} %sub.198, f32[3,2048]{1,0:T(4,128)S(1)} %constant_dynamic-slice_fusion, f32[3,2048]{1,0:T(4,128)} %param.22), kind=kLoop, calls=%fused_computation.7 | loop fusion | flops 13631488 | bytes 8443904 | tf_op jit(solution)/shard_map/reduce_sum | solution.py:268
  33.9 19.3 %fusion.20 = f32[2048]{0:T(1024)S(1)} fusion(f32[512,2048]{1,0:T(8,128)S(1)} %get-tuple-element.21, f32[512,2048]{1,0:T(8,128)S(1)} %get-tuple-element.20, f32[512]{0:T(512)S(1)} %mul.692, f32[]{:T(128)} %bitcast.19, f32[512]{0:T(512)S(1)} %mul.684, f32[512]{0:T(512)S(1)} %mul.682), kind=kLoop, calls=%fused_computation.22 | loop fusion | flops 11532288 | bytes 8402948 | tf_op jit(solution)/shard_map/reduce_sum | solution.py:277
  53.2 1.6 %fusion.13 = f32[3,8,1024]{2,1,0:T(8,128)S(1)} fusion(s32[2048]{0:T(1024)S(1)} %get-tuple-element.166, bf16[1,8,2048]{2,1,0:T(8,128)(2,1)S(1)} %get-tuple-element.164, bf16[1,8,2048]{2,1,0:T(8,128)(2,1)S(1)} %get-tuple-element.163, bf16[1,8,2048]{2,1,0:T(8,128)(2,1)S(1)} %get-tuple-element.162), kind=kOutput, calls=%fused_computation.14 | convolution fusion | flops 102858752 | bytes 204800 | tf_op jit(solution)/shard_map/plq,qb->plb/dot_general | solution.py:122
  54.8 3.6 %fusion.21 = f32[4,3,40,1024]{3,2,1,0:T(8,128)S(1)} fusion(s32[4,1024]{1,0:T(4,128)S(1)} %copy-done.10, bf16[1,40,1024]{2,1,0:T(8,128)(2,1)S(1)} %get-tuple-element.138, bf16[1,40,1024]{2,1,0:T(8,128)(2,1)S(1)} %get-tuple-element.139, bf16[1,40,1024]{2,1,0:T(8,128)(2,1)S(1)} %get-tuple-element.137), kind=kOutput, calls=%fused_computation.23 | convolution fusion | flops 1011564544 | bytes 2228224 | tf_op jit(solution)/shard_map/pra,kba->kprb/dot_general | solution.py:109
  58.4 0.1 slice_add_fusion.4
  58.7 0.5 copy-done.8
  59.2 0.6 compare_select_fusion.table_ref
  59.8 19.6 %instance_coupling_0.1 = f32[5,8,1024]{2,1,0:T(8,128)} custom-call(f32[5,8,1024]{2,1,0:T(8,128)} %bitcast.182, f32[8]{0:T(128)} %compare_select_fusion.table_ref), custom_call_target="tpu_custom_call" | custom-call | tf_op jit(solution)/shard_map/instance_coupling_0/pallas_call | solution.py:182
  79.8 1.1 reduce-precision_convert_fusion.3
  81.0 3.6 %fusion.24 = f32[4,3,40,1024]{3,2,1,0:T(8,128)S(1)} fusion(s32[4,1024]{1,0:T(4,128)S(1)} %copy-done.10, bf16[1,40,1024]{2,1,0:T(8,128)(2,1)S(1)} %get-tuple-element.124, bf16[1,40,1024]{2,1,0:T(8,128)(2,1)S(1)} %get-tuple-element.123, bf16[1,40,1024]{2,1,0:T(8,128)(2,1)S(1)} %get-tuple-element.32), kind=kOutput, calls=%fused_computation.24 | convolution fusion | flops 1011564544 | bytes 2228224 | tf_op jit(solution)/shard_map/pra,kba->kprb/dot_general | solution.py:109
  84.5 0.1 slice_add_fusion.2
  84.8 0.5 collective-permute-start.2
  85.4 20.9 %instance_coupling_1.1 = f32[5,8,1024]{2,1,0:T(8,128)} custom-call(f32[5,8,1024]{2,1,0:T(8,128)} %copy-done.3, f32[8]{0:T(128)} %compare_select_fusion.table_ref), custom_call_target="tpu_custom_call" | custom-call | tf_op jit(solution)/shard_map/instance_coupling_1/pallas_call | solution.py:182
  106.3 1.1 subtract_multiply_fusion.5
  107.6 1.1 reduce-precision_convert_fusion.1
  108.8 0.3 collective-permute-start.4
  109.1 1.7 %collective-permute-start.5 = (f32[5,1,1024]{2,1,0:T(1,128)S(1)}, f32[5,1,1024]{2,1,0:T(1,128)S(1)}, u32[]{:S(2)}, u32[]{:S(2)}) collective-permute-start(f32[5,1,1024]{2,1,0:T(1,128)S(1)} %get-tuple-element.110), channel_id=1, source_target_pairs={{1,0},{2,1},{3,2},{4,3},{5,4},{6,5},{7,6},{8,7},{9,8},{10,9},{11,1... | collective-permute-start | bytes 61448 | tf_op jit(solution)/shard_map/ppermute | solution.py:32
  110.8 3.6 %fusion.27 = f32[4,3,40,1024]{3,2,1,0:T(8,128)S(1)} fusion(s32[4,1024]{1,0:T(4,128)S(1)} %copy-done.10, bf16[1,40,1024]{2,1,0:T(8,128)(2,1)S(1)} %get-tuple-element.109, bf16[1,40,1024]{2,1,0:T(8,128)(2,1)S(1)} %get-tuple-element.108, bf16[1,40,1024]{2,1,0:T(8,128)(2,1)S(1)} %get-tuple-element.26), kind=kOutput, calls=%fused_computation.25 | convolution fusion | flops 1011564544 | bytes 2228224 | tf_op jit(solution)/shard_map/pra,kba->kprb/dot_general | solution.py:109
  114.4 0.1 slice_add_fusion
  114.6 18.0 %instance_coupling_2.1 = f32[5,8,1024]{2,1,0:T(8,128)} custom-call(f32[5,8,1024]{2,1,0:T(8,128)} %copy-done.1, f32[8]{0:T(128)} %compare_select_fusion.table_ref), custom_call_target="tpu_custom_call" | custom-call | tf_op jit(solution)/shard_map/instance_coupling_2/pallas_call | solution.py:182
  132.6 1.1 subtract_multiply_fusion.2
  133.9 1.7 %subtract_bitcast_fusion = f32[5,1,8,1024]{3,2,1,0:T(8,128)} fusion(f32[5,8,1024]{2,1,0:T(8,128)S(1)} %copy-done.2, f32[5,8,1024]{2,1,0:T(8,128)} %instance_coupling_2.1, f32[1,8,1024]{2,1,0:T(8,128)S(1)} %negate_bitcast_fusion, f32[3,8,1024]{2,1,0:T(8,128)S(1)} %get-tuple-element.24, f32[1,8,1024]{2,1,0:T(8,128)S(1)} %get-tuple-element.22, ...), kind=kLoop, calls=%fused_computation.81 | loop fusion | flops 819200 | bytes 1548288 | tf_op jit(solution)/shard_map/broadcast_in_dim | solution.py:307
  (70 shorter events, 1.7 us)
Async XLA Ops:
  0.0 24.3 %copy-start = (f32[3,65536]{1,0:T(4,128)S(1)}, f32[3,65536]{1,0:T(4,128)}, u32[]{:S(2)}) copy-start(f32[3,65536]{1,0:T(4,128)} %param.21) | copy-start | bytes 2359300
  1.1 78.3 %collective-permute-start.1 = (f32[5,1,1024]{2,1,0:T(1,128)S(1)}, f32[5,1,1024]{2,1,0:T(1,128)S(1)}, u32[]{:S(2)}, u32[]{:S(2)}) collective-permute-start(f32[5,1,1024]{2,1,0:T(1,128)S(1)} %get-tuple-element.136), channel_id=1, source_target_pairs={{1,0},{2,1},{3,2},{4,3},{5,4},{6,5},{7,6},{8,7},{9,8},{10,9},{11,1... | collective-permute-start | bytes 61448 | tf_op jit(solution)/shard_map/ppermute | solution.py:32
  1.2 78.3 %collective-permute-start = (f32[5,1,1024]{2,1,0:T(1,128)S(1)}, f32[5,1,1024]{2,1,0:T(1,128)S(1)}, u32[]{:S(2)}, u32[]{:S(2)}) collective-permute-start(f32[5,1,1024]{2,1,0:T(1,128)S(1)} %get-tuple-element.135), channel_id=1, source_target_pairs={{0,1},{1,2},{2,3},{3,4},{4,5},{5,6},{6,7},{7,8},{8,9},{9,10},{10,1... | collective-permute-start | bytes 61448 | tf_op jit(solution)/shard_map/ppermute | solution.py:30
  33.9 20.9 %copy-start.10 = (s32[4,1024]{1,0:T(4,128)S(1)}, s32[4,1024]{1,0:T(4,128)}, u32[]{:S(2)}) copy-start(s32[4,1024]{1,0:T(4,128)} %param.24) | copy-start | bytes 49156
  54.8 3.8 %copy-start.6 = (f32[1,8,1024]{2,1,0:T(8,128)S(1)}, f32[1,8,1024]{2,1,0:T(8,128)}, u32[]{:S(2)}) copy-start(f32[1,8,1024]{2,1,0:T(8,128)} %param.15) | copy-start | bytes 98308
  54.8 3.8 %copy-start.7 = (f32[3,1,8,1024]{3,2,1,0:T(8,128)S(1)}, f32[3,1,8,1024]{3,2,1,0:T(8,128)}, u32[]{:S(2)}) copy-start(f32[3,1,8,1024]{3,2,1,0:T(8,128)} %param.16) | copy-start | bytes 294916
  58.4 0.8 copy-start.8
  58.4 21.1 %copy-start.5 = (f32[5,1,8,1024]{3,2,1,0:T(8,128)S(1)}, f32[5,1,8,1024]{3,2,1,0:T(8,128)}, u32[]{:S(2)}) copy-start(f32[5,1,8,1024]{3,2,1,0:T(8,128)} %param.14) | copy-start | bytes 491524
  58.4 21.2 %copy-start.9 = (pred[3]{0:T(512)(128)(4,1)S(1)}, pred[3]{0:T(512)(128)(4,1)}, u32[]{:S(2)}) copy-start(pred[3]{0:T(512)(128)(4,1)} %constant.96.clone.1) | copy-start | bytes 13
  80.9 3.6 %copy-start.3 = (f32[5,8,1024]{2,1,0:T(8,128)}, f32[5,8,1024]{2,1,0:T(8,128)S(1)}, u32[]{:S(2)}) copy-start(f32[5,8,1024]{2,1,0:T(8,128)S(1)} %get-tuple-element.33.psi_ref) | copy-start | bytes 491524
  84.7 22.9 %copy-start.4 = (f32[5,8,1024]{2,1,0:T(8,128)S(1)}, f32[5,8,1024]{2,1,0:T(8,128)}, u32[]{:S(2)}) copy-start(f32[5,8,1024]{2,1,0:T(8,128)} %copy-done.3) | copy-start | bytes 491524
  84.7 21.6 %collective-permute-start.3 = (f32[5,1,1024]{2,1,0:T(1,128)S(1)}, f32[5,1,1024]{2,1,0:T(1,128)S(1)}, u32[]{:S(2)}, u32[]{:S(2)}) collective-permute-start(f32[5,1,1024]{2,1,0:T(1,128)S(1)} %get-tuple-element.122), channel_id=1, source_target_pairs={{1,0},{2,1},{3,2},{4,3},{5,4},{6,5},{7,6},{8,7},{9,8},{10,9},{11,1... | collective-permute-start | bytes 61448 | tf_op jit(solution)/shard_map/ppermute | solution.py:32
  84.8 21.5 %collective-permute-start.2 = (f32[5,1,1024]{2,1,0:T(1,128)S(1)}, f32[5,1,1024]{2,1,0:T(1,128)S(1)}, u32[]{:S(2)}, u32[]{:S(2)}) collective-permute-start(f32[5,1,1024]{2,1,0:T(1,128)S(1)} %get-tuple-element.121), channel_id=1, source_target_pairs={{0,1},{1,2},{2,3},{3,4},{4,5},{5,6},{6,7},{7,8},{8,9},{9,10},{10,1... | collective-permute-start | bytes 61448 | tf_op jit(solution)/shard_map/ppermute | solution.py:30
  108.7 5.7 %copy-start.1 = (f32[5,8,1024]{2,1,0:T(8,128)}, f32[5,8,1024]{2,1,0:T(8,128)S(1)}, u32[]{:S(2)}) copy-start(f32[5,8,1024]{2,1,0:T(8,128)S(1)} %get-tuple-element.27.psi_ref) | copy-start | bytes 491524
  108.8 23.8 %collective-permute-start.4 = (f32[5,1,1024]{2,1,0:T(1,128)S(1)}, f32[5,1,1024]{2,1,0:T(1,128)S(1)}, u32[]{:S(2)}, u32[]{:S(2)}) collective-permute-start(f32[5,1,1024]{2,1,0:T(1,128)S(1)} %get-tuple-element.111), channel_id=1, source_target_pairs={{0,1},{1,2},{2,3},{3,4},{4,5},{5,6},{6,7},{7,8},{8,9},{9,10},{10,1... | collective-permute-start | bytes 61448 | tf_op jit(solution)/shard_map/ppermute | solution.py:30
  109.1 23.5 %collective-permute-start.5 = (f32[5,1,1024]{2,1,0:T(1,128)S(1)}, f32[5,1,1024]{2,1,0:T(1,128)S(1)}, u32[]{:S(2)}, u32[]{:S(2)}) collective-permute-start(f32[5,1,1024]{2,1,0:T(1,128)S(1)} %get-tuple-element.110), channel_id=1, source_target_pairs={{1,0},{2,1},{3,2},{4,3},{5,4},{6,5},{7,6},{8,7},{9,8},{10,9},{11,1... | collective-permute-start | bytes 61448 | tf_op jit(solution)/shard_map/ppermute | solution.py:32
  114.5 19.4 %copy-start.2 = (f32[5,8,1024]{2,1,0:T(8,128)S(1)}, f32[5,8,1024]{2,1,0:T(8,128)}, u32[]{:S(2)}) copy-start(f32[5,8,1024]{2,1,0:T(8,128)} %copy-done.1) | copy-start | bytes 491524

commit v2 on v1

--- a/solution.py
+++ b/solution.py
@@ -236,6 +236,41 @@
     )(block)
 
 
+def route_kernel(count, rows_ref, out_ref, held, send_sem, recv_sem):
+    me = lax.axis_index("inst")
+    peers = [(me + d) % count for d in range(1, count)]
+    greet("inst", peers)
+    copies = []
+    for slot, peer in enumerate(peers):
+        copy = pltpu.make_async_remote_copy(
+            src_ref=rows_ref.at[peer], dst_ref=held.at[me], send_sem=send_sem.at[slot],
+            recv_sem=recv_sem.at[slot], device_id={"inst": peer},
+            device_id_type=pl.DeviceIdType.MESH)
+        copy.start()
+        copies.append(copy)
+    for copy in copies:
+        copy.wait()
+    held[me] = rows_ref[me]
+    out_ref[...] = held[...]
+
+
+def inst_route(rows, collective):
+    count = lax.axis_size("inst")
+    return pl.pallas_call(
+        functools.partial(route_kernel, count),
+        out_shape=jax.ShapeDtypeStruct(rows.shape, rows.dtype),
+        in_specs=[pl.BlockSpec(memory_space=pltpu.VMEM)],
+        out_specs=pl.BlockSpec(memory_space=pltpu.VMEM),
+        scratch_shapes=[
+            pltpu.VMEM(rows.shape, rows.dtype),
+            pltpu.SemaphoreType.DMA((count - 1,)),
+            pltpu.SemaphoreType.DMA((count - 1,)),
+        ],
+        compiler_params=pltpu.CompilerParams(collective_id=collective, has_side_effects=True),
+        name="inst_route",
+    )(rows)
+
+
 def shards(
     psi_start,
     density,
@@ -253,7 +288,6 @@
     inst_id = lax.axis_index("inst")
     space_id = lax.axis_index("space")
     times = jnp.array([2.0 * math.pi * i / inst_count for i in range(inst_count)], jnp.float32)
-    time_now = times[inst_id]
     local_obs = jnp.concatenate(
         [obs_pos, obs_weight, obs_harmonic[None].astype(jnp.float32)], axis=0
     )
@@ -263,18 +297,28 @@
     stacked = space_gather(packed, ITERS)
     observers = stacked[:, :rows, :per].transpose(1, 0, 2).reshape(rows, -1)
     owned_count = panel_normal.shape[1]
-    mine = lax.dynamic_slice_in_dim(panel_pos, space_id * owned_count, owned_count, 1)
+    piece = owned_count // inst_count
+    assert piece * inst_count == owned_count and piece % 128 == 0
+    mine = lax.dynamic_slice_in_dim(
+        panel_pos, space_id * owned_count + inst_id * piece, piece, 1
+    )
+    normal = lax.dynamic_slice_in_dim(panel_normal, inst_id * piece, piece, 1)
     delta = mine[:, None, :] - observers[:3, :, None]
     dist2 = jnp.sum(delta * delta, axis=0)
     dist = jnp.sqrt(dist2)
-    phase = observers[5][:, None] * (time_now - KWAVE * dist)
-    amp = (
-        (observers[3][:, None] * jnp.cos(phase) + observers[4][:, None] * jnp.sin(phase))
-        * (RADIUS * RADIUS)
-        / (dist2 * dist)
-    )
-    along = jnp.sum(delta * panel_normal[:, None, :], axis=0)
-    weight = jnp.sum(amp * along, axis=0)
+    harm = observers[5]
+    lag = harm[:, None] * (KWAVE * dist)
+    along = jnp.sum(delta * normal[:, None, :], axis=0) * (RADIUS * RADIUS) / (dist2 * dist)
+    pairs = jnp.concatenate([along * jnp.cos(lag), along * jnp.sin(lag)], axis=0)
+    beat = times[:, None] * harm[None, :]
+    cos_beat, sin_beat = jnp.cos(beat), jnp.sin(beat)
+    real, imag = observers[3][None, :], observers[4][None, :]
+    mixes = jnp.concatenate(
+        [real * cos_beat + imag * sin_beat, real * sin_beat - imag * cos_beat], axis=1
+    )
+    partial = jnp.dot(mixes, pairs, precision=lax.Precision.HIGHEST)
+    routed = inst_route(partial.reshape(inst_count, piece // 128, 128), ITERS + 1)
+    weight = routed.reshape(owned_count)
     layers = psi_start.shape[2]
     plane = psi_start.shape[3]
     wall = cell_sum(weight, panel_cell, layers, plane)

time: 136 us -> 120 us (0.88)
  the two profiles are of different devices: /device:TPU:8 before, /device:TPU:1 now
where the time goes in v2:
time: 120 us; the launch traced here: 118 us
  Pallas kernels  71.6 us (60%)
  starting transfers between devices  15 us (12%)
  matrix products  13.5 us (11%)
  other arithmetic  11.7 us (10%)
  local copies, waits for them, and re-layouts  5.51 us (5%)
    pallas_call x3, Pallas kernels, instance_coupling(): pl.pallas_call(functools.partial(coupling_kernel, count, inner), out_shap...  46.7 us
    pallas_call x1, Pallas kernels, space_gather(): pl.pallas_call(functools.partial(gather_kernel, count), out_shape=jax.Sha...  15.9 us
    ppermute x3, starting transfers between devices, padded_2(): lax.ppermute(tail, axis, [(i, (i + 1) % count) for i in range(count)])  13.7 us
    dot_general x3, matrix products, plane_gather(): jnp.einsum('pra,kba->kprb', parts, onehot, preferred_element_type=jnp.flo...  11.4 us
    pallas_call x1, Pallas kernels, inst_route(): pl.pallas_call(functools.partial(route_kernel, count), out_shape=jax.Shap...  8.99 us
    mul x1, other arithmetic, shards(): along * jnp.cos(lag)  2.57 us
  transfers between devices with their start and end apart: 6, of which 0 were waited for; matrix products, arithmetic and copies ran while one was open for 16% of the time, Pallas kernels for 61%

profile of v2, /device:TPU:1, one launch (start us, length us, event | category | flops | bytes accessed | tf_op | source)
XLA Modules:
  0.0 118.0 jit_solution(1926703405052155618)
XLA Ops:
  0.0 1.0 fusion.87
  1.0 2.8 %collective-permute-start = (f32[5,1,1024]{2,1,0:T(1,128)S(1)}, f32[5,1,1024]{2,1,0:T(1,128)S(1)}, u32[]{:S(2)}, u32[]{:S(2)}) collective-permute-start(f32[5,1,1024]{2,1,0:T(1,128)S(1)} %get-tuple-element.137), channel_id=1, source_target_pairs={{0,1},{1,2},{2,3},{3,4},{4,5},{5,6},{6,7},{7,8},{8,9},{9,10},{10,1... | collective-permute-start | bytes 61448 | tf_op jit(solution)/shard_map/ppermute | solution.py:30
  3.8 0.6 collective-permute-start.1
  4.4 0.9 reduce-precision_convert_fusion.5
  5.4 0.7 convert_bitcast_fusion
  6.0 1.3 %select_maximum_fusion.block_ref = f32[8,128]{1,0:T(8,128)} fusion(f32[1,16]{1,0:T(1,128)S(1)} %convert_bitcast_fusion, f32[2,16]{1,0:T(2,128)} %param.19, f32[3,16]{1,0:T(4,128)} %param.18), kind=kLoop, calls=%fused_computation.248 | loop fusion | flops 11264 | bytes 4480 | tf_op jit(solution)/shard_map/concatenate | solution.py:291
  7.3 15.9 %space_gather.1 = f32[32,8,128]{2,1,0:T(8,128)} custom-call(f32[8,128]{1,0:T(8,128)} %select_maximum_fusion.block_ref), custom_call_target="tpu_custom_call" | custom-call | tf_op jit(solution)/shard_map/space_gather/pallas_call | solution.py:224
  23.3 0.9 slice_bitcast_fusion.12
  24.3 0.9 broadcast_divide_fusion
  25.3 0.8 multiply_reduce_fusion.3
  26.1 4.3 %fusion.14 = f32[4,3,40,1024]{3,2,1,0:T(8,128)S(1)} fusion(s32[4,1024]{1,0:T(4,128)} %param.24, bf16[1,40,1024]{2,1,0:T(8,128)(2,1)S(1)} %get-tuple-element.140, bf16[1,40,1024]{2,1,0:T(8,128)(2,1)S(1)} %get-tuple-element.141, bf16[1,40,1024]{2,1,0:T(8,128)(2,1)S(1)} %get-tuple-element.139), kind=kOutput, calls=%fused_computation.14 | convolution fusion | flops 1011564544 | bytes 2228224 | tf_op jit(solution)/shard_map/pra,kba->kprb/dot_general | solution.py:109
  30.9 0.7 constant_dynamic-slice_fusion
  31.6 0.3 fusion.23
  32.0 2.6 %cosine_multiply_fusion = (f32[512,256]{1,0:T(8,128)S(1)}, f32[512,256]{1,0:T(8,128)S(1)}) fusion(f32[512,256]{1,0:T(8,128)S(1)} %get-tuple-element.21, f32[512]{0:T(512)S(1)} %broadcast_multiply_fusion, f32[512,256]{1,0:T(8,128)S(1)} %get-tuple-element.20), kind=kLoop, calls=%fused_computation.33 | loop fusion | flops 786432 | bytes 2099200 | tf_op jit(solution)/shard_map/mul | solution.py:312
  34.7 0.5 fusion.25
  35.2 0.6 reshape.481.rows_ref
  35.9 9.0 %inst_route.1 = f32[8,2,128]{2,1,0:T(2,128)} custom-call(f32[8,2,128]{2,1,0:T(2,128)} %reshape.481.rows_ref), custom_call_target="tpu_custom_call" | custom-call | tf_op jit(solution)/shard_map/inst_route/pallas_call | solution.py:259
  44.9 0.8 reduce-precision_convert_fusion.7
  45.7 1.6 %fusion.11 = f32[3,8,1024]{2,1,0:T(8,128)S(1)} fusion(s32[2048]{0:T(1024)S(1)} %get-tuple-element.168, bf16[1,8,2048]{2,1,0:T(8,128)(2,1)S(1)} %get-tuple-element.166, bf16[1,8,2048]{2,1,0:T(8,128)(2,1)S(1)} %get-tuple-element.165, bf16[1,8,2048]{2,1,0:T(8,128)(2,1)S(1)} %get-tuple-element.164), kind=kOutput, calls=%fused_computation.10 | convolution fusion | flops 102858752 | bytes 204800 | tf_op jit(solution)/shard_map/plq,qb->plb/dot_general | solution.py:122
  47.3 0.6 compare_select_fusion.table_ref
  48.0 16.2 %instance_coupling_0.1 = f32[5,8,1024]{2,1,0:T(8,128)} custom-call(f32[5,8,1024]{2,1,0:T(8,128)} %bitcast.182, f32[8]{0:T(128)} %compare_select_fusion.table_ref), custom_call_target="tpu_custom_call" | custom-call | tf_op jit(solution)/shard_map/instance_coupling_0/pallas_call | solution.py:182
  64.6 0.5 copy-done.7
  65.4 3.6 %fusion.17 = f32[4,3,40,1024]{3,2,1,0:T(8,128)S(1)} fusion(s32[4,1024]{1,0:T(4,128)S(1)} %copy-done.13, bf16[1,40,1024]{2,1,0:T(8,128)(2,1)S(1)} %get-tuple-element.126, bf16[1,40,1024]{2,1,0:T(8,128)(2,1)S(1)} %get-tuple-element.125, bf16[1,40,1024]{2,1,0:T(8,128)(2,1)S(1)} %get-tuple-element.32), kind=kOutput, calls=%fused_computation.15 | convolution fusion | flops 1011564544 | bytes 2228224 | tf_op jit(solution)/shard_map/pra,kba->kprb/dot_general | solution.py:109
  69.1 3.1 %collective-permute-start.2 = (f32[5,1,1024]{2,1,0:T(1,128)S(1)}, f32[5,1,1024]{2,1,0:T(1,128)S(1)}, u32[]{:S(2)}, u32[]{:S(2)}) collective-permute-start(f32[5,1,1024]{2,1,0:T(1,128)S(1)} %get-tuple-element.123), channel_id=1, source_target_pairs={{0,1},{1,2},{2,3},{3,4},{4,5},{5,6},{6,7},{7,8},{8,9},{9,10},{10,1... | collective-permute-start | bytes 61448 | tf_op jit(solution)/shard_map/ppermute | solution.py:30
  72.2 0.7 collective-permute-start.3
  72.9 14.5 %instance_coupling_1.1 = f32[5,8,1024]{2,1,0:T(8,128)} custom-call(f32[5,8,1024]{2,1,0:T(8,128)} %copy-done.2, f32[8]{0:T(128)} %compare_select_fusion.table_ref), custom_call_target="tpu_custom_call" | custom-call | tf_op jit(solution)/shard_map/instance_coupling_1/pallas_call | solution.py:182
  87.8 0.6 copy-done.8
  88.6 3.6 %fusion.20 = f32[4,3,40,1024]{3,2,1,0:T(8,128)S(1)} fusion(s32[4,1024]{1,0:T(4,128)S(1)} %copy-done.13, bf16[1,40,1024]{2,1,0:T(8,128)(2,1)S(1)} %get-tuple-element.111, bf16[1,40,1024]{2,1,0:T(8,128)(2,1)S(1)} %get-tuple-element.110, bf16[1,40,1024]{2,1,0:T(8,128)(2,1)S(1)} %get-tuple-element.26), kind=kOutput, calls=%fused_computation.16 | convolution fusion | flops 1011564544 | bytes 2228224 | tf_op jit(solution)/shard_map/pra,kba->kprb/dot_general | solution.py:109
  92.4 7.8 %collective-permute-start.4 = (f32[5,1,1024]{2,1,0:T(1,128)S(1)}, f32[5,1,1024]{2,1,0:T(1,128)S(1)}, u32[]{:S(2)}, u32[]{:S(2)}) collective-permute-start(f32[5,1,1024]{2,1,0:T(1,128)S(1)} %get-tuple-element.113), channel_id=1, source_target_pairs={{0,1},{1,2},{2,3},{3,4},{4,5},{5,6},{6,7},{7,8},{8,9},{9,10},{10,1... | collective-permute-start | bytes 61448 | tf_op jit(solution)/shard_map/ppermute | solution.py:30
  100.2 16.0 %instance_coupling_2.1 = f32[5,8,1024]{2,1,0:T(8,128)} custom-call(f32[5,8,1024]{2,1,0:T(8,128)} %copy-done, f32[8]{0:T(128)} %compare_select_fusion.table_ref), custom_call_target="tpu_custom_call" | custom-call | tf_op jit(solution)/shard_map/instance_coupling_2/pallas_call | solution.py:182
  116.6 0.6 copy-done.6
  117.1 0.8 subtract_bitcast_fusion
  (80 shorter events, 2.6 us)
Async XLA Ops:
  1.0 63.2 %collective-permute-start = (f32[5,1,1024]{2,1,0:T(1,128)S(1)}, f32[5,1,1024]{2,1,0:T(1,128)S(1)}, u32[]{:S(2)}, u32[]{:S(2)}) collective-permute-start(f32[5,1,1024]{2,1,0:T(1,128)S(1)} %get-tuple-element.137), channel_id=1, source_target_pairs={{0,1},{1,2},{2,3},{3,4},{4,5},{5,6},{6,7},{7,8},{8,9},{9,10},{10,1... | collective-permute-start | bytes 61448 | tf_op jit(solution)/shard_map/ppermute | solution.py:30
  3.8 60.4 %collective-permute-start.1 = (f32[5,1,1024]{2,1,0:T(1,128)S(1)}, f32[5,1,1024]{2,1,0:T(1,128)S(1)}, u32[]{:S(2)}, u32[]{:S(2)}) collective-permute-start(f32[5,1,1024]{2,1,0:T(1,128)S(1)} %get-tuple-element.138), channel_id=1, source_target_pairs={{1,0},{2,1},{3,2},{4,3},{5,4},{6,5},{7,6},{8,7},{9,8},{10,9},{11,1... | collective-permute-start | bytes 61448 | tf_op jit(solution)/shard_map/ppermute | solution.py:32
  30.5 4.0 %copy-start.12 = (f32[8]{0:T(128)S(1)}, f32[8]{0:T(128)}, u32[]{:S(2)}) copy-start(f32[8]{0:T(128)} %constant.121.clone) | copy-start | bytes 100
  31.6 13.2 %copy-start.10 = (s32[2048]{0:T(1024)S(1)}, s32[2048]{0:T(1024)}, u32[]{:S(2)}) copy-start(s32[2048]{0:T(1024)} %param.23) | copy-start | bytes 24580
  34.7 12.6 %copy-start.5 = (f32[1,8,1024]{2,1,0:T(8,128)S(1)}, f32[1,8,1024]{2,1,0:T(8,128)}, u32[]{:S(2)}) copy-start(f32[1,8,1024]{2,1,0:T(8,128)} %param.15) | copy-start | bytes 98308
  34.7 12.6 %copy-start.9 = (f32[1,8,1024]{2,1,0:T(8,128)S(1)}, f32[1,8,1024]{2,1,0:T(8,128)}, u32[]{:S(2)}) copy-start(f32[1,8,1024]{2,1,0:T(8,128)} %param.17) | copy-start | bytes 98308
  44.9 19.3 %copy-start.4 = (f32[5,1,8,1024]{3,2,1,0:T(8,128)S(1)}, f32[5,1,8,1024]{3,2,1,0:T(8,128)}, u32[]{:S(2)}) copy-start(f32[5,1,8,1024]{3,2,1,0:T(8,128)} %param.14) | copy-start | bytes 491524
  47.3 17.2 %copy-start.11 = (pred[3]{0:T(512)(128)(4,1)S(1)}, pred[3]{0:T(512)(128)(4,1)}, u32[]{:S(2)}) copy-start(pred[3]{0:T(512)(128)(4,1)} %constant.96.clone.1) | copy-start | bytes 13
  64.2 0.9 copy-start.7
  64.4 1.0 copy-start.13
  65.3 3.7 %copy-start.2 = (f32[5,8,1024]{2,1,0:T(8,128)}, f32[5,8,1024]{2,1,0:T(8,128)S(1)}, u32[]{:S(2)}) copy-start(f32[5,8,1024]{2,1,0:T(8,128)S(1)} %get-tuple-element.33.psi_ref) | copy-start | bytes 491524
  69.1 18.4 %copy-start.3 = (f32[5,8,1024]{2,1,0:T(8,128)S(1)}, f32[5,8,1024]{2,1,0:T(8,128)}, u32[]{:S(2)}) copy-start(f32[5,8,1024]{2,1,0:T(8,128)} %copy-done.2) | copy-start | bytes 491524
  69.1 18.3 %collective-permute-start.2 = (f32[5,1,1024]{2,1,0:T(1,128)S(1)}, f32[5,1,1024]{2,1,0:T(1,128)S(1)}, u32[]{:S(2)}, u32[]{:S(2)}) collective-permute-start(f32[5,1,1024]{2,1,0:T(1,128)S(1)} %get-tuple-element.123), channel_id=1, source_target_pairs={{0,1},{1,2},{2,3},{3,4},{4,5},{5,6},{6,7},{7,8},{8,9},{9,10},{10,1... | collective-permute-start | bytes 61448 | tf_op jit(solution)/shard_map/ppermute | solution.py:30
  72.2 15.2 %collective-permute-start.3 = (f32[5,1,1024]{2,1,0:T(1,128)S(1)}, f32[5,1,1024]{2,1,0:T(1,128)S(1)}, u32[]{:S(2)}, u32[]{:S(2)}) collective-permute-start(f32[5,1,1024]{2,1,0:T(1,128)S(1)} %get-tuple-element.124), channel_id=1, source_target_pairs={{1,0},{2,1},{3,2},{4,3},{5,4},{6,5},{7,6},{8,7},{9,8},{10,9},{11,1... | collective-permute-start | bytes 61448 | tf_op jit(solution)/shard_map/ppermute | solution.py:32
  87.5 0.9 copy-start.8
  88.5 3.6 %copy-start = (f32[5,8,1024]{2,1,0:T(8,128)}, f32[5,8,1024]{2,1,0:T(8,128)S(1)}, u32[]{:S(2)}) copy-start(f32[5,8,1024]{2,1,0:T(8,128)S(1)} %get-tuple-element.27.psi_ref) | copy-start | bytes 491524
  92.3 23.9 %copy-start.1 = (f32[5,8,1024]{2,1,0:T(8,128)S(1)}, f32[5,8,1024]{2,1,0:T(8,128)}, u32[]{:S(2)}) copy-start(f32[5,8,1024]{2,1,0:T(8,128)} %copy-done) | copy-start | bytes 491524
  92.4 23.9 %collective-permute-start.4 = (f32[5,1,1024]{2,1,0:T(1,128)S(1)}, f32[5,1,1024]{2,1,0:T(1,128)S(1)}, u32[]{:S(2)}, u32[]{:S(2)}) collective-permute-start(f32[5,1,1024]{2,1,0:T(1,128)S(1)} %get-tuple-element.113), channel_id=1, source_target_pairs={{0,1},{1,2},{2,3},{3,4},{4,5},{5,6},{6,7},{7,8},{8,9},{9,10},{10,1... | collective-permute-start | bytes 61448 | tf_op jit(solution)/shard_map/ppermute | solution.py:30
  100.2 16.1 %collective-permute-start.5 = (f32[5,1,1024]{2,1,0:T(1,128)S(1)}, f32[5,1,1024]{2,1,0:T(1,128)S(1)}, u32[]{:S(2)}, u32[]{:S(2)}) collective-permute-start(f32[5,1,1024]{2,1,0:T(1,128)S(1)} %get-tuple-element.112), channel_id=1, source_target_pairs={{1,0},{2,1},{3,2},{4,3},{5,4},{6,5},{7,6},{8,7},{9,8},{10,9},{11,1... | collective-permute-start | bytes 61448 | tf_op jit(solution)/shard_map/ppermute | solution.py:32
  116.2 0.9 copy-start.6

commit v3 on v2

--- a/solution.py
+++ b/solution.py
@@ -124,22 +124,39 @@
 
 
 def greet(axis, peers):
+    greet_all([{axis: peer} for peer in peers])
+
+
+def greet_all(devices):
     barrier = pltpu.get_barrier_semaphore()
-    for peer in peers:
-        pl.semaphore_signal(barrier, inc=1, device_id={axis: peer},
+    for device in devices:
+        pl.semaphore_signal(barrier, inc=1, device_id=device,
                             device_id_type=pl.DeviceIdType.MESH)
-    pl.semaphore_wait(barrier, len(peers))
-
-
-def coupling_kernel(count, inner, psi_ref, table_ref, out_ref, held, outbox, inbox,
-                    ring_send, ring_recv, cross_send, cross_recv):
+    pl.semaphore_wait(barrier, len(devices))
+
+
+def coupling_kernel(count, inner, psi_ref, table_ref, out_ref, below_ref, above_ref, held,
+                    outbox, inbox, below, above, ring_send, ring_recv, cross_send, cross_recv,
+                    edge_send, edge_recv):
     outer = count // inner
     me = lax.axis_index("inst")
     me_hi, me_lo = me // inner, me % inner
     ring = [me_hi * inner + (me_lo + d) % inner for d in range(1, inner)]
     ring_from = [me_hi * inner + (me_lo - d) % inner for d in range(1, inner)]
     partners = [((me_hi + h) % outer) * inner + me_lo for h in range(1, outer)]
-    greet("inst", ring + partners)
+    slabs = lax.axis_size("space")
+    here = lax.axis_index("space")
+    up, down = (here + 1) % slabs, (here + slabs - 1) % slabs
+    greet_all([{"inst": p} for p in ring + partners] + [{"space": up}, {"space": down}])
+    last = psi_ref.shape[1] - 1
+    edges = []
+    for slot, (peer, layer, land) in enumerate(((up, last, below), (down, 0, above))):
+        copy = pltpu.make_async_remote_copy(
+            src_ref=psi_ref.at[:, pl.ds(layer, 1), :], dst_ref=land.at[:, pl.ds(layer, 1), :],
+            send_sem=edge_send.at[slot], recv_sem=edge_recv.at[slot],
+            device_id={"space": peer}, device_id_type=pl.DeviceIdType.MESH)
+        copy.start()
+        edges.append(copy)
 
     def coef(row, col):
         return table_ref[(row - col) % count]
@@ -173,28 +190,39 @@
         copy.wait()
         total = total + inbox[slot]
     out_ref[...] = total
+    for copy in edges:
+        copy.wait()
+    below_ref[...] = below[:, last:, :]
+    above_ref[...] = above[:, :1, :]
 
 
 def instance_coupling(psi, table, step):
     count = lax.axis_size("inst")
+    assert lax.axis_size("space") > 1
     inner = 4 if count % 4 == 0 else count
     outer = count // inner
+    comps, layers, plane = psi.shape
+    edge = jax.ShapeDtypeStruct((comps, 1, plane), psi.dtype)
     return pl.pallas_call(
         functools.partial(coupling_kernel, count, inner),
-        out_shape=jax.ShapeDtypeStruct(psi.shape, psi.dtype),
+        out_shape=(jax.ShapeDtypeStruct(psi.shape, psi.dtype), edge, edge),
         in_specs=[
             pl.BlockSpec(memory_space=pltpu.VMEM),
             pl.BlockSpec(memory_space=pltpu.SMEM),
         ],
-        out_specs=pl.BlockSpec(memory_space=pltpu.VMEM),
+        out_specs=[pl.BlockSpec(memory_space=pltpu.VMEM)] * 3,
         scratch_shapes=[
             pltpu.VMEM((inner - 1, *psi.shape), psi.dtype),
             pltpu.VMEM((max(outer - 1, 1), *psi.shape), psi.dtype),
             pltpu.VMEM((max(outer - 1, 1), *psi.shape), psi.dtype),
+            pltpu.VMEM(psi.shape, psi.dtype),
+            pltpu.VMEM(psi.shape, psi.dtype),
             pltpu.SemaphoreType.DMA((inner - 1,)),
             pltpu.SemaphoreType.DMA((inner - 1,)),
             pltpu.SemaphoreType.DMA((max(outer - 1, 1),)),
             pltpu.SemaphoreType.DMA((max(outer - 1, 1),)),
+            pltpu.SemaphoreType.DMA((2,)),
+            pltpu.SemaphoreType.DMA((2,)),
         ],
         compiler_params=pltpu.CompilerParams(collective_id=step, has_side_effects=True),
         name=f"instance_coupling_{step}",
@@ -338,15 +366,14 @@
     )
     psi = psi_start[:, 0]
     for step in range(ITERS):
-        padded = padded_2(psi, (("space", 1),), 1)
-        minus_a = padded[:, :-2]
-        plus_a = padded[:, 2:]
+        spectral_operator, below, above = instance_coupling(psi, row_entry, step)
+        minus_a = jnp.concatenate([below, psi[:, :-1]], axis=1)
+        plus_a = jnp.concatenate([psi[:, 1:], above], axis=1)
         plus_y, minus_y, plus_z, minus_z = plane_gather(psi, onehot)
         middle_point = pull(
             (0.5 * (minus_a - plus_a), 0.5 * (minus_y - plus_y), 0.5 * (minus_z - plus_z))
         )[0]
         spread = 6.0 * psi - (minus_a + plus_a + plus_y + minus_y + plus_z + minus_z)
-        spectral_operator = instance_coupling(psi, row_entry, step)
         psi = psi - TAU * (middle_point + DISSIP * spread + spectral_operator + source)
     return psi[:, None]
 

time: 120 us -> 115 us (0.958)
  starting transfers between devices: 15 us -> 0 us
  Pallas kernels: 71.6 us -> 82.3 us
  local copies, waits for them, and re-layouts: 5.51 us -> 3.54 us
  other arithmetic: 11.7 us -> 13.5 us
    ppermute x6 -> x0, starting transfers between devices: 15 us -> none  [the longest x3 13.7 us: padded_2(): lax.ppermute(tail, axis, [(i, (i + 1) % count) for i in range(count)])]
    pallas_call x3, Pallas kernels: 46.7 us -> 54.9 us  [instance_coupling(): pl.pallas_call(functools.partial(coupling_kernel, count, inner), out_shap...]
    pallas_call x1, Pallas kernels: 15.9 us -> 19.7 us  [space_gather(): pl.pallas_call(functools.partial(gather_kernel, count), out_shape=jax.Sha...]
    mul x3 -> x2, other arithmetic: 0.21 us -> 1.73 us  [shards(): 0.5 * (minus_a - plus_a)]
    pallas_call x1, Pallas kernels: 8.99 us -> 7.78 us  [inst_route(): pl.pallas_call(functools.partial(route_kernel, count), out_shape=jax.Shap...]
  transfers between devices with their start and end apart: 6 -> 0, of which waited for: 0 -> 0; matrix products, arithmetic and copies ran while one was open for 16% -> 0% of each run, Pallas kernels for 61% -> 0%
where the time goes in v3:
time: 115 us; the launch traced here: 114 us
  Pallas kernels  82.3 us (72%)
  other arithmetic  13.5 us (12%)
  matrix products  13.5 us (12%)
  local copies, waits for them, and re-layouts  3.54 us (3%)
    pallas_call x3, Pallas kernels, instance_coupling(): pl.pallas_call(functools.partial(coupling_kernel, count, inner), out_shap...  54.9 us
    pallas_call x1, Pallas kernels, space_gather(): pl.pallas_call(functools.partial(gather_kernel, count), out_shape=jax.Sha...  19.7 us
    dot_general x3, matrix products, plane_gather(): jnp.einsum('pra,kba->kprb', parts, onehot, preferred_element_type=jnp.flo...  11.4 us
    pallas_call x1, Pallas kernels, inst_route(): pl.pallas_call(functools.partial(route_kernel, count), out_shape=jax.Shap...  7.78 us
    mul x1, other arithmetic, shards(): along * jnp.cos(lag)  2.56 us

profile of v3, /device:TPU:1, one launch (start us, length us, event | category | flops | bytes accessed | tf_op | source)
XLA Modules:
  0.0 113.7 jit_solution(8714989284856175036)
XLA Ops:
  0.0 0.9 reduce-precision_convert_fusion.5
  1.0 4.3 %fusion.14 = f32[4,3,40,1024]{3,2,1,0:T(8,128)S(1)} fusion(s32[4,1024]{1,0:T(4,128)} %param.24, bf16[1,40,1024]{2,1,0:T(8,128)(2,1)S(1)} %get-tuple-element.158, bf16[1,40,1024]{2,1,0:T(8,128)(2,1)S(1)} %get-tuple-element.159, bf16[1,40,1024]{2,1,0:T(8,128)(2,1)S(1)} %get-tuple-element.157), kind=kOutput, calls=%fused_computation.14 | convolution fusion | flops 1011564544 | bytes 2228224 | tf_op jit(solution)/shard_map/pra,kba->kprb/dot_general | solution.py:109
  5.4 0.6 compare_select_fusion.table_ref
  6.1 17.3 %instance_coupling_0.1 = (f32[5,8,1024]{2,1,0:T(8,128)}, f32[5,1,1024]{2,1,0:T(1,128)}, f32[5,1,1024]{2,1,0:T(1,128)}) custom-call(f32[5,8,1024]{2,1,0:T(8,128)} %bitcast.183, f32[8]{0:T(128)} %compare_select_fusion.table_ref), custom_call_target="tpu_custom_call" | custom-call | tf_op jit(solution)/shard_map/instance_coupling_0/pallas_call | solution.py:206
  23.4 0.9 subtract_multiply_fusion.10
  24.5 0.6 slice_multiply_fusion.70
  25.2 0.6 add_add_fusion.2
  25.8 0.7 fusion.53
  26.6 0.6 negate_bitcast_fusion.2
  27.2 0.7 constant_dynamic-slice_fusion
  27.9 0.6 select_maximum_fusion.block_ref
  28.5 19.7 %space_gather.1 = f32[32,8,128]{2,1,0:T(8,128)} custom-call(f32[8,128]{1,0:T(8,128)} %select_maximum_fusion.block_ref), custom_call_target="tpu_custom_call" | custom-call | tf_op jit(solution)/shard_map/space_gather/pallas_call | solution.py:252
  48.2 0.9 slice_bitcast_fusion.12
  49.3 0.3 fusion.23
  49.6 0.1 slice_reduce_fusion.2
  49.9 2.6 %cosine_multiply_fusion = (f32[512,256]{1,0:T(8,128)S(1)}, f32[512,256]{1,0:T(8,128)S(1)}) fusion(f32[512,256]{1,0:T(8,128)S(1)} %get-tuple-element.39, f32[512]{0:T(512)S(1)} %broadcast_multiply_fusion, f32[512,256]{1,0:T(8,128)S(1)} %get-tuple-element.38), kind=kLoop, calls=%fused_computation.33 | loop fusion | flops 786432 | bytes 2099200 | tf_op jit(solution)/shard_map/mul | solution.py:340
  52.6 0.1 fusion.73
  52.8 0.5 fusion.25
  53.4 0.6 reshape.481.rows_ref
  54.0 7.8 %inst_route.1 = f32[8,2,128]{2,1,0:T(2,128)} custom-call(f32[8,2,128]{2,1,0:T(2,128)} %reshape.481.rows_ref), custom_call_target="tpu_custom_call" | custom-call | tf_op jit(solution)/shard_map/inst_route/pallas_call | solution.py:287
  61.8 0.7 reduce-precision_convert_fusion.7
  62.5 1.6 %fusion.11 = f32[3,8,1024]{2,1,0:T(8,128)S(1)} fusion(s32[2048]{0:T(1024)S(1)} %get-tuple-element.186, bf16[1,8,2048]{2,1,0:T(8,128)(2,1)S(1)} %get-tuple-element.184, bf16[1,8,2048]{2,1,0:T(8,128)(2,1)S(1)} %get-tuple-element.183, bf16[1,8,2048]{2,1,0:T(8,128)(2,1)S(1)} %get-tuple-element.182), kind=kOutput, calls=%fused_computation.10 | convolution fusion | flops 102858752 | bytes 204800 | tf_op jit(solution)/shard_map/plq,qb->plb/dot_general | solution.py:122
  64.2 0.2 reduce-precision_convert_fusion.3
  64.5 3.5 %fusion.17 = f32[4,3,40,1024]{3,2,1,0:T(8,128)S(1)} fusion(s32[4,1024]{1,0:T(4,128)S(1)} %copy-done.33, bf16[1,40,1024]{2,1,0:T(8,128)(2,1)S(1)} %get-tuple-element.144, bf16[1,40,1024]{2,1,0:T(8,128)(2,1)S(1)} %get-tuple-element.143, bf16[1,40,1024]{2,1,0:T(8,128)(2,1)S(1)} %get-tuple-element.50), kind=kOutput, calls=%fused_computation.15 | convolution fusion | flops 1011564544 | bytes 2228224 | tf_op jit(solution)/shard_map/pra,kba->kprb/dot_general | solution.py:109
  68.2 0.6 copy-done.10
  68.9 16.9 %instance_coupling_1.1 = (f32[5,8,1024]{2,1,0:T(8,128)}, f32[5,1,1024]{2,1,0:T(1,128)}, f32[5,1,1024]{2,1,0:T(1,128)}) custom-call(f32[5,8,1024]{2,1,0:T(8,128)} %copy-done.2, f32[8]{0:T(128)} %compare_select_fusion.table_ref), custom_call_target="tpu_custom_call" | custom-call | tf_op jit(solution)/shard_map/instance_coupling_1/pallas_call | solution.py:206
  85.8 0.9 subtract_multiply_fusion.5
  87.0 0.2 reduce-precision_convert_fusion.1
  87.2 3.6 %fusion.20 = f32[4,3,40,1024]{3,2,1,0:T(8,128)S(1)} fusion(s32[4,1024]{1,0:T(4,128)S(1)} %copy-done.33, bf16[1,40,1024]{2,1,0:T(8,128)(2,1)S(1)} %get-tuple-element.129, bf16[1,40,1024]{2,1,0:T(8,128)(2,1)S(1)} %get-tuple-element.128, bf16[1,40,1024]{2,1,0:T(8,128)(2,1)S(1)} %get-tuple-element.44), kind=kOutput, calls=%fused_computation.16 | convolution fusion | flops 1011564544 | bytes 2228224 | tf_op jit(solution)/shard_map/pra,kba->kprb/dot_general | solution.py:109
  91.0 20.7 %instance_coupling_2.1 = (f32[5,8,1024]{2,1,0:T(8,128)}, f32[5,1,1024]{2,1,0:T(1,128)}, f32[5,1,1024]{2,1,0:T(1,128)}) custom-call(f32[5,8,1024]{2,1,0:T(8,128)} %copy-done, f32[8]{0:T(128)} %compare_select_fusion.table_ref), custom_call_target="tpu_custom_call" | custom-call | tf_op jit(solution)/shard_map/instance_coupling_2/pallas_call | solution.py:206
  111.7 0.9 subtract_multiply_fusion.2
  112.9 0.8 subtract_bitcast_fusion
  (109 shorter events, 1.7 us)
Async XLA Ops:
  5.2 18.1 %copy-start.4 = (f32[5,1,8,1024]{3,2,1,0:T(8,128)S(1)}, f32[5,1,8,1024]{3,2,1,0:T(8,128)}, u32[]{:S(2)}) copy-start(f32[5,1,8,1024]{3,2,1,0:T(8,128)} %param.14) | copy-start | bytes 491524
  5.3 19.1 %copy-start.7 = (f32[1,8,1024]{2,1,0:T(8,128)S(1)}, f32[1,8,1024]{2,1,0:T(8,128)}, u32[]{:S(2)}) copy-start(f32[1,8,1024]{2,1,0:T(8,128)} %param.15) | copy-start | bytes 98308
  5.3 19.1 %copy-start.20 = (f32[3,1,8,1024]{3,2,1,0:T(8,128)S(1)}, f32[3,1,8,1024]{3,2,1,0:T(8,128)}, u32[]{:S(2)}) copy-start(f32[3,1,8,1024]{3,2,1,0:T(8,128)} %param.16) | copy-start | bytes 294916
  5.4 19.0 %copy-start.27 = (f32[1,8,1024]{2,1,0:T(8,128)S(1)}, f32[1,8,1024]{2,1,0:T(8,128)}, u32[]{:S(2)}) copy-start(f32[1,8,1024]{2,1,0:T(8,128)} %param.17) | copy-start | bytes 98308
  23.4 2.4 %copy-start.29 = (pred[3]{0:T(512)(128)(4,1)S(1)}, pred[3]{0:T(512)(128)(4,1)}, u32[]{:S(2)}) copy-start(pred[3]{0:T(512)(128)(4,1)} %constant.102.clone.1) | copy-start | bytes 13
  24.5 3.4 %copy-start.34 = (s32[16]{0:T(128)S(1)}, s32[16]{0:T(128)}, u32[]{:S(2)}) copy-start(s32[16]{0:T(128)} %param.20) | copy-start | bytes 196
  24.5 3.4 %copy-start.30 = (f32[3,16]{1,0:T(4,128)S(1)}, f32[3,16]{1,0:T(4,128)}, u32[]{:S(2)}) copy-start(f32[3,16]{1,0:T(4,128)} %param.18) | copy-start | bytes 580
  24.5 3.4 %copy-start.31 = (f32[2,16]{1,0:T(2,128)S(1)}, f32[2,16]{1,0:T(2,128)}, u32[]{:S(2)}) copy-start(f32[2,16]{1,0:T(2,128)} %param.19) | copy-start | bytes 388
  25.1 24.5 %copy-start.9 = (f32[1,8,1024]{2,1,0:T(8,128)}, f32[1,8,1024]{2,1,0:T(8,128)S(1)}, u32[]{:S(2)}) copy-start(f32[1,8,1024]{2,1,0:T(8,128)S(1)} %get-tuple-element.146) | copy-start | bytes 98308
  25.1 24.5 %copy-start.12 = (f32[8,1024]{1,0:T(8,128)}, f32[8,1024]{1,0:T(8,128)S(1)}, u32[]{:S(2)}) copy-start(f32[8,1024]{1,0:T(8,128)S(1)} %get-tuple-element.180) | copy-start | bytes 98308
  48.2 4.4 %copy-start.32 = (f32[8]{0:T(128)S(1)}, f32[8]{0:T(128)}, u32[]{:S(2)}) copy-start(f32[8]{0:T(128)} %constant.121.clone) | copy-start | bytes 100
  49.6 12.1 %copy-start.28 = (s32[2048]{0:T(1024)S(1)}, s32[2048]{0:T(1024)}, u32[]{:S(2)}) copy-start(s32[2048]{0:T(1024)} %param.23) | copy-start | bytes 24580
  52.8 11.4 %copy-start.6 = (f32[5,7,1024]{2,1,0:T(8,128)S(1)}, f32[5,7,1024]{2,1,0:T(8,128)}, u32[]{:S(2)}) copy-start(f32[5,7,1024]{2,1,0:T(8,128)} %copy-done.5) | copy-start | bytes 430084
  52.8 11.4 %copy-start.11 = (f32[1,8,1024]{2,1,0:T(8,128)S(1)}, f32[1,8,1024]{2,1,0:T(8,128)}, u32[]{:S(2)}) copy-start(f32[1,8,1024]{2,1,0:T(8,128)} %get-tuple-element.181) | copy-start | bytes 98308
  52.8 11.4 %copy-start.14 = (f32[3,8,1024]{2,1,0:T(8,128)S(1)}, f32[3,8,1024]{2,1,0:T(8,128)}, u32[]{:S(2)}) copy-start(f32[3,8,1024]{2,1,0:T(8,128)} %get-tuple-element.54) | copy-start | bytes 294916
  52.8 11.4 %copy-start.16 = (f32[5,8,1024]{2,1,0:T(8,128)S(1)}, f32[5,8,1024]{2,1,0:T(8,128)}, u32[]{:S(2)}) copy-start(f32[5,8,1024]{2,1,0:T(8,128)} %get-tuple-element.28) | copy-start | bytes 491524
  52.8 11.4 %copy-start.18 = (f32[1,8,1024]{2,1,0:T(8,128)S(1)}, f32[1,8,1024]{2,1,0:T(8,128)}, u32[]{:S(2)}) copy-start(f32[1,8,1024]{2,1,0:T(8,128)} %get-tuple-element.52) | copy-start | bytes 98308
  52.8 11.4 %copy-start.19 = (f32[1,8,1024]{2,1,0:T(8,128)S(1)}, f32[1,8,1024]{2,1,0:T(8,128)}, u32[]{:S(2)}) copy-start(f32[1,8,1024]{2,1,0:T(8,128)} %negate_bitcast_fusion.2) | copy-start | bytes 98308
  52.8 11.4 %copy-start.25 = (f32[5,1,1024]{2,1,0:T(1,128)S(1)}, f32[5,1,1024]{2,1,0:T(1,128)}, u32[]{:S(2)}) copy-start(f32[5,1,1024]{2,1,0:T(1,128)} %get-tuple-element.26) | copy-start | bytes 61444
  52.8 11.4 %copy-start.26 = (f32[5,1,1024]{2,1,0:T(1,128)S(1)}, f32[5,1,1024]{2,1,0:T(1,128)}, u32[]{:S(2)}) copy-start(f32[5,1,1024]{2,1,0:T(1,128)} %get-tuple-element.27) | copy-start | bytes 61444
  62.5 1.9 %copy-start.33 = (s32[4,1024]{1,0:T(4,128)S(1)}, s32[4,1024]{1,0:T(4,128)}, u32[]{:S(2)}) copy-start(s32[4,1024]{1,0:T(4,128)} %param.24) | copy-start | bytes 49156
  64.4 4.4 %copy-start.2 = (f32[5,8,1024]{2,1,0:T(8,128)}, f32[5,8,1024]{2,1,0:T(8,128)S(1)}, u32[]{:S(2)}) copy-start(f32[5,8,1024]{2,1,0:T(8,128)S(1)} %get-tuple-element.51.psi_ref) | copy-start | bytes 491524
  68.2 18.6 %copy-start.8 = (f32[1,8,1024]{2,1,0:T(8,128)S(1)}, f32[1,8,1024]{2,1,0:T(8,128)}, u32[]{:S(2)}) copy-start(f32[1,8,1024]{2,1,0:T(8,128)} %param.15) | copy-start | bytes 98308
  68.8 18.1 %copy-start.13 = (f32[8,1024]{1,0:T(8,128)S(1)}, f32[8,1024]{1,0:T(8,128)}, u32[]{:S(2)}) copy-start(f32[8,1024]{1,0:T(8,128)} %copy-done.12) | copy-start | bytes 98308
  68.9 18.1 %copy-start.3 = (f32[5,8,1024]{2,1,0:T(8,128)S(1)}, f32[5,8,1024]{2,1,0:T(8,128)}, u32[]{:S(2)}) copy-start(f32[5,8,1024]{2,1,0:T(8,128)} %copy-done.2) | copy-start | bytes 491524
  85.8 1.2 %copy-start.17 = (f32[5,8,1024]{2,1,0:T(8,128)S(1)}, f32[5,8,1024]{2,1,0:T(8,128)}, u32[]{:S(2)}) copy-start(f32[5,8,1024]{2,1,0:T(8,128)} %get-tuple-element.31) | copy-start | bytes 491524
  85.8 1.2 %copy-start.23 = (f32[5,1,1024]{2,1,0:T(1,128)S(1)}, f32[5,1,1024]{2,1,0:T(1,128)}, u32[]{:S(2)}) copy-start(f32[5,1,1024]{2,1,0:T(1,128)} %get-tuple-element.29) | copy-start | bytes 61444
  85.8 1.2 %copy-start.24 = (f32[5,1,1024]{2,1,0:T(1,128)S(1)}, f32[5,1,1024]{2,1,0:T(1,128)}, u32[]{:S(2)}) copy-start(f32[5,1,1024]{2,1,0:T(1,128)} %get-tuple-element.30) | copy-start | bytes 61444
  87.2 3.8 %copy-start = (f32[5,8,1024]{2,1,0:T(8,128)}, f32[5,8,1024]{2,1,0:T(8,128)S(1)}, u32[]{:S(2)}) copy-start(f32[5,8,1024]{2,1,0:T(8,128)S(1)} %get-tuple-element.45.psi_ref) | copy-start | bytes 491524
  91.0 21.8 %copy-start.1 = (f32[5,8,1024]{2,1,0:T(8,128)S(1)}, f32[5,8,1024]{2,1,0:T(8,128)}, u32[]{:S(2)}) copy-start(f32[5,8,1024]{2,1,0:T(8,128)} %copy-done) | copy-start | bytes 491524
  111.7 1.2 %copy-start.15 = (f32[5,8,1024]{2,1,0:T(8,128)S(1)}, f32[5,8,1024]{2,1,0:T(8,128)}, u32[]{:S(2)}) copy-start(f32[5,8,1024]{2,1,0:T(8,128)} %get-tuple-element.34) | copy-start | bytes 491524
  111.7 1.2 %copy-start.21 = (f32[5,1,1024]{2,1,0:T(1,128)S(1)}, f32[5,1,1024]{2,1,0:T(1,128)}, u32[]{:S(2)}) copy-start(f32[5,1,1024]{2,1,0:T(1,128)} %get-tuple-element.32) | copy-start | bytes 61444
  (3 other events, 2.9 us)

commit v4 on v3

--- a/solution.py
+++ b/solution.py
@@ -135,9 +135,14 @@
     pl.semaphore_wait(barrier, len(devices))
 
 
-def coupling_kernel(count, inner, psi_ref, table_ref, out_ref, below_ref, above_ref, held,
-                    outbox, inbox, below, above, ring_send, ring_recv, cross_send, cross_recv,
-                    edge_send, edge_recv):
+def coupling_kernel(count, inner, gather, psi_ref, table_ref, *refs):
+    if gather:
+        (block_ref, out_ref, below_ref, above_ref, stacked_ref, held, outbox, inbox, below, above,
+         ring_send, ring_recv, cross_send, cross_recv, edge_send, edge_recv, gheld, gsend,
+         grecv) = refs
+    else:
+        (out_ref, below_ref, above_ref, held, outbox, inbox, below, above, ring_send, ring_recv,
+         cross_send, cross_recv, edge_send, edge_recv) = refs
     outer = count // inner
     me = lax.axis_index("inst")
     me_hi, me_lo = me // inner, me % inner
@@ -147,7 +152,19 @@
     slabs = lax.axis_size("space")
     here = lax.axis_index("space")
     up, down = (here + 1) % slabs, (here + slabs - 1) % slabs
-    greet_all([{"inst": p} for p in ring + partners] + [{"space": up}, {"space": down}])
+    if gather:
+        others = [(here + d) % slabs for d in range(1, slabs)]
+        greet_all([{"inst": p} for p in ring + partners] + [{"space": s} for s in others])
+        gathered = []
+        for slot, peer in enumerate(others):
+            copy = pltpu.make_async_remote_copy(
+                src_ref=block_ref, dst_ref=gheld.at[here], send_sem=gsend.at[slot],
+                recv_sem=grecv.at[slot], device_id={"space": peer},
+                device_id_type=pl.DeviceIdType.MESH)
+            copy.start()
+            gathered.append(copy)
+    else:
+        greet_all([{"inst": p} for p in ring + partners] + [{"space": up}, {"space": down}])
     last = psi_ref.shape[1] - 1
     edges = []
     for slot, (peer, layer, land) in enumerate(((up, last, below), (down, 0, above))):
@@ -194,23 +211,39 @@
         copy.wait()
     below_ref[...] = below[:, last:, :]
     above_ref[...] = above[:, :1, :]
-
-
-def instance_coupling(psi, table, step):
+    if gather:
+        for copy in gathered:
+            copy.wait()
+        gheld[here] = block_ref[...]
+        stacked_ref[...] = gheld[...]
+
+
+def instance_coupling(psi, table, step, block=None):
     count = lax.axis_size("inst")
-    assert lax.axis_size("space") > 1
+    slabs = lax.axis_size("space")
+    assert slabs > 2
+    gather = block is not None
     inner = 4 if count % 4 == 0 else count
     outer = count // inner
     comps, layers, plane = psi.shape
     edge = jax.ShapeDtypeStruct((comps, 1, plane), psi.dtype)
+    extra_out, extra_scratch, operands = (), [], (psi, table)
+    if gather:
+        extra_out = (jax.ShapeDtypeStruct((slabs, *block.shape), block.dtype),)
+        extra_scratch = [
+            pltpu.VMEM((slabs, *block.shape), block.dtype),
+            pltpu.SemaphoreType.DMA((slabs - 1,)),
+            pltpu.SemaphoreType.DMA((slabs - 1,)),
+        ]
+        operands = (psi, table, block)
     return pl.pallas_call(
-        functools.partial(coupling_kernel, count, inner),
-        out_shape=(jax.ShapeDtypeStruct(psi.shape, psi.dtype), edge, edge),
+        functools.partial(coupling_kernel, count, inner, gather),
+        out_shape=(jax.ShapeDtypeStruct(psi.shape, psi.dtype), edge, edge) + extra_out,
         in_specs=[
             pl.BlockSpec(memory_space=pltpu.VMEM),
             pl.BlockSpec(memory_space=pltpu.SMEM),
-        ],
-        out_specs=[pl.BlockSpec(memory_space=pltpu.VMEM)] * 3,
+        ] + [pl.BlockSpec(memory_space=pltpu.VMEM)] * gather,
+        out_specs=[pl.BlockSpec(memory_space=pltpu.VMEM)] * (3 + gather),
         scratch_shapes=[
             pltpu.VMEM((inner - 1, *psi.shape), psi.dtype),
             pltpu.VMEM((max(outer - 1, 1), *psi.shape), psi.dtype),
@@ -223,10 +256,10 @@
             pltpu.SemaphoreType.DMA((max(outer - 1, 1),)),
             pltpu.SemaphoreType.DMA((2,)),
             pltpu.SemaphoreType.DMA((2,)),
-        ],
+        ] + extra_scratch,
         compiler_params=pltpu.CompilerParams(collective_id=step, has_side_effects=True),
         name=f"instance_coupling_{step}",
-    )(psi, table)
+    )(*operands)
 
 
 def gather_kernel(count, block_ref, out_ref, held, send_sem, recv_sem):
@@ -322,7 +355,12 @@
     rows, per = local_obs.shape
     assert rows <= 8 and per <= 128
     packed = jnp.zeros((8, 128), jnp.float32).at[:rows, :per].set(local_obs)
-    stacked = space_gather(packed, ITERS)
+    psi = psi_start[:, 0]
+    row_entry = spectral_coeff(
+        jnp.arange(inst_count, dtype=jnp.int32).astype(jnp.float32), float(inst_count)
+    )
+    first = instance_coupling(psi, row_entry, 0, packed)
+    stacked = first[3]
     observers = stacked[:, :rows, :per].transpose(1, 0, 2).reshape(rows, -1)
     owned_count = panel_normal.shape[1]
     piece = owned_count // inst_count
@@ -361,12 +399,11 @@
     onehot = (plane_nbr[:, :, None] == jnp.arange(plane, dtype=jnp.int32)[None, None, :]).astype(
         jnp.bfloat16
     )
-    row_entry = spectral_coeff(
-        jnp.arange(inst_count, dtype=jnp.int32).astype(jnp.float32), float(inst_count)
-    )
-    psi = psi_start[:, 0]
     for step in range(ITERS):
-        spectral_operator, below, above = instance_coupling(psi, row_entry, step)
+        if step == 0:
+            spectral_operator, below, above = first[:3]
+        else:
+            spectral_operator, below, above = instance_coupling(psi, row_entry, step)
         minus_a = jnp.concatenate([below, psi[:, :-1]], axis=1)
         plus_a = jnp.concatenate([psi[:, 1:], above], axis=1)
         plus_y, minus_y, plus_z, minus_z = plane_gather(psi, onehot)

time: 115 us -> 107 us (0.930)
  Pallas kernels: 82.3 us -> 76.1 us
    pallas_call x4 -> x3, Pallas kernels: 74.6 us -> 68.3 us  [instance_coupling(): pl.pallas_call(functools.partial(coupling_kernel, count, inner, gather),...]
where the time goes in v4:
time: 107 us
  Pallas kernels  76.1 us (71%)
  other arithmetic  13.5 us (13%)
  matrix products  13.5 us (13%)
  local copies, waits for them, and re-layouts  2.65 us (2%)
    pallas_call x3, Pallas kernels, instance_coupling(): pl.pallas_call(functools.partial(coupling_kernel, count, inner, gather),...  68.3 us
    dot_general x3, matrix products, plane_gather(): jnp.einsum('pra,kba->kprb', parts, onehot, preferred_element_type=jnp.flo...  11.4 us
    pallas_call x1, Pallas kernels, inst_route(): pl.pallas_call(functools.partial(route_kernel, count), out_shape=jax.Shap...  7.78 us
    mul x1, other arithmetic, shards(): along * jnp.cos(lag)  2.56 us

profile of v4, /device:TPU:1, one launch (start us, length us, event | category | flops | bytes accessed | tf_op | source)
XLA Modules:
  0.0 106.6 jit_solution(10287758069285719780)
XLA Ops:
  0.0 0.9 reduce-precision_convert_fusion.5
  1.0 4.3 %fusion.14 = f32[4,3,40,1024]{3,2,1,0:T(8,128)S(1)} fusion(s32[4,1024]{1,0:T(4,128)} %param.24, bf16[1,40,1024]{2,1,0:T(8,128)(2,1)S(1)} %get-tuple-element.160, bf16[1,40,1024]{2,1,0:T(8,128)(2,1)S(1)} %get-tuple-element.161, bf16[1,40,1024]{2,1,0:T(8,128)(2,1)S(1)} %get-tuple-element.159), kind=kOutput, calls=%fused_computation.14 | convolution fusion | flops 1011564544 | bytes 2228224 | tf_op jit(solution)/shard_map/pra,kba->kprb/dot_general | solution.py:109
  5.3 0.1 slice_add_fusion.4
  5.5 0.6 compare_select_fusion.table_ref
  6.1 0.6 select_maximum_fusion.refs_0_
  6.7 28.9 %instance_coupling_0.1 = (f32[5,8,1024]{2,1,0:T(8,128)}, f32[5,1,1024]{2,1,0:T(1,128)}, f32[5,1,1024]{2,1,0:T(1,128)}, f32[32,8,128]{2,1,0:T(8,128)}) custom-call(f32[5,8,1024]{2,1,0:T(8,128)} %bitcast.183, f32[8]{0:T(128)} %compare_select_fusion.table_ref, f32[8,128]{1,0:T(8,128)} %select_maximum_fusion.refs_0_), custom_call_target="tpu_custom_call" | custom-call | tf_op jit(solution)/shard_map/instance_coupling_0/pallas_call | solution.py:239
  35.7 0.9 subtract_multiply_fusion.10
  36.7 0.6 slice_multiply_fusion.70
  37.4 0.6 add_add_fusion.2
  38.0 0.7 fusion.53
  38.8 0.6 negate_bitcast_fusion.2
  39.4 0.7 constant_dynamic-slice_fusion
  40.3 0.3 fusion.23
  40.6 0.1 slice_reduce_fusion.2
  40.9 2.6 %cosine_multiply_fusion = (f32[512,256]{1,0:T(8,128)S(1)}, f32[512,256]{1,0:T(8,128)S(1)}) fusion(f32[512,256]{1,0:T(8,128)S(1)} %get-tuple-element.41, f32[512]{0:T(512)S(1)} %broadcast_multiply_fusion, f32[512,256]{1,0:T(8,128)S(1)} %get-tuple-element.40), kind=kLoop, calls=%fused_computation.33 | loop fusion | flops 786432 | bytes 2099200 | tf_op jit(solution)/shard_map/mul | solution.py:378
  43.6 0.1 fusion.73
  43.8 0.5 fusion.25
  44.4 0.6 reshape.481.rows_ref
  45.0 7.8 %inst_route.1 = f32[8,2,128]{2,1,0:T(2,128)} custom-call(f32[8,2,128]{2,1,0:T(2,128)} %reshape.481.rows_ref), custom_call_target="tpu_custom_call" | custom-call | tf_op jit(solution)/shard_map/inst_route/pallas_call | solution.py:320
  52.8 0.7 reduce-precision_convert_fusion.7
  53.5 1.6 %fusion.11 = f32[3,8,1024]{2,1,0:T(8,128)S(1)} fusion(s32[2048]{0:T(1024)S(1)} %get-tuple-element.188, bf16[1,8,2048]{2,1,0:T(8,128)(2,1)S(1)} %get-tuple-element.186, bf16[1,8,2048]{2,1,0:T(8,128)(2,1)S(1)} %get-tuple-element.185, bf16[1,8,2048]{2,1,0:T(8,128)(2,1)S(1)} %get-tuple-element.184), kind=kOutput, calls=%fused_computation.10 | convolution fusion | flops 102858752 | bytes 204800 | tf_op jit(solution)/shard_map/plq,qb->plb/dot_general | solution.py:122
  55.2 0.2 reduce-precision_convert_fusion.3
  55.5 3.6 %fusion.17 = f32[4,3,40,1024]{3,2,1,0:T(8,128)S(1)} fusion(s32[4,1024]{1,0:T(4,128)S(1)} %copy-done.34, bf16[1,40,1024]{2,1,0:T(8,128)(2,1)S(1)} %get-tuple-element.146, bf16[1,40,1024]{2,1,0:T(8,128)(2,1)S(1)} %get-tuple-element.145, bf16[1,40,1024]{2,1,0:T(8,128)(2,1)S(1)} %get-tuple-element.52), kind=kOutput, calls=%fused_computation.15 | convolution fusion | flops 1011564544 | bytes 2228224 | tf_op jit(solution)/shard_map/pra,kba->kprb/dot_general | solution.py:109
  59.0 0.1 slice_add_fusion.2
  59.2 0.6 copy-done.10
  59.9 15.4 %instance_coupling_1.1 = (f32[5,8,1024]{2,1,0:T(8,128)}, f32[5,1,1024]{2,1,0:T(1,128)}, f32[5,1,1024]{2,1,0:T(1,128)}) custom-call(f32[5,8,1024]{2,1,0:T(8,128)} %copy-done.2, f32[8]{0:T(128)} %compare_select_fusion.table_ref), custom_call_target="tpu_custom_call" | custom-call | tf_op jit(solution)/shard_map/instance_coupling_1/pallas_call | solution.py:239
  75.3 0.9 subtract_multiply_fusion.5
  76.5 0.2 reduce-precision_convert_fusion.1
  76.7 3.5 %fusion.20 = f32[4,3,40,1024]{3,2,1,0:T(8,128)S(1)} fusion(s32[4,1024]{1,0:T(4,128)S(1)} %copy-done.34, bf16[1,40,1024]{2,1,0:T(8,128)(2,1)S(1)} %get-tuple-element.131, bf16[1,40,1024]{2,1,0:T(8,128)(2,1)S(1)} %get-tuple-element.130, bf16[1,40,1024]{2,1,0:T(8,128)(2,1)S(1)} %get-tuple-element.46), kind=kOutput, calls=%fused_computation.16 | convolution fusion | flops 1011564544 | bytes 2228224 | tf_op jit(solution)/shard_map/pra,kba->kprb/dot_general | solution.py:109
  80.5 24.0 %instance_coupling_2.1 = (f32[5,8,1024]{2,1,0:T(8,128)}, f32[5,1,1024]{2,1,0:T(1,128)}, f32[5,1,1024]{2,1,0:T(1,128)}) custom-call(f32[5,8,1024]{2,1,0:T(8,128)} %copy-done, f32[8]{0:T(128)} %compare_select_fusion.table_ref), custom_call_target="tpu_custom_call" | custom-call | tf_op jit(solution)/shard_map/instance_coupling_2/pallas_call | solution.py:239
  104.6 0.9 subtract_multiply_fusion.2
  105.7 0.8 subtract_bitcast_fusion
  (110 shorter events, 1.5 us)
Async XLA Ops:
  5.3 30.3 %copy-start.4 = (f32[5,1,8,1024]{3,2,1,0:T(8,128)S(1)}, f32[5,1,8,1024]{3,2,1,0:T(8,128)}, u32[]{:S(2)}) copy-start(f32[5,1,8,1024]{3,2,1,0:T(8,128)} %param.14) | copy-start | bytes 491524
  5.3 31.3 %copy-start.7 = (f32[1,8,1024]{2,1,0:T(8,128)S(1)}, f32[1,8,1024]{2,1,0:T(8,128)}, u32[]{:S(2)}) copy-start(f32[1,8,1024]{2,1,0:T(8,128)} %param.15) | copy-start | bytes 98308
  5.3 31.3 %copy-start.21 = (f32[3,1,8,1024]{3,2,1,0:T(8,128)S(1)}, f32[3,1,8,1024]{3,2,1,0:T(8,128)}, u32[]{:S(2)}) copy-start(f32[3,1,8,1024]{3,2,1,0:T(8,128)} %param.16) | copy-start | bytes 294916
  5.4 31.2 %copy-start.28 = (f32[1,8,1024]{2,1,0:T(8,128)S(1)}, f32[1,8,1024]{2,1,0:T(8,128)}, u32[]{:S(2)}) copy-start(f32[1,8,1024]{2,1,0:T(8,128)} %param.17) | copy-start | bytes 98308
  35.7 0.9 copy-start.5
  35.7 2.4 %copy-start.30 = (pred[3]{0:T(512)(128)(4,1)S(1)}, pred[3]{0:T(512)(128)(4,1)}, u32[]{:S(2)}) copy-start(pred[3]{0:T(512)(128)(4,1)} %constant.102.clone.1) | copy-start | bytes 13
  36.7 3.4 %copy-start.20 = (f32[32,8,128]{2,1,0:T(8,128)S(1)}, f32[32,8,128]{2,1,0:T(8,128)}, u32[]{:S(2)}) copy-start(f32[32,8,128]{2,1,0:T(8,128)} %get-tuple-element.30) | copy-start | bytes 393220
  37.3 3.2 %copy-start.9 = (f32[1,8,1024]{2,1,0:T(8,128)}, f32[1,8,1024]{2,1,0:T(8,128)S(1)}, u32[]{:S(2)}) copy-start(f32[1,8,1024]{2,1,0:T(8,128)S(1)} %get-tuple-element.148) | copy-start | bytes 98308
  37.4 3.3 %copy-start.12 = (f32[8,1024]{1,0:T(8,128)}, f32[8,1024]{1,0:T(8,128)S(1)}, u32[]{:S(2)}) copy-start(f32[8,1024]{1,0:T(8,128)S(1)} %get-tuple-element.182) | copy-start | bytes 98308
  39.4 4.2 %copy-start.33 = (f32[8]{0:T(128)S(1)}, f32[8]{0:T(128)}, u32[]{:S(2)}) copy-start(f32[8]{0:T(128)} %constant.121.clone) | copy-start | bytes 100
  40.6 12.1 %copy-start.29 = (s32[2048]{0:T(1024)S(1)}, s32[2048]{0:T(1024)}, u32[]{:S(2)}) copy-start(s32[2048]{0:T(1024)} %param.23) | copy-start | bytes 24580
  43.7 11.4 %copy-start.6 = (f32[5,7,1024]{2,1,0:T(8,128)S(1)}, f32[5,7,1024]{2,1,0:T(8,128)}, u32[]{:S(2)}) copy-start(f32[5,7,1024]{2,1,0:T(8,128)} %copy-done.5) | copy-start | bytes 430084
  43.8 11.4 %copy-start.11 = (f32[1,8,1024]{2,1,0:T(8,128)S(1)}, f32[1,8,1024]{2,1,0:T(8,128)}, u32[]{:S(2)}) copy-start(f32[1,8,1024]{2,1,0:T(8,128)} %get-tuple-element.183) | copy-start | bytes 98308
  43.8 11.4 %copy-start.14 = (f32[3,8,1024]{2,1,0:T(8,128)S(1)}, f32[3,8,1024]{2,1,0:T(8,128)}, u32[]{:S(2)}) copy-start(f32[3,8,1024]{2,1,0:T(8,128)} %get-tuple-element.56) | copy-start | bytes 294916
  43.8 11.4 %copy-start.16 = (f32[5,8,1024]{2,1,0:T(8,128)S(1)}, f32[5,8,1024]{2,1,0:T(8,128)}, u32[]{:S(2)}) copy-start(f32[5,8,1024]{2,1,0:T(8,128)} %get-tuple-element.29) | copy-start | bytes 491524
  43.8 11.4 %copy-start.18 = (f32[1,8,1024]{2,1,0:T(8,128)S(1)}, f32[1,8,1024]{2,1,0:T(8,128)}, u32[]{:S(2)}) copy-start(f32[1,8,1024]{2,1,0:T(8,128)} %get-tuple-element.54) | copy-start | bytes 98308
  43.8 11.4 %copy-start.19 = (f32[1,8,1024]{2,1,0:T(8,128)S(1)}, f32[1,8,1024]{2,1,0:T(8,128)}, u32[]{:S(2)}) copy-start(f32[1,8,1024]{2,1,0:T(8,128)} %negate_bitcast_fusion.2) | copy-start | bytes 98308
  43.8 11.4 %copy-start.26 = (f32[5,1,1024]{2,1,0:T(1,128)S(1)}, f32[5,1,1024]{2,1,0:T(1,128)}, u32[]{:S(2)}) copy-start(f32[5,1,1024]{2,1,0:T(1,128)} %get-tuple-element.27) | copy-start | bytes 61444
  43.8 11.4 %copy-start.27 = (f32[5,1,1024]{2,1,0:T(1,128)S(1)}, f32[5,1,1024]{2,1,0:T(1,128)}, u32[]{:S(2)}) copy-start(f32[5,1,1024]{2,1,0:T(1,128)} %get-tuple-element.28) | copy-start | bytes 61444
  53.5 1.9 %copy-start.34 = (s32[4,1024]{1,0:T(4,128)S(1)}, s32[4,1024]{1,0:T(4,128)}, u32[]{:S(2)}) copy-start(s32[4,1024]{1,0:T(4,128)} %param.24) | copy-start | bytes 49156
  55.4 4.4 %copy-start.2 = (f32[5,8,1024]{2,1,0:T(8,128)}, f32[5,8,1024]{2,1,0:T(8,128)S(1)}, u32[]{:S(2)}) copy-start(f32[5,8,1024]{2,1,0:T(8,128)S(1)} %get-tuple-element.53.psi_ref) | copy-start | bytes 491524
  59.2 17.1 %copy-start.8 = (f32[1,8,1024]{2,1,0:T(8,128)S(1)}, f32[1,8,1024]{2,1,0:T(8,128)}, u32[]{:S(2)}) copy-start(f32[1,8,1024]{2,1,0:T(8,128)} %param.15) | copy-start | bytes 98308
  59.8 16.6 %copy-start.13 = (f32[8,1024]{1,0:T(8,128)S(1)}, f32[8,1024]{1,0:T(8,128)}, u32[]{:S(2)}) copy-start(f32[8,1024]{1,0:T(8,128)} %copy-done.12) | copy-start | bytes 98308
  59.9 16.6 %copy-start.3 = (f32[5,8,1024]{2,1,0:T(8,128)S(1)}, f32[5,8,1024]{2,1,0:T(8,128)}, u32[]{:S(2)}) copy-start(f32[5,8,1024]{2,1,0:T(8,128)} %copy-done.2) | copy-start | bytes 491524
  75.3 1.2 %copy-start.17 = (f32[5,8,1024]{2,1,0:T(8,128)S(1)}, f32[5,8,1024]{2,1,0:T(8,128)}, u32[]{:S(2)}) copy-start(f32[5,8,1024]{2,1,0:T(8,128)} %get-tuple-element.33) | copy-start | bytes 491524
  75.3 1.2 %copy-start.24 = (f32[5,1,1024]{2,1,0:T(1,128)S(1)}, f32[5,1,1024]{2,1,0:T(1,128)}, u32[]{:S(2)}) copy-start(f32[5,1,1024]{2,1,0:T(1,128)} %get-tuple-element.31) | copy-start | bytes 61444
  75.3 1.2 %copy-start.25 = (f32[5,1,1024]{2,1,0:T(1,128)S(1)}, f32[5,1,1024]{2,1,0:T(1,128)}, u32[]{:S(2)}) copy-start(f32[5,1,1024]{2,1,0:T(1,128)} %get-tuple-element.32) | copy-start | bytes 61444
  76.6 3.8 %copy-start = (f32[5,8,1024]{2,1,0:T(8,128)}, f32[5,8,1024]{2,1,0:T(8,128)S(1)}, u32[]{:S(2)}) copy-start(f32[5,8,1024]{2,1,0:T(8,128)S(1)} %get-tuple-element.47.psi_ref) | copy-start | bytes 491524
  80.5 25.2 %copy-start.1 = (f32[5,8,1024]{2,1,0:T(8,128)S(1)}, f32[5,8,1024]{2,1,0:T(8,128)}, u32[]{:S(2)}) copy-start(f32[5,8,1024]{2,1,0:T(8,128)} %copy-done) | copy-start | bytes 491524
  104.6 1.2 %copy-start.15 = (f32[5,8,1024]{2,1,0:T(8,128)S(1)}, f32[5,8,1024]{2,1,0:T(8,128)}, u32[]{:S(2)}) copy-start(f32[5,8,1024]{2,1,0:T(8,128)} %get-tuple-element.36) | copy-start | bytes 491524
  104.6 1.2 %copy-start.22 = (f32[5,1,1024]{2,1,0:T(1,128)S(1)}, f32[5,1,1024]{2,1,0:T(1,128)}, u32[]{:S(2)}) copy-start(f32[5,1,1024]{2,1,0:T(1,128)} %get-tuple-element.34) | copy-start | bytes 61444
  104.6 1.2 %copy-start.23 = (f32[5,1,1024]{2,1,0:T(1,128)S(1)}, f32[5,1,1024]{2,1,0:T(1,128)}, u32[]{:S(2)}) copy-start(f32[5,1,1024]{2,1,0:T(1,128)} %get-tuple-element.35) | copy-start | bytes 61444
  (4 other events, 3.4 us)

commit v5 on v4

--- a/solution.py
+++ b/solution.py
@@ -178,35 +178,45 @@
     def coef(row, col):
         return table_ref[(row - col) % count]
 
+    halves = 2
+    width = psi_ref.shape[2] // halves
+    spans = [pl.ds(h * width, width) for h in range(halves)]
     copies = []
-    for slot, peer in enumerate(ring):
-        copy = pltpu.make_async_remote_copy(
-            src_ref=psi_ref, dst_ref=held.at[slot], send_sem=ring_send.at[slot],
-            recv_sem=ring_recv.at[slot], device_id={"inst": peer},
-            device_id_type=pl.DeviceIdType.MESH)
-        copy.start()
-        copies.append(copy)
-    for copy in copies:
+    for h, cols in enumerate(spans):
+        row = []
+        for slot, peer in enumerate(ring):
+            at = h * len(ring) + slot
+            copy = pltpu.make_async_remote_copy(
+                src_ref=psi_ref.at[:, :, cols], dst_ref=held.at[slot, :, :, cols],
+                send_sem=ring_send.at[at], recv_sem=ring_recv.at[at],
+                device_id={"inst": peer}, device_id_type=pl.DeviceIdType.MESH)
+            copy.start()
+            row.append(copy)
+        copies.append(row)
+    cross = []
+    for h, cols in enumerate(spans):
+        for copy in copies[h]:
+            copy.wait()
+        for slot, partner in enumerate(partners):
+            at = h * len(partners) + slot
+            part = coef(partner, me) * psi_ref[:, :, cols]
+            for d, source in enumerate(ring_from):
+                part = part + coef(partner, source) * held[d, :, :, cols]
+            outbox[slot, :, :, cols] = part
+            copy = pltpu.make_async_remote_copy(
+                src_ref=outbox.at[slot, :, :, cols], dst_ref=inbox.at[slot, :, :, cols],
+                send_sem=cross_send.at[at], recv_sem=cross_recv.at[at],
+                device_id={"inst": partner}, device_id_type=pl.DeviceIdType.MESH)
+            copy.start()
+            cross.append((h, slot, copy))
+    for h, cols in enumerate(spans):
+        total = coef(me, me) * psi_ref[:, :, cols]
+        for d, source in enumerate(ring_from):
+            total = total + coef(me, source) * held[d, :, :, cols]
+        out_ref[:, :, cols] = total
+    for h, slot, copy in cross:
         copy.wait()
-    cross = []
-    for slot, partner in enumerate(partners):
-        part = coef(partner, me) * psi_ref[...]
-        for d, source in enumerate(ring_from):
-            part = part + coef(partner, source) * held[d]
-        outbox[slot] = part
-        copy = pltpu.make_async_remote_copy(
-            src_ref=outbox.at[slot], dst_ref=inbox.at[slot], send_sem=cross_send.at[slot],
-            recv_sem=cross_recv.at[slot], device_id={"inst": partner},
-            device_id_type=pl.DeviceIdType.MESH)
-        copy.start()
-        cross.append(copy)
-    total = coef(me, me) * psi_ref[...]
-    for d, source in enumerate(ring_from):
-        total = total + coef(me, source) * held[d]
-    for slot, copy in enumerate(cross):
-        copy.wait()
-        total = total + inbox[slot]
-    out_ref[...] = total
+        out_ref[:, :, spans[h]] = out_ref[:, :, spans[h]] + inbox[slot, :, :, spans[h]]
     for copy in edges:
         copy.wait()
     below_ref[...] = below[:, last:, :]
@@ -250,10 +260,10 @@
             pltpu.VMEM((max(outer - 1, 1), *psi.shape), psi.dtype),
             pltpu.VMEM(psi.shape, psi.dtype),
             pltpu.VMEM(psi.shape, psi.dtype),
-            pltpu.SemaphoreType.DMA((inner - 1,)),
-            pltpu.SemaphoreType.DMA((inner - 1,)),
-            pltpu.SemaphoreType.DMA((max(outer - 1, 1),)),
-            pltpu.SemaphoreType.DMA((max(outer - 1, 1),)),
+            pltpu.SemaphoreType.DMA((2 * (inner - 1),)),
+            pltpu.SemaphoreType.DMA((2 * (inner - 1),)),
+            pltpu.SemaphoreType.DMA((2 * max(outer - 1, 1),)),
+            pltpu.SemaphoreType.DMA((2 * max(outer - 1, 1),)),
             pltpu.SemaphoreType.DMA((2,)),
             pltpu.SemaphoreType.DMA((2,)),
         ] + extra_scratch,

time: 107 us -> 102 us (0.953)
  Pallas kernels: 76.1 us -> 71.4 us
    pallas_call x3, Pallas kernels: 68.3 us -> 63.6 us  [instance_coupling(): pl.pallas_call(functools.partial(coupling_kernel, count, inner, gather),...]
where the time goes in v5:
time: 102 us
  Pallas kernels  71.4 us (70%)
  other arithmetic  13.5 us (13%)
  matrix products  13.5 us (13%)
  local copies, waits for them, and re-layouts  2.65 us (3%)
    pallas_call x3, Pallas kernels, instance_coupling(): pl.pallas_call(functools.partial(coupling_kernel, count, inner, gather),...  63.6 us
    dot_general x3, matrix products, plane_gather(): jnp.einsum('pra,kba->kprb', parts, onehot, preferred_element_type=jnp.flo...  11.4 us
    pallas_call x1, Pallas kernels, inst_route(): pl.pallas_call(functools.partial(route_kernel, count), out_shape=jax.Shap...  7.78 us
    mul x1, other arithmetic, shards(): along * jnp.cos(lag)  2.56 us
    another operation x6, other arithmetic  2.08 us

profile of v5, /device:TPU:1, one launch (start us, length us, event | category | flops | bytes accessed | tf_op | source)
XLA Modules:
  0.0 101.9 jit_solution(11223641355023229732)
XLA Ops:
  0.0 0.9 reduce-precision_convert_fusion.5
  1.0 4.3 %fusion.14 = f32[4,3,40,1024]{3,2,1,0:T(8,128)S(1)} fusion(s32[4,1024]{1,0:T(4,128)} %param.24, bf16[1,40,1024]{2,1,0:T(8,128)(2,1)S(1)} %get-tuple-element.160, bf16[1,40,1024]{2,1,0:T(8,128)(2,1)S(1)} %get-tuple-element.161, bf16[1,40,1024]{2,1,0:T(8,128)(2,1)S(1)} %get-tuple-element.159), kind=kOutput, calls=%fused_computation.14 | convolution fusion | flops 1011564544 | bytes 2228224 | tf_op jit(solution)/shard_map/pra,kba->kprb/dot_general | solution.py:109
  5.3 0.1 slice_add_fusion.4
  5.5 0.6 compare_select_fusion.table_ref
  6.1 0.6 select_maximum_fusion.refs_0_
  6.7 27.1 %instance_coupling_0.1 = (f32[5,8,1024]{2,1,0:T(8,128)}, f32[5,1,1024]{2,1,0:T(1,128)}, f32[5,1,1024]{2,1,0:T(1,128)}, f32[32,8,128]{2,1,0:T(8,128)}) custom-call(f32[5,8,1024]{2,1,0:T(8,128)} %bitcast.183, f32[8]{0:T(128)} %compare_select_fusion.table_ref, f32[8,128]{1,0:T(8,128)} %select_maximum_fusion.refs_0_), custom_call_target="tpu_custom_call" | custom-call | tf_op jit(solution)/shard_map/instance_coupling_0/pallas_call | solution.py:249
  33.9 0.9 subtract_multiply_fusion.10
  35.0 0.6 slice_multiply_fusion.70
  35.6 0.6 add_add_fusion.2
  36.3 0.7 fusion.53
  37.1 0.6 negate_bitcast_fusion.2
  37.7 0.7 constant_dynamic-slice_fusion
  38.5 0.3 fusion.23
  38.9 0.1 slice_reduce_fusion.2
  39.1 2.6 %cosine_multiply_fusion = (f32[512,256]{1,0:T(8,128)S(1)}, f32[512,256]{1,0:T(8,128)S(1)}) fusion(f32[512,256]{1,0:T(8,128)S(1)} %get-tuple-element.41, f32[512]{0:T(512)S(1)} %broadcast_multiply_fusion, f32[512,256]{1,0:T(8,128)S(1)} %get-tuple-element.40), kind=kLoop, calls=%fused_computation.33 | loop fusion | flops 786432 | bytes 2099200 | tf_op jit(solution)/shard_map/mul | solution.py:388
  41.9 0.1 fusion.73
  42.1 0.5 fusion.25
  42.6 0.6 reshape.481.rows_ref
  43.2 7.8 %inst_route.1 = f32[8,2,128]{2,1,0:T(2,128)} custom-call(f32[8,2,128]{2,1,0:T(2,128)} %reshape.481.rows_ref), custom_call_target="tpu_custom_call" | custom-call | tf_op jit(solution)/shard_map/inst_route/pallas_call | solution.py:330
  51.0 0.7 reduce-precision_convert_fusion.7
  51.8 1.6 %fusion.11 = f32[3,8,1024]{2,1,0:T(8,128)S(1)} fusion(s32[2048]{0:T(1024)S(1)} %get-tuple-element.188, bf16[1,8,2048]{2,1,0:T(8,128)(2,1)S(1)} %get-tuple-element.186, bf16[1,8,2048]{2,1,0:T(8,128)(2,1)S(1)} %get-tuple-element.185, bf16[1,8,2048]{2,1,0:T(8,128)(2,1)S(1)} %get-tuple-element.184), kind=kOutput, calls=%fused_computation.10 | convolution fusion | flops 102858752 | bytes 204800 | tf_op jit(solution)/shard_map/plq,qb->plb/dot_general | solution.py:122
  53.5 0.2 reduce-precision_convert_fusion.3
  53.7 3.5 %fusion.17 = f32[4,3,40,1024]{3,2,1,0:T(8,128)S(1)} fusion(s32[4,1024]{1,0:T(4,128)S(1)} %copy-done.34, bf16[1,40,1024]{2,1,0:T(8,128)(2,1)S(1)} %get-tuple-element.146, bf16[1,40,1024]{2,1,0:T(8,128)(2,1)S(1)} %get-tuple-element.145, bf16[1,40,1024]{2,1,0:T(8,128)(2,1)S(1)} %get-tuple-element.52), kind=kOutput, calls=%fused_computation.15 | convolution fusion | flops 1011564544 | bytes 2228224 | tf_op jit(solution)/shard_map/pra,kba->kprb/dot_general | solution.py:109
  57.3 0.1 slice_add_fusion.2
  57.5 0.6 copy-done.10
  58.1 15.0 %instance_coupling_1.1 = (f32[5,8,1024]{2,1,0:T(8,128)}, f32[5,1,1024]{2,1,0:T(1,128)}, f32[5,1,1024]{2,1,0:T(1,128)}) custom-call(f32[5,8,1024]{2,1,0:T(8,128)} %copy-done.2, f32[8]{0:T(128)} %compare_select_fusion.table_ref), custom_call_target="tpu_custom_call" | custom-call | tf_op jit(solution)/shard_map/instance_coupling_1/pallas_call | solution.py:249
  73.1 0.9 subtract_multiply_fusion.5
  74.3 0.2 reduce-precision_convert_fusion.1
  74.5 3.5 %fusion.20 = f32[4,3,40,1024]{3,2,1,0:T(8,128)S(1)} fusion(s32[4,1024]{1,0:T(4,128)S(1)} %copy-done.34, bf16[1,40,1024]{2,1,0:T(8,128)(2,1)S(1)} %get-tuple-element.131, bf16[1,40,1024]{2,1,0:T(8,128)(2,1)S(1)} %get-tuple-element.130, bf16[1,40,1024]{2,1,0:T(8,128)(2,1)S(1)} %get-tuple-element.46), kind=kOutput, calls=%fused_computation.16 | convolution fusion | flops 1011564544 | bytes 2228224 | tf_op jit(solution)/shard_map/pra,kba->kprb/dot_general | solution.py:109
  78.4 21.5 %instance_coupling_2.1 = (f32[5,8,1024]{2,1,0:T(8,128)}, f32[5,1,1024]{2,1,0:T(1,128)}, f32[5,1,1024]{2,1,0:T(1,128)}) custom-call(f32[5,8,1024]{2,1,0:T(8,128)} %copy-done, f32[8]{0:T(128)} %compare_select_fusion.table_ref), custom_call_target="tpu_custom_call" | custom-call | tf_op jit(solution)/shard_map/instance_coupling_2/pallas_call | solution.py:249
  99.9 0.9 subtract_multiply_fusion.2
  101.1 0.8 subtract_bitcast_fusion
  (110 shorter events, 1.5 us)
Async XLA Ops:
  5.3 28.6 %copy-start.4 = (f32[5,1,8,1024]{3,2,1,0:T(8,128)S(1)}, f32[5,1,8,1024]{3,2,1,0:T(8,128)}, u32[]{:S(2)}) copy-start(f32[5,1,8,1024]{3,2,1,0:T(8,128)} %param.14) | copy-start | bytes 491524
  5.3 29.6 %copy-start.7 = (f32[1,8,1024]{2,1,0:T(8,128)S(1)}, f32[1,8,1024]{2,1,0:T(8,128)}, u32[]{:S(2)}) copy-start(f32[1,8,1024]{2,1,0:T(8,128)} %param.15) | copy-start | bytes 98308
  5.3 29.6 %copy-start.21 = (f32[3,1,8,1024]{3,2,1,0:T(8,128)S(1)}, f32[3,1,8,1024]{3,2,1,0:T(8,128)}, u32[]{:S(2)}) copy-start(f32[3,1,8,1024]{3,2,1,0:T(8,128)} %param.16) | copy-start | bytes 294916
  5.4 29.5 %copy-start.28 = (f32[1,8,1024]{2,1,0:T(8,128)S(1)}, f32[1,8,1024]{2,1,0:T(8,128)}, u32[]{:S(2)}) copy-start(f32[1,8,1024]{2,1,0:T(8,128)} %param.17) | copy-start | bytes 98308
  33.9 0.9 copy-start.5
  33.9 2.4 %copy-start.30 = (pred[3]{0:T(512)(128)(4,1)S(1)}, pred[3]{0:T(512)(128)(4,1)}, u32[]{:S(2)}) copy-start(pred[3]{0:T(512)(128)(4,1)} %constant.102.clone.1) | copy-start | bytes 13
  35.0 3.4 %copy-start.20 = (f32[32,8,128]{2,1,0:T(8,128)S(1)}, f32[32,8,128]{2,1,0:T(8,128)}, u32[]{:S(2)}) copy-start(f32[32,8,128]{2,1,0:T(8,128)} %get-tuple-element.30) | copy-start | bytes 393220
  35.6 3.2 %copy-start.9 = (f32[1,8,1024]{2,1,0:T(8,128)}, f32[1,8,1024]{2,1,0:T(8,128)S(1)}, u32[]{:S(2)}) copy-start(f32[1,8,1024]{2,1,0:T(8,128)S(1)} %get-tuple-element.148) | copy-start | bytes 98308
  35.6 3.3 %copy-start.12 = (f32[8,1024]{1,0:T(8,128)}, f32[8,1024]{1,0:T(8,128)S(1)}, u32[]{:S(2)}) copy-start(f32[8,1024]{1,0:T(8,128)S(1)} %get-tuple-element.182) | copy-start | bytes 98308
  37.7 4.2 %copy-start.33 = (f32[8]{0:T(128)S(1)}, f32[8]{0:T(128)}, u32[]{:S(2)}) copy-start(f32[8]{0:T(128)} %constant.121.clone) | copy-start | bytes 100
  38.9 12.1 %copy-start.29 = (s32[2048]{0:T(1024)S(1)}, s32[2048]{0:T(1024)}, u32[]{:S(2)}) copy-start(s32[2048]{0:T(1024)} %param.23) | copy-start | bytes 24580
  42.0 11.4 %copy-start.6 = (f32[5,7,1024]{2,1,0:T(8,128)S(1)}, f32[5,7,1024]{2,1,0:T(8,128)}, u32[]{:S(2)}) copy-start(f32[5,7,1024]{2,1,0:T(8,128)} %copy-done.5) | copy-start | bytes 430084
  42.0 11.4 %copy-start.11 = (f32[1,8,1024]{2,1,0:T(8,128)S(1)}, f32[1,8,1024]{2,1,0:T(8,128)}, u32[]{:S(2)}) copy-start(f32[1,8,1024]{2,1,0:T(8,128)} %get-tuple-element.183) | copy-start | bytes 98308
  42.0 11.4 %copy-start.14 = (f32[3,8,1024]{2,1,0:T(8,128)S(1)}, f32[3,8,1024]{2,1,0:T(8,128)}, u32[]{:S(2)}) copy-start(f32[3,8,1024]{2,1,0:T(8,128)} %get-tuple-element.56) | copy-start | bytes 294916
  42.0 11.4 %copy-start.16 = (f32[5,8,1024]{2,1,0:T(8,128)S(1)}, f32[5,8,1024]{2,1,0:T(8,128)}, u32[]{:S(2)}) copy-start(f32[5,8,1024]{2,1,0:T(8,128)} %get-tuple-element.29) | copy-start | bytes 491524
  42.0 11.4 %copy-start.18 = (f32[1,8,1024]{2,1,0:T(8,128)S(1)}, f32[1,8,1024]{2,1,0:T(8,128)}, u32[]{:S(2)}) copy-start(f32[1,8,1024]{2,1,0:T(8,128)} %get-tuple-element.54) | copy-start | bytes 98308
  42.1 11.4 %copy-start.19 = (f32[1,8,1024]{2,1,0:T(8,128)S(1)}, f32[1,8,1024]{2,1,0:T(8,128)}, u32[]{:S(2)}) copy-start(f32[1,8,1024]{2,1,0:T(8,128)} %negate_bitcast_fusion.2) | copy-start | bytes 98308
  42.1 11.4 %copy-start.26 = (f32[5,1,1024]{2,1,0:T(1,128)S(1)}, f32[5,1,1024]{2,1,0:T(1,128)}, u32[]{:S(2)}) copy-start(f32[5,1,1024]{2,1,0:T(1,128)} %get-tuple-element.27) | copy-start | bytes 61444
  42.1 11.4 %copy-start.27 = (f32[5,1,1024]{2,1,0:T(1,128)S(1)}, f32[5,1,1024]{2,1,0:T(1,128)}, u32[]{:S(2)}) copy-start(f32[5,1,1024]{2,1,0:T(1,128)} %get-tuple-element.28) | copy-start | bytes 61444
  51.8 1.9 %copy-start.34 = (s32[4,1024]{1,0:T(4,128)S(1)}, s32[4,1024]{1,0:T(4,128)}, u32[]{:S(2)}) copy-start(s32[4,1024]{1,0:T(4,128)} %param.24) | copy-start | bytes 49156
  53.7 4.4 %copy-start.2 = (f32[5,8,1024]{2,1,0:T(8,128)}, f32[5,8,1024]{2,1,0:T(8,128)S(1)}, u32[]{:S(2)}) copy-start(f32[5,8,1024]{2,1,0:T(8,128)S(1)} %get-tuple-element.53.psi_ref) | copy-start | bytes 491524
  57.5 16.6 %copy-start.8 = (f32[1,8,1024]{2,1,0:T(8,128)S(1)}, f32[1,8,1024]{2,1,0:T(8,128)}, u32[]{:S(2)}) copy-start(f32[1,8,1024]{2,1,0:T(8,128)} %param.15) | copy-start | bytes 98308
  58.1 16.2 %copy-start.13 = (f32[8,1024]{1,0:T(8,128)S(1)}, f32[8,1024]{1,0:T(8,128)}, u32[]{:S(2)}) copy-start(f32[8,1024]{1,0:T(8,128)} %copy-done.12) | copy-start | bytes 98308
  58.1 16.2 %copy-start.3 = (f32[5,8,1024]{2,1,0:T(8,128)S(1)}, f32[5,8,1024]{2,1,0:T(8,128)}, u32[]{:S(2)}) copy-start(f32[5,8,1024]{2,1,0:T(8,128)} %copy-done.2) | copy-start | bytes 491524
  73.1 1.2 %copy-start.17 = (f32[5,8,1024]{2,1,0:T(8,128)S(1)}, f32[5,8,1024]{2,1,0:T(8,128)}, u32[]{:S(2)}) copy-start(f32[5,8,1024]{2,1,0:T(8,128)} %get-tuple-element.33) | copy-start | bytes 491524
  73.1 1.2 %copy-start.24 = (f32[5,1,1024]{2,1,0:T(1,128)S(1)}, f32[5,1,1024]{2,1,0:T(1,128)}, u32[]{:S(2)}) copy-start(f32[5,1,1024]{2,1,0:T(1,128)} %get-tuple-element.31) | copy-start | bytes 61444
  73.1 1.2 %copy-start.25 = (f32[5,1,1024]{2,1,0:T(1,128)S(1)}, f32[5,1,1024]{2,1,0:T(1,128)}, u32[]{:S(2)}) copy-start(f32[5,1,1024]{2,1,0:T(1,128)} %get-tuple-element.32) | copy-start | bytes 61444
  74.5 3.8 %copy-start = (f32[5,8,1024]{2,1,0:T(8,128)}, f32[5,8,1024]{2,1,0:T(8,128)S(1)}, u32[]{:S(2)}) copy-start(f32[5,8,1024]{2,1,0:T(8,128)S(1)} %get-tuple-element.47.psi_ref) | copy-start | bytes 491524
  78.3 22.7 %copy-start.1 = (f32[5,8,1024]{2,1,0:T(8,128)S(1)}, f32[5,8,1024]{2,1,0:T(8,128)}, u32[]{:S(2)}) copy-start(f32[5,8,1024]{2,1,0:T(8,128)} %copy-done) | copy-start | bytes 491524
  99.9 1.2 %copy-start.15 = (f32[5,8,1024]{2,1,0:T(8,128)S(1)}, f32[5,8,1024]{2,1,0:T(8,128)}, u32[]{:S(2)}) copy-start(f32[5,8,1024]{2,1,0:T(8,128)} %get-tuple-element.36) | copy-start | bytes 491524
  99.9 1.2 %copy-start.22 = (f32[5,1,1024]{2,1,0:T(1,128)S(1)}, f32[5,1,1024]{2,1,0:T(1,128)}, u32[]{:S(2)}) copy-start(f32[5,1,1024]{2,1,0:T(1,128)} %get-tuple-element.34) | copy-start | bytes 61444
  99.9 1.2 %copy-start.23 = (f32[5,1,1024]{2,1,0:T(1,128)S(1)}, f32[5,1,1024]{2,1,0:T(1,128)}, u32[]{:S(2)}) copy-start(f32[5,1,1024]{2,1,0:T(1,128)} %get-tuple-element.35) | copy-start | bytes 61444
  (4 other events, 3.3 us)

commit v6 on v5

--- a/solution.py
+++ b/solution.py
@@ -9,6 +9,7 @@
 from jax.experimental.pallas import tpu as pltpu
 
 ITERS = 3
+PIECES = 4
 
 
 GAMMA = 1.4
@@ -178,7 +179,7 @@
     def coef(row, col):
         return table_ref[(row - col) % count]
 
-    halves = 2
+    halves = PIECES
     width = psi_ref.shape[2] // halves
     spans = [pl.ds(h * width, width) for h in range(halves)]
     copies = []
@@ -260,10 +261,10 @@
             pltpu.VMEM((max(outer - 1, 1), *psi.shape), psi.dtype),
             pltpu.VMEM(psi.shape, psi.dtype),
             pltpu.VMEM(psi.shape, psi.dtype),
-            pltpu.SemaphoreType.DMA((2 * (inner - 1),)),
-            pltpu.SemaphoreType.DMA((2 * (inner - 1),)),
-            pltpu.SemaphoreType.DMA((2 * max(outer - 1, 1),)),
-            pltpu.SemaphoreType.DMA((2 * max(outer - 1, 1),)),
+            pltpu.SemaphoreType.DMA((PIECES * (inner - 1),)),
+            pltpu.SemaphoreType.DMA((PIECES * (inner - 1),)),
+            pltpu.SemaphoreType.DMA((PIECES * max(outer - 1, 1),)),
+            pltpu.SemaphoreType.DMA((PIECES * max(outer - 1, 1),)),
             pltpu.SemaphoreType.DMA((2,)),
             pltpu.SemaphoreType.DMA((2,)),
         ] + extra_scratch,

time: 102 us -> 101 us (level)
  Pallas kernels: 71.4 us -> 69.7 us
    pallas_call x3, Pallas kernels: 63.6 us -> 61.9 us  [instance_coupling(): pl.pallas_call(functools.partial(coupling_kernel, count, inner, gather),...]
where the time goes in v6:
time: 101 us; the launch traced here: 100 us
  Pallas kernels  69.7 us (69%)
  other arithmetic  13.5 us (13%)
  matrix products  13.5 us (13%)
  local copies, waits for them, and re-layouts  2.65 us (3%)
    pallas_call x3, Pallas kernels, instance_coupling(): pl.pallas_call(functools.partial(coupling_kernel, count, inner, gather),...  61.9 us
    dot_general x3, matrix products, plane_gather(): jnp.einsum('pra,kba->kprb', parts, onehot, preferred_element_type=jnp.flo...  11.4 us
    pallas_call x1, Pallas kernels, inst_route(): pl.pallas_call(functools.partial(route_kernel, count), out_shape=jax.Shap...  7.78 us
    mul x1, other arithmetic, shards(): along * jnp.cos(lag)  2.56 us
    another operation x6, other arithmetic  2.08 us

profile of v6, /device:TPU:1, one launch (start us, length us, event | category | flops | bytes accessed | tf_op | source)
XLA Modules:
  0.0 100.2 jit_solution(7486449290870542114)
XLA Ops:
  0.0 0.9 reduce-precision_convert_fusion.5
  1.0 4.3 %fusion.14 = f32[4,3,40,1024]{3,2,1,0:T(8,128)S(1)} fusion(s32[4,1024]{1,0:T(4,128)} %param.24, bf16[1,40,1024]{2,1,0:T(8,128)(2,1)S(1)} %get-tuple-element.160, bf16[1,40,1024]{2,1,0:T(8,128)(2,1)S(1)} %get-tuple-element.161, bf16[1,40,1024]{2,1,0:T(8,128)(2,1)S(1)} %get-tuple-element.159), kind=kOutput, calls=%fused_computation.14 | convolution fusion | flops 1011564544 | bytes 2228224 | tf_op jit(solution)/shard_map/pra,kba->kprb/dot_general | solution.py:110
  5.3 0.1 slice_add_fusion.4
  5.5 0.6 compare_select_fusion.table_ref
  6.1 0.6 select_maximum_fusion.refs_0_
  6.7 27.0 %instance_coupling_0.1 = (f32[5,8,1024]{2,1,0:T(8,128)}, f32[5,1,1024]{2,1,0:T(1,128)}, f32[5,1,1024]{2,1,0:T(1,128)}, f32[32,8,128]{2,1,0:T(8,128)}) custom-call(f32[5,8,1024]{2,1,0:T(8,128)} %bitcast.183, f32[8]{0:T(128)} %compare_select_fusion.table_ref, f32[8,128]{1,0:T(8,128)} %select_maximum_fusion.refs_0_), custom_call_target="tpu_custom_call" | custom-call | tf_op jit(solution)/shard_map/instance_coupling_0/pallas_call | solution.py:250
  33.8 0.9 subtract_multiply_fusion.10
  34.9 0.6 slice_multiply_fusion.70
  35.5 0.6 add_add_fusion.2
  36.2 0.7 fusion.53
  36.9 0.6 negate_bitcast_fusion.2
  37.6 0.7 constant_dynamic-slice_fusion
  38.4 0.3 fusion.23
  38.8 0.1 slice_reduce_fusion.2
  39.0 2.6 %cosine_multiply_fusion = (f32[512,256]{1,0:T(8,128)S(1)}, f32[512,256]{1,0:T(8,128)S(1)}) fusion(f32[512,256]{1,0:T(8,128)S(1)} %get-tuple-element.41, f32[512]{0:T(512)S(1)} %broadcast_multiply_fusion, f32[512,256]{1,0:T(8,128)S(1)} %get-tuple-element.40), kind=kLoop, calls=%fused_computation.33 | loop fusion | flops 786432 | bytes 2099200 | tf_op jit(solution)/shard_map/mul | solution.py:389
  41.7 0.1 fusion.73
  42.0 0.5 fusion.25
  42.5 0.6 reshape.481.rows_ref
  43.1 7.8 %inst_route.1 = f32[8,2,128]{2,1,0:T(2,128)} custom-call(f32[8,2,128]{2,1,0:T(2,128)} %reshape.481.rows_ref), custom_call_target="tpu_custom_call" | custom-call | tf_op jit(solution)/shard_map/inst_route/pallas_call | solution.py:331
  50.9 0.7 reduce-precision_convert_fusion.7
  51.7 1.6 %fusion.11 = f32[3,8,1024]{2,1,0:T(8,128)S(1)} fusion(s32[2048]{0:T(1024)S(1)} %get-tuple-element.188, bf16[1,8,2048]{2,1,0:T(8,128)(2,1)S(1)} %get-tuple-element.186, bf16[1,8,2048]{2,1,0:T(8,128)(2,1)S(1)} %get-tuple-element.185, bf16[1,8,2048]{2,1,0:T(8,128)(2,1)S(1)} %get-tuple-element.184), kind=kOutput, calls=%fused_computation.10 | convolution fusion | flops 102858752 | bytes 204800 | tf_op jit(solution)/shard_map/plq,qb->plb/dot_general | solution.py:123
  53.4 0.2 reduce-precision_convert_fusion.3
  53.6 3.6 %fusion.17 = f32[4,3,40,1024]{3,2,1,0:T(8,128)S(1)} fusion(s32[4,1024]{1,0:T(4,128)S(1)} %copy-done.34, bf16[1,40,1024]{2,1,0:T(8,128)(2,1)S(1)} %get-tuple-element.146, bf16[1,40,1024]{2,1,0:T(8,128)(2,1)S(1)} %get-tuple-element.145, bf16[1,40,1024]{2,1,0:T(8,128)(2,1)S(1)} %get-tuple-element.52), kind=kOutput, calls=%fused_computation.15 | convolution fusion | flops 1011564544 | bytes 2228224 | tf_op jit(solution)/shard_map/pra,kba->kprb/dot_general | solution.py:110
  57.2 0.1 slice_add_fusion.2
  57.4 0.6 copy-done.10
  58.0 14.7 %instance_coupling_1.1 = (f32[5,8,1024]{2,1,0:T(8,128)}, f32[5,1,1024]{2,1,0:T(1,128)}, f32[5,1,1024]{2,1,0:T(1,128)}) custom-call(f32[5,8,1024]{2,1,0:T(8,128)} %copy-done.2, f32[8]{0:T(128)} %compare_select_fusion.table_ref), custom_call_target="tpu_custom_call" | custom-call | tf_op jit(solution)/shard_map/instance_coupling_1/pallas_call | solution.py:250
  72.8 0.9 subtract_multiply_fusion.5
  73.9 0.2 reduce-precision_convert_fusion.1
  74.2 3.6 %fusion.20 = f32[4,3,40,1024]{3,2,1,0:T(8,128)S(1)} fusion(s32[4,1024]{1,0:T(4,128)S(1)} %copy-done.34, bf16[1,40,1024]{2,1,0:T(8,128)(2,1)S(1)} %get-tuple-element.131, bf16[1,40,1024]{2,1,0:T(8,128)(2,1)S(1)} %get-tuple-element.130, bf16[1,40,1024]{2,1,0:T(8,128)(2,1)S(1)} %get-tuple-element.46), kind=kOutput, calls=%fused_computation.16 | convolution fusion | flops 1011564544 | bytes 2228224 | tf_op jit(solution)/shard_map/pra,kba->kprb/dot_general | solution.py:110
  78.0 20.2 %instance_coupling_2.1 = (f32[5,8,1024]{2,1,0:T(8,128)}, f32[5,1,1024]{2,1,0:T(1,128)}, f32[5,1,1024]{2,1,0:T(1,128)}) custom-call(f32[5,8,1024]{2,1,0:T(8,128)} %copy-done, f32[8]{0:T(128)} %compare_select_fusion.table_ref), custom_call_target="tpu_custom_call" | custom-call | tf_op jit(solution)/shard_map/instance_coupling_2/pallas_call | solution.py:250
  98.2 0.9 subtract_multiply_fusion.2
  99.3 0.8 subtract_bitcast_fusion
  (110 shorter events, 1.5 us)
Async XLA Ops:
  5.3 28.5 %copy-start.4 = (f32[5,1,8,1024]{3,2,1,0:T(8,128)S(1)}, f32[5,1,8,1024]{3,2,1,0:T(8,128)}, u32[]{:S(2)}) copy-start(f32[5,1,8,1024]{3,2,1,0:T(8,128)} %param.14) | copy-start | bytes 491524
  5.3 29.5 %copy-start.7 = (f32[1,8,1024]{2,1,0:T(8,128)S(1)}, f32[1,8,1024]{2,1,0:T(8,128)}, u32[]{:S(2)}) copy-start(f32[1,8,1024]{2,1,0:T(8,128)} %param.15) | copy-start | bytes 98308
  5.3 29.5 %copy-start.21 = (f32[3,1,8,1024]{3,2,1,0:T(8,128)S(1)}, f32[3,1,8,1024]{3,2,1,0:T(8,128)}, u32[]{:S(2)}) copy-start(f32[3,1,8,1024]{3,2,1,0:T(8,128)} %param.16) | copy-start | bytes 294916
  5.4 29.4 %copy-start.28 = (f32[1,8,1024]{2,1,0:T(8,128)S(1)}, f32[1,8,1024]{2,1,0:T(8,128)}, u32[]{:S(2)}) copy-start(f32[1,8,1024]{2,1,0:T(8,128)} %param.17) | copy-start | bytes 98308
  33.8 0.9 copy-start.5
  33.8 2.4 %copy-start.30 = (pred[3]{0:T(512)(128)(4,1)S(1)}, pred[3]{0:T(512)(128)(4,1)}, u32[]{:S(2)}) copy-start(pred[3]{0:T(512)(128)(4,1)} %constant.102.clone.1) | copy-start | bytes 13
  34.8 3.4 %copy-start.20 = (f32[32,8,128]{2,1,0:T(8,128)S(1)}, f32[32,8,128]{2,1,0:T(8,128)}, u32[]{:S(2)}) copy-start(f32[32,8,128]{2,1,0:T(8,128)} %get-tuple-element.30) | copy-start | bytes 393220
  35.5 3.2 %copy-start.9 = (f32[1,8,1024]{2,1,0:T(8,128)}, f32[1,8,1024]{2,1,0:T(8,128)S(1)}, u32[]{:S(2)}) copy-start(f32[1,8,1024]{2,1,0:T(8,128)S(1)} %get-tuple-element.148) | copy-start | bytes 98308
  35.5 3.3 %copy-start.12 = (f32[8,1024]{1,0:T(8,128)}, f32[8,1024]{1,0:T(8,128)S(1)}, u32[]{:S(2)}) copy-start(f32[8,1024]{1,0:T(8,128)S(1)} %get-tuple-element.182) | copy-start | bytes 98308
  37.6 4.2 %copy-start.33 = (f32[8]{0:T(128)S(1)}, f32[8]{0:T(128)}, u32[]{:S(2)}) copy-start(f32[8]{0:T(128)} %constant.121.clone) | copy-start | bytes 100
  38.8 12.1 %copy-start.29 = (s32[2048]{0:T(1024)S(1)}, s32[2048]{0:T(1024)}, u32[]{:S(2)}) copy-start(s32[2048]{0:T(1024)} %param.23) | copy-start | bytes 24580
  41.9 11.4 %copy-start.6 = (f32[5,7,1024]{2,1,0:T(8,128)S(1)}, f32[5,7,1024]{2,1,0:T(8,128)}, u32[]{:S(2)}) copy-start(f32[5,7,1024]{2,1,0:T(8,128)} %copy-done.5) | copy-start | bytes 430084
  41.9 11.4 %copy-start.11 = (f32[1,8,1024]{2,1,0:T(8,128)S(1)}, f32[1,8,1024]{2,1,0:T(8,128)}, u32[]{:S(2)}) copy-start(f32[1,8,1024]{2,1,0:T(8,128)} %get-tuple-element.183) | copy-start | bytes 98308
  41.9 11.4 %copy-start.14 = (f32[3,8,1024]{2,1,0:T(8,128)S(1)}, f32[3,8,1024]{2,1,0:T(8,128)}, u32[]{:S(2)}) copy-start(f32[3,8,1024]{2,1,0:T(8,128)} %get-tuple-element.56) | copy-start | bytes 294916
  41.9 11.4 %copy-start.16 = (f32[5,8,1024]{2,1,0:T(8,128)S(1)}, f32[5,8,1024]{2,1,0:T(8,128)}, u32[]{:S(2)}) copy-start(f32[5,8,1024]{2,1,0:T(8,128)} %get-tuple-element.29) | copy-start | bytes 491524
  41.9 11.4 %copy-start.18 = (f32[1,8,1024]{2,1,0:T(8,128)S(1)}, f32[1,8,1024]{2,1,0:T(8,128)}, u32[]{:S(2)}) copy-start(f32[1,8,1024]{2,1,0:T(8,128)} %get-tuple-element.54) | copy-start | bytes 98308
  41.9 11.4 %copy-start.19 = (f32[1,8,1024]{2,1,0:T(8,128)S(1)}, f32[1,8,1024]{2,1,0:T(8,128)}, u32[]{:S(2)}) copy-start(f32[1,8,1024]{2,1,0:T(8,128)} %negate_bitcast_fusion.2) | copy-start | bytes 98308
  42.0 11.4 %copy-start.26 = (f32[5,1,1024]{2,1,0:T(1,128)S(1)}, f32[5,1,1024]{2,1,0:T(1,128)}, u32[]{:S(2)}) copy-start(f32[5,1,1024]{2,1,0:T(1,128)} %get-tuple-element.27) | copy-start | bytes 61444
  42.0 11.4 %copy-start.27 = (f32[5,1,1024]{2,1,0:T(1,128)S(1)}, f32[5,1,1024]{2,1,0:T(1,128)}, u32[]{:S(2)}) copy-start(f32[5,1,1024]{2,1,0:T(1,128)} %get-tuple-element.28) | copy-start | bytes 61444
  51.7 1.9 %copy-start.34 = (s32[4,1024]{1,0:T(4,128)S(1)}, s32[4,1024]{1,0:T(4,128)}, u32[]{:S(2)}) copy-start(s32[4,1024]{1,0:T(4,128)} %param.24) | copy-start | bytes 49156
  53.5 4.4 %copy-start.2 = (f32[5,8,1024]{2,1,0:T(8,128)}, f32[5,8,1024]{2,1,0:T(8,128)S(1)}, u32[]{:S(2)}) copy-start(f32[5,8,1024]{2,1,0:T(8,128)S(1)} %get-tuple-element.53.psi_ref) | copy-start | bytes 491524
  57.4 16.4 %copy-start.8 = (f32[1,8,1024]{2,1,0:T(8,128)S(1)}, f32[1,8,1024]{2,1,0:T(8,128)}, u32[]{:S(2)}) copy-start(f32[1,8,1024]{2,1,0:T(8,128)} %param.15) | copy-start | bytes 98308
  58.0 15.9 %copy-start.13 = (f32[8,1024]{1,0:T(8,128)S(1)}, f32[8,1024]{1,0:T(8,128)}, u32[]{:S(2)}) copy-start(f32[8,1024]{1,0:T(8,128)} %copy-done.12) | copy-start | bytes 98308
  58.0 15.9 %copy-start.3 = (f32[5,8,1024]{2,1,0:T(8,128)S(1)}, f32[5,8,1024]{2,1,0:T(8,128)}, u32[]{:S(2)}) copy-start(f32[5,8,1024]{2,1,0:T(8,128)} %copy-done.2) | copy-start | bytes 491524
  72.7 1.2 %copy-start.17 = (f32[5,8,1024]{2,1,0:T(8,128)S(1)}, f32[5,8,1024]{2,1,0:T(8,128)}, u32[]{:S(2)}) copy-start(f32[5,8,1024]{2,1,0:T(8,128)} %get-tuple-element.33) | copy-start | bytes 491524
  72.7 1.2 %copy-start.24 = (f32[5,1,1024]{2,1,0:T(1,128)S(1)}, f32[5,1,1024]{2,1,0:T(1,128)}, u32[]{:S(2)}) copy-start(f32[5,1,1024]{2,1,0:T(1,128)} %get-tuple-element.31) | copy-start | bytes 61444
  72.7 1.2 %copy-start.25 = (f32[5,1,1024]{2,1,0:T(1,128)S(1)}, f32[5,1,1024]{2,1,0:T(1,128)}, u32[]{:S(2)}) copy-start(f32[5,1,1024]{2,1,0:T(1,128)} %get-tuple-element.32) | copy-start | bytes 61444
  74.1 3.8 %copy-start = (f32[5,8,1024]{2,1,0:T(8,128)}, f32[5,8,1024]{2,1,0:T(8,128)S(1)}, u32[]{:S(2)}) copy-start(f32[5,8,1024]{2,1,0:T(8,128)S(1)} %get-tuple-element.47.psi_ref) | copy-start | bytes 491524
  78.0 21.3 %copy-start.1 = (f32[5,8,1024]{2,1,0:T(8,128)S(1)}, f32[5,8,1024]{2,1,0:T(8,128)}, u32[]{:S(2)}) copy-start(f32[5,8,1024]{2,1,0:T(8,128)} %copy-done) | copy-start | bytes 491524
  98.2 1.2 %copy-start.15 = (f32[5,8,1024]{2,1,0:T(8,128)S(1)}, f32[5,8,1024]{2,1,0:T(8,128)}, u32[]{:S(2)}) copy-start(f32[5,8,1024]{2,1,0:T(8,128)} %get-tuple-element.36) | copy-start | bytes 491524
  98.2 1.2 %copy-start.22 = (f32[5,1,1024]{2,1,0:T(1,128)S(1)}, f32[5,1,1024]{2,1,0:T(1,128)}, u32[]{:S(2)}) copy-start(f32[5,1,1024]{2,1,0:T(1,128)} %get-tuple-element.34) | copy-start | bytes 61444
  98.2 1.2 %copy-start.23 = (f32[5,1,1024]{2,1,0:T(1,128)S(1)}, f32[5,1,1024]{2,1,0:T(1,128)}, u32[]{:S(2)}) copy-start(f32[5,1,1024]{2,1,0:T(1,128)} %get-tuple-element.35) | copy-start | bytes 61444
  (4 other events, 3.3 us)

commit v7 on v6

--- a/solution.py
+++ b/solution.py
@@ -9,7 +9,7 @@
 from jax.experimental.pallas import tpu as pltpu
 
 ITERS = 3
-PIECES = 4
+PIECES = 8
 
 
 GAMMA = 1.4

time: 101 us -> 101 us (level)
  no operation moved by 1% of the time
where the time goes in v7:
time: 101 us
  Pallas kernels  70.3 us (70%)
  other arithmetic  13.5 us (13%)
  matrix products  13.5 us (13%)
  local copies, waits for them, and re-layouts  2.65 us (3%)
    pallas_call x3, Pallas kernels, instance_coupling(): pl.pallas_call(functools.partial(coupling_kernel, count, inner, gather),...  62.5 us
    dot_general x3, matrix products, plane_gather(): jnp.einsum('pra,kba->kprb', parts, onehot, preferred_element_type=jnp.flo...  11.4 us
    pallas_call x1, Pallas kernels, inst_route(): pl.pallas_call(functools.partial(route_kernel, count), out_shape=jax.Shap...  7.78 us
    mul x1, other arithmetic, shards(): along * jnp.cos(lag)  2.56 us
    another operation x6, other arithmetic  2.08 us

profile of v7, /device:TPU:1, one launch (start us, length us, event | category | flops | bytes accessed | tf_op | source)
XLA Modules:
  0.0 100.8 jit_solution(16073257462342720803)
XLA Ops:
  0.0 0.9 reduce-precision_convert_fusion.5
  1.0 4.3 %fusion.14 = f32[4,3,40,1024]{3,2,1,0:T(8,128)S(1)} fusion(s32[4,1024]{1,0:T(4,128)} %param.24, bf16[1,40,1024]{2,1,0:T(8,128)(2,1)S(1)} %get-tuple-element.160, bf16[1,40,1024]{2,1,0:T(8,128)(2,1)S(1)} %get-tuple-element.161, bf16[1,40,1024]{2,1,0:T(8,128)(2,1)S(1)} %get-tuple-element.159), kind=kOutput, calls=%fused_computation.14 | convolution fusion | flops 1011564544 | bytes 2228224 | tf_op jit(solution)/shard_map/pra,kba->kprb/dot_general | solution.py:110
  5.3 0.1 slice_add_fusion.4
  5.5 0.6 compare_select_fusion.table_ref
  6.1 0.6 select_maximum_fusion.refs_0_
  6.7 27.3 %instance_coupling_0.1 = (f32[5,8,1024]{2,1,0:T(8,128)}, f32[5,1,1024]{2,1,0:T(1,128)}, f32[5,1,1024]{2,1,0:T(1,128)}, f32[32,8,128]{2,1,0:T(8,128)}) custom-call(f32[5,8,1024]{2,1,0:T(8,128)} %bitcast.183, f32[8]{0:T(128)} %compare_select_fusion.table_ref, f32[8,128]{1,0:T(8,128)} %select_maximum_fusion.refs_0_), custom_call_target="tpu_custom_call" | custom-call | tf_op jit(solution)/shard_map/instance_coupling_0/pallas_call | solution.py:250
  34.1 0.9 subtract_multiply_fusion.10
  35.1 0.6 slice_multiply_fusion.70
  35.8 0.6 add_add_fusion.2
  36.5 0.7 fusion.53
  37.2 0.6 negate_bitcast_fusion.2
  37.8 0.7 constant_dynamic-slice_fusion
  38.7 0.3 fusion.23
  39.0 0.1 slice_reduce_fusion.2
  39.3 2.6 %cosine_multiply_fusion = (f32[512,256]{1,0:T(8,128)S(1)}, f32[512,256]{1,0:T(8,128)S(1)}) fusion(f32[512,256]{1,0:T(8,128)S(1)} %get-tuple-element.41, f32[512]{0:T(512)S(1)} %broadcast_multiply_fusion, f32[512,256]{1,0:T(8,128)S(1)} %get-tuple-element.40), kind=kLoop, calls=%fused_computation.33 | loop fusion | flops 786432 | bytes 2099200 | tf_op jit(solution)/shard_map/mul | solution.py:389
  42.0 0.1 fusion.73
  42.2 0.5 fusion.25
  42.8 0.6 reshape.481.rows_ref
  43.4 7.8 %inst_route.1 = f32[8,2,128]{2,1,0:T(2,128)} custom-call(f32[8,2,128]{2,1,0:T(2,128)} %reshape.481.rows_ref), custom_call_target="tpu_custom_call" | custom-call | tf_op jit(solution)/shard_map/inst_route/pallas_call | solution.py:331
  51.2 0.7 reduce-precision_convert_fusion.7
  51.9 1.6 %fusion.11 = f32[3,8,1024]{2,1,0:T(8,128)S(1)} fusion(s32[2048]{0:T(1024)S(1)} %get-tuple-element.188, bf16[1,8,2048]{2,1,0:T(8,128)(2,1)S(1)} %get-tuple-element.186, bf16[1,8,2048]{2,1,0:T(8,128)(2,1)S(1)} %get-tuple-element.185, bf16[1,8,2048]{2,1,0:T(8,128)(2,1)S(1)} %get-tuple-element.184), kind=kOutput, calls=%fused_computation.10 | convolution fusion | flops 102858752 | bytes 204800 | tf_op jit(solution)/shard_map/plq,qb->plb/dot_general | solution.py:123
  53.6 0.2 reduce-precision_convert_fusion.3
  53.9 3.5 %fusion.17 = f32[4,3,40,1024]{3,2,1,0:T(8,128)S(1)} fusion(s32[4,1024]{1,0:T(4,128)S(1)} %copy-done.34, bf16[1,40,1024]{2,1,0:T(8,128)(2,1)S(1)} %get-tuple-element.146, bf16[1,40,1024]{2,1,0:T(8,128)(2,1)S(1)} %get-tuple-element.145, bf16[1,40,1024]{2,1,0:T(8,128)(2,1)S(1)} %get-tuple-element.52), kind=kOutput, calls=%fused_computation.15 | convolution fusion | flops 1011564544 | bytes 2228224 | tf_op jit(solution)/shard_map/pra,kba->kprb/dot_general | solution.py:110
  57.6 0.6 copy-done.10
  58.3 14.5 %instance_coupling_1.1 = (f32[5,8,1024]{2,1,0:T(8,128)}, f32[5,1,1024]{2,1,0:T(1,128)}, f32[5,1,1024]{2,1,0:T(1,128)}) custom-call(f32[5,8,1024]{2,1,0:T(8,128)} %copy-done.2, f32[8]{0:T(128)} %compare_select_fusion.table_ref), custom_call_target="tpu_custom_call" | custom-call | tf_op jit(solution)/shard_map/instance_coupling_1/pallas_call | solution.py:250
  72.8 0.9 subtract_multiply_fusion.5
  74.0 0.2 reduce-precision_convert_fusion.1
  74.2 3.6 %fusion.20 = f32[4,3,40,1024]{3,2,1,0:T(8,128)S(1)} fusion(s32[4,1024]{1,0:T(4,128)S(1)} %copy-done.34, bf16[1,40,1024]{2,1,0:T(8,128)(2,1)S(1)} %get-tuple-element.131, bf16[1,40,1024]{2,1,0:T(8,128)(2,1)S(1)} %get-tuple-element.130, bf16[1,40,1024]{2,1,0:T(8,128)(2,1)S(1)} %get-tuple-element.46), kind=kOutput, calls=%fused_computation.16 | convolution fusion | flops 1011564544 | bytes 2228224 | tf_op jit(solution)/shard_map/pra,kba->kprb/dot_general | solution.py:110
  77.8 0.1 slice_add_fusion
  78.0 20.7 %instance_coupling_2.1 = (f32[5,8,1024]{2,1,0:T(8,128)}, f32[5,1,1024]{2,1,0:T(1,128)}, f32[5,1,1024]{2,1,0:T(1,128)}) custom-call(f32[5,8,1024]{2,1,0:T(8,128)} %copy-done, f32[8]{0:T(128)} %compare_select_fusion.table_ref), custom_call_target="tpu_custom_call" | custom-call | tf_op jit(solution)/shard_map/instance_coupling_2/pallas_call | solution.py:250
  98.8 0.9 subtract_multiply_fusion.2
  99.9 0.8 subtract_bitcast_fusion
  (110 shorter events, 1.5 us)
Async XLA Ops:
  5.3 28.8 %copy-start.4 = (f32[5,1,8,1024]{3,2,1,0:T(8,128)S(1)}, f32[5,1,8,1024]{3,2,1,0:T(8,128)}, u32[]{:S(2)}) copy-start(f32[5,1,8,1024]{3,2,1,0:T(8,128)} %param.14) | copy-start | bytes 491524
  5.3 29.7 %copy-start.7 = (f32[1,8,1024]{2,1,0:T(8,128)S(1)}, f32[1,8,1024]{2,1,0:T(8,128)}, u32[]{:S(2)}) copy-start(f32[1,8,1024]{2,1,0:T(8,128)} %param.15) | copy-start | bytes 98308
  5.3 29.7 %copy-start.21 = (f32[3,1,8,1024]{3,2,1,0:T(8,128)S(1)}, f32[3,1,8,1024]{3,2,1,0:T(8,128)}, u32[]{:S(2)}) copy-start(f32[3,1,8,1024]{3,2,1,0:T(8,128)} %param.16) | copy-start | bytes 294916
  5.4 29.7 %copy-start.28 = (f32[1,8,1024]{2,1,0:T(8,128)S(1)}, f32[1,8,1024]{2,1,0:T(8,128)}, u32[]{:S(2)}) copy-start(f32[1,8,1024]{2,1,0:T(8,128)} %param.17) | copy-start | bytes 98308
  34.1 0.9 copy-start.5
  34.1 2.4 %copy-start.30 = (pred[3]{0:T(512)(128)(4,1)S(1)}, pred[3]{0:T(512)(128)(4,1)}, u32[]{:S(2)}) copy-start(pred[3]{0:T(512)(128)(4,1)} %constant.102.clone.1) | copy-start | bytes 13
  35.1 3.4 %copy-start.20 = (f32[32,8,128]{2,1,0:T(8,128)S(1)}, f32[32,8,128]{2,1,0:T(8,128)}, u32[]{:S(2)}) copy-start(f32[32,8,128]{2,1,0:T(8,128)} %get-tuple-element.30) | copy-start | bytes 393220
  35.8 3.2 %copy-start.9 = (f32[1,8,1024]{2,1,0:T(8,128)}, f32[1,8,1024]{2,1,0:T(8,128)S(1)}, u32[]{:S(2)}) copy-start(f32[1,8,1024]{2,1,0:T(8,128)S(1)} %get-tuple-element.148) | copy-start | bytes 98308
  35.8 3.3 %copy-start.12 = (f32[8,1024]{1,0:T(8,128)}, f32[8,1024]{1,0:T(8,128)S(1)}, u32[]{:S(2)}) copy-start(f32[8,1024]{1,0:T(8,128)S(1)} %get-tuple-element.182) | copy-start | bytes 98308
  37.8 4.2 %copy-start.33 = (f32[8]{0:T(128)S(1)}, f32[8]{0:T(128)}, u32[]{:S(2)}) copy-start(f32[8]{0:T(128)} %constant.121.clone) | copy-start | bytes 100
  39.0 12.1 %copy-start.29 = (s32[2048]{0:T(1024)S(1)}, s32[2048]{0:T(1024)}, u32[]{:S(2)}) copy-start(s32[2048]{0:T(1024)} %param.23) | copy-start | bytes 24580
  42.2 11.4 %copy-start.6 = (f32[5,7,1024]{2,1,0:T(8,128)S(1)}, f32[5,7,1024]{2,1,0:T(8,128)}, u32[]{:S(2)}) copy-start(f32[5,7,1024]{2,1,0:T(8,128)} %copy-done.5) | copy-start | bytes 430084
  42.2 11.4 %copy-start.11 = (f32[1,8,1024]{2,1,0:T(8,128)S(1)}, f32[1,8,1024]{2,1,0:T(8,128)}, u32[]{:S(2)}) copy-start(f32[1,8,1024]{2,1,0:T(8,128)} %get-tuple-element.183) | copy-start | bytes 98308
  42.2 11.4 %copy-start.14 = (f32[3,8,1024]{2,1,0:T(8,128)S(1)}, f32[3,8,1024]{2,1,0:T(8,128)}, u32[]{:S(2)}) copy-start(f32[3,8,1024]{2,1,0:T(8,128)} %get-tuple-element.56) | copy-start | bytes 294916
  42.2 11.4 %copy-start.16 = (f32[5,8,1024]{2,1,0:T(8,128)S(1)}, f32[5,8,1024]{2,1,0:T(8,128)}, u32[]{:S(2)}) copy-start(f32[5,8,1024]{2,1,0:T(8,128)} %get-tuple-element.29) | copy-start | bytes 491524
  42.2 11.4 %copy-start.18 = (f32[1,8,1024]{2,1,0:T(8,128)S(1)}, f32[1,8,1024]{2,1,0:T(8,128)}, u32[]{:S(2)}) copy-start(f32[1,8,1024]{2,1,0:T(8,128)} %get-tuple-element.54) | copy-start | bytes 98308
  42.2 11.4 %copy-start.19 = (f32[1,8,1024]{2,1,0:T(8,128)S(1)}, f32[1,8,1024]{2,1,0:T(8,128)}, u32[]{:S(2)}) copy-start(f32[1,8,1024]{2,1,0:T(8,128)} %negate_bitcast_fusion.2) | copy-start | bytes 98308
  42.2 11.4 %copy-start.26 = (f32[5,1,1024]{2,1,0:T(1,128)S(1)}, f32[5,1,1024]{2,1,0:T(1,128)}, u32[]{:S(2)}) copy-start(f32[5,1,1024]{2,1,0:T(1,128)} %get-tuple-element.27) | copy-start | bytes 61444
  42.2 11.4 %copy-start.27 = (f32[5,1,1024]{2,1,0:T(1,128)S(1)}, f32[5,1,1024]{2,1,0:T(1,128)}, u32[]{:S(2)}) copy-start(f32[5,1,1024]{2,1,0:T(1,128)} %get-tuple-element.28) | copy-start | bytes 61444
  51.9 1.9 %copy-start.34 = (s32[4,1024]{1,0:T(4,128)S(1)}, s32[4,1024]{1,0:T(4,128)}, u32[]{:S(2)}) copy-start(s32[4,1024]{1,0:T(4,128)} %param.24) | copy-start | bytes 49156
  53.8 4.4 %copy-start.2 = (f32[5,8,1024]{2,1,0:T(8,128)}, f32[5,8,1024]{2,1,0:T(8,128)S(1)}, u32[]{:S(2)}) copy-start(f32[5,8,1024]{2,1,0:T(8,128)S(1)} %get-tuple-element.53.psi_ref) | copy-start | bytes 491524
  57.6 16.1 %copy-start.8 = (f32[1,8,1024]{2,1,0:T(8,128)S(1)}, f32[1,8,1024]{2,1,0:T(8,128)}, u32[]{:S(2)}) copy-start(f32[1,8,1024]{2,1,0:T(8,128)} %param.15) | copy-start | bytes 98308
  58.2 15.7 %copy-start.13 = (f32[8,1024]{1,0:T(8,128)S(1)}, f32[8,1024]{1,0:T(8,128)}, u32[]{:S(2)}) copy-start(f32[8,1024]{1,0:T(8,128)} %copy-done.12) | copy-start | bytes 98308
  58.3 15.7 %copy-start.3 = (f32[5,8,1024]{2,1,0:T(8,128)S(1)}, f32[5,8,1024]{2,1,0:T(8,128)}, u32[]{:S(2)}) copy-start(f32[5,8,1024]{2,1,0:T(8,128)} %copy-done.2) | copy-start | bytes 491524
  72.8 1.2 %copy-start.17 = (f32[5,8,1024]{2,1,0:T(8,128)S(1)}, f32[5,8,1024]{2,1,0:T(8,128)}, u32[]{:S(2)}) copy-start(f32[5,8,1024]{2,1,0:T(8,128)} %get-tuple-element.33) | copy-start | bytes 491524
  72.8 1.2 %copy-start.24 = (f32[5,1,1024]{2,1,0:T(1,128)S(1)}, f32[5,1,1024]{2,1,0:T(1,128)}, u32[]{:S(2)}) copy-start(f32[5,1,1024]{2,1,0:T(1,128)} %get-tuple-element.31) | copy-start | bytes 61444
  72.8 1.2 %copy-start.25 = (f32[5,1,1024]{2,1,0:T(1,128)S(1)}, f32[5,1,1024]{2,1,0:T(1,128)}, u32[]{:S(2)}) copy-start(f32[5,1,1024]{2,1,0:T(1,128)} %get-tuple-element.32) | copy-start | bytes 61444
  74.1 3.8 %copy-start = (f32[5,8,1024]{2,1,0:T(8,128)}, f32[5,8,1024]{2,1,0:T(8,128)S(1)}, u32[]{:S(2)}) copy-start(f32[5,8,1024]{2,1,0:T(8,128)S(1)} %get-tuple-element.47.psi_ref) | copy-start | bytes 491524
  78.0 21.9 %copy-start.1 = (f32[5,8,1024]{2,1,0:T(8,128)S(1)}, f32[5,8,1024]{2,1,0:T(8,128)}, u32[]{:S(2)}) copy-start(f32[5,8,1024]{2,1,0:T(8,128)} %copy-done) | copy-start | bytes 491524
  98.8 1.2 %copy-start.15 = (f32[5,8,1024]{2,1,0:T(8,128)S(1)}, f32[5,8,1024]{2,1,0:T(8,128)}, u32[]{:S(2)}) copy-start(f32[5,8,1024]{2,1,0:T(8,128)} %get-tuple-element.36) | copy-start | bytes 491524
  98.8 1.2 %copy-start.22 = (f32[5,1,1024]{2,1,0:T(1,128)S(1)}, f32[5,1,1024]{2,1,0:T(1,128)}, u32[]{:S(2)}) copy-start(f32[5,1,1024]{2,1,0:T(1,128)} %get-tuple-element.34) | copy-start | bytes 61444
  98.8 1.2 %copy-start.23 = (f32[5,1,1024]{2,1,0:T(1,128)S(1)}, f32[5,1,1024]{2,1,0:T(1,128)}, u32[]{:S(2)}) copy-start(f32[5,1,1024]{2,1,0:T(1,128)} %get-tuple-element.35) | copy-start | bytes 61444
  (4 other events, 3.3 us)

commit v8 on v6

--- a/solution.py
+++ b/solution.py
@@ -407,9 +407,12 @@
     ) * (GAMMA - 1.0)
     source = slope * wall[None]
     _, pull = jax.vjp(fluxes, state)
-    onehot = (plane_nbr[:, :, None] == jnp.arange(plane, dtype=jnp.int32)[None, None, :]).astype(
-        jnp.bfloat16
-    )
+    hits = (plane_nbr[:, :, None] == jnp.arange(plane, dtype=jnp.int32)[None, None, :]).astype(
+        jnp.float32
+    )
+    onehot = jnp.stack(
+        [hits[0] + hits[1] + hits[2] + hits[3], hits[1] - hits[0], hits[3] - hits[2]]
+    ).astype(jnp.bfloat16)
     for step in range(ITERS):
         if step == 0:
             spectral_operator, below, above = first[:3]
@@ -417,11 +420,9 @@
             spectral_operator, below, above = instance_coupling(psi, row_entry, step)
         minus_a = jnp.concatenate([below, psi[:, :-1]], axis=1)
         plus_a = jnp.concatenate([psi[:, 1:], above], axis=1)
-        plus_y, minus_y, plus_z, minus_z = plane_gather(psi, onehot)
-        middle_point = pull(
-            (0.5 * (minus_a - plus_a), 0.5 * (minus_y - plus_y), 0.5 * (minus_z - plus_z))
-        )[0]
-        spread = 6.0 * psi - (minus_a + plus_a + plus_y + minus_y + plus_z + minus_z)
+        around, across_y, across_z = plane_gather(psi, onehot)
+        middle_point = pull((0.5 * (minus_a - plus_a), 0.5 * across_y, 0.5 * across_z))[0]
+        spread = 6.0 * psi - (minus_a + plus_a + around)
         psi = psi - TAU * (middle_point + DISSIP * spread + spectral_operator + source)
     return psi[:, None]
 

time: 101 us -> 109 us (1.079)
  other arithmetic: 13.5 us -> 24.8 us
  matrix products: 13.5 us -> 10.9 us
    another operation x6 -> x7, other arithmetic: 2.08 us -> 5.82 us
    dot_general x3, matrix products: 11.4 us -> 8.8 us  [plane_gather(): jnp.einsum('pra,kba->kprb', parts, onehot, preferred_element_type=jnp.flo...]
    convert_element_type x0 -> x1, other arithmetic: none -> 2.44 us  [shards(): (plane_nbr[:, :, None] == jnp.arange(plane, dtype=jnp.int32)[None, None,...]
    mul x2 -> x3, other arithmetic: 1.73 us -> 2.64 us  [shards(): 0.5 * (minus_a - plus_a)]
where the time goes in v8:
time: 109 us; the launch traced here: 108 us
  Pallas kernels  69.6 us (64%)
  other arithmetic  24.8 us (23%)
  matrix products  10.9 us (10%)
  local copies, waits for them, and re-layouts  2.25 us (2%)
    pallas_call x3, Pallas kernels, instance_coupling(): pl.pallas_call(functools.partial(coupling_kernel, count, inner, gather),...  61.9 us
    dot_general x3, matrix products, plane_gather(): jnp.einsum('pra,kba->kprb', parts, onehot, preferred_element_type=jnp.flo...  8.8 us
    pallas_call x1, Pallas kernels, inst_route(): pl.pallas_call(functools.partial(route_kernel, count), out_shape=jax.Shap...  7.78 us
    another operation x7, other arithmetic  5.82 us
    mul x3, other arithmetic, shards(): 0.5 * (minus_a - plus_a)  2.64 us
    convert_element_type x1, other arithmetic, shards(): (plane_nbr[:, :, None] == jnp.arange(plane, dtype=jnp.int32)[None, None,...  2.44 us
    mul x1, other arithmetic, shards(): along * jnp.cos(lag)  2.39 us

profile of v8, /device:TPU:1, one launch (start us, length us, event | category | flops | bytes accessed | tf_op | source)
XLA Modules:
  0.0 108.2 jit_solution(14207991778044758485)
XLA Ops:
  0.0 0.9 broadcast_divide_fusion
  0.9 0.8 multiply_reduce_fusion.3
  1.7 2.4 %fusion = f32[4,1024,1024]{2,1,0:T(8,128)S(1)} fusion(s32[4,1024]{1,0:T(4,128)} %param.24), kind=kLoop, calls=%fused_computation.1 | loop fusion | flops 8388608 | bytes 16793600 | tf_op jit(solution)/shard_map/convert_element_type | solution.py:410
  4.2 2.8 %add_convert_fusion = (bf16[1,1024,1024]{2,1,0:T(8,128)(2,1)S(1)}, bf16[1,1024,1024]{2,1,0:T(8,128)(2,1)S(1)}, bf16[1,1024,1024]{2,1,0:T(8,128)(2,1)S(1)}) fusion(f32[4,1024,1024]{2,1,0:T(8,128)S(1)} %fusion), kind=kLoop, calls=%fused_computation.9 | loop fusion | flops 8388608 | bytes 23068672 | tf_op jit(solution)/shard_map/convert.12
  7.1 2.2 %convolution_bitcast_fusion.2 = f32[3,3,40,1024]{3,2,1,0:T(8,128)S(1)} fusion(bf16[1,1024,1024]{2,1,0:T(8,128)(2,1)S(1)} %get-tuple-element.63, bf16[1,1024,1024]{2,1,0:T(8,128)(2,1)S(1)} %get-tuple-element.64, bf16[1,1024,1024]{2,1,0:T(8,128)(2,1)S(1)} %get-tuple-element.62, bf16[1,40,1024]{2,1,0:T(8,128)(2,1)S(1)} %get-tuple-element.163, ...), kind=kOutput, calls=%fused_computation.16 | convolution fusion | flops 774586368 | bytes 8011776 | tf_op jit(solution)/shard_map/pra,kba->kprb/dot_general | solution.py:110
  9.8 0.6 compare_select_fusion.table_ref
  10.4 0.6 select_maximum_fusion.refs_0_
  11.0 27.0 %instance_coupling_0.1 = (f32[5,8,1024]{2,1,0:T(8,128)}, f32[5,1,1024]{2,1,0:T(1,128)}, f32[5,1,1024]{2,1,0:T(1,128)}, f32[32,8,128]{2,1,0:T(8,128)}) custom-call(f32[5,8,1024]{2,1,0:T(8,128)} %bitcast.167, f32[8]{0:T(128)} %compare_select_fusion.table_ref, f32[8,128]{1,0:T(8,128)} %select_maximum_fusion.refs_0_), custom_call_target="tpu_custom_call" | custom-call | tf_op jit(solution)/shard_map/instance_coupling_0/pallas_call | solution.py:250
  38.1 0.8 subtract_multiply_fusion.4
  39.0 0.7 add_add_fusion.2
  39.6 0.7 fusion.66
  40.4 0.6 negate_bitcast_fusion.2
  41.0 0.7 constant_dynamic-slice_fusion
  42.4 2.4 %cosine_multiply_fusion = (f32[512,256]{1,0:T(8,128)S(1)}, f32[512,256]{1,0:T(8,128)S(1)}) fusion(f32[512,256]{1,0:T(8,128)S(1)} %get-tuple-element.41, f32[512]{0:T(512)S(1)} %broadcast_multiply_fusion, f32[512,256]{1,0:T(8,128)S(1)} %get-tuple-element.40), kind=kLoop, calls=%fused_computation.25 | loop fusion | flops 786432 | bytes 2099200 | tf_op jit(solution)/shard_map/mul | solution.py:389
  45.1 0.5 fusion.7
  45.7 0.6 reshape.517.rows_ref
  46.3 7.8 %inst_route.1 = f32[8,2,128]{2,1,0:T(2,128)} custom-call(f32[8,2,128]{2,1,0:T(2,128)} %reshape.517.rows_ref), custom_call_target="tpu_custom_call" | custom-call | tf_op jit(solution)/shard_map/inst_route/pallas_call | solution.py:331
  54.1 0.7 reduce-precision_convert_fusion.7
  54.8 1.6 %fusion.2 = f32[3,8,1024]{2,1,0:T(8,128)S(1)} fusion(s32[2048]{0:T(1024)S(1)} %get-tuple-element.191, bf16[1,8,2048]{2,1,0:T(8,128)(2,1)S(1)} %get-tuple-element.189, bf16[1,8,2048]{2,1,0:T(8,128)(2,1)S(1)} %get-tuple-element.188, bf16[1,8,2048]{2,1,0:T(8,128)(2,1)S(1)} %get-tuple-element.187), kind=kOutput, calls=%fused_computation.4 | convolution fusion | flops 102858752 | bytes 204800 | tf_op jit(solution)/shard_map/plq,qb->plb/dot_general | solution.py:123
  56.5 1.1 %reduce-precision_convert_fusion.3 = (bf16[1,40,1024]{2,1,0:T(8,128)(2,1)S(1)}, f32[5,8,1024]{2,1,0:T(8,128)S(1)}) fusion(f32[8,1024]{1,0:T(8,128)S(1)} %fusion.75, f32[1,8,1024]{2,1,0:T(8,128)S(1)} %broadcast.492, f32[3,8,1024]{2,1,0:T(8,128)S(1)} %get-tuple-element.184, f32[1,8,1024]{2,1,0:T(8,128)S(1)} %get-tuple-element.186, ...), kind=kLoop, calls=%fused_computation.54 | loop fusion | flops 778240 | bytes 1425408 | tf_op jit(solution)/shard_map/convert.3
  57.6 4.4 %convolution_bitcast_fusion.1 = f32[3,3,40,1024]{3,2,1,0:T(8,128)S(1)} fusion(bf16[1,1024,1024]{2,1,0:T(8,128)(2,1)} %copy-done.6, bf16[1,1024,1024]{2,1,0:T(8,128)(2,1)} %copy-done.8, bf16[1,1024,1024]{2,1,0:T(8,128)(2,1)} %copy-done.4, bf16[1,40,1024]{2,1,0:T(8,128)(2,1)S(1)} %get-tuple-element.149, bf16[1,40,1024]{2,1,0:T(8,128)(2,1)S(1)} %get-tuple-element.148, ...), kind=kOutput, calls=%fused_computation.15 | convolution fusion | flops 774586368 | bytes 8011776 | tf_op jit(solution)/shard_map/pra,kba->kprb/dot_general | solution.py:110
  62.2 0.7 slice_multiply_fusion.70
  62.9 14.7 %instance_coupling_1.1 = (f32[5,8,1024]{2,1,0:T(8,128)}, f32[5,1,1024]{2,1,0:T(1,128)}, f32[5,1,1024]{2,1,0:T(1,128)}) custom-call(f32[5,8,1024]{2,1,0:T(8,128)} %copy-done.1, f32[8]{0:T(128)} %compare_select_fusion.table_ref), custom_call_target="tpu_custom_call" | custom-call | tf_op jit(solution)/shard_map/instance_coupling_1/pallas_call | solution.py:250
  77.6 1.0 subtract_multiply_fusion.3
  78.7 1.1 add_add_fusion.1
  79.7 1.0 fusion.63
  80.8 0.8 multiply_reduce_fusion.1
  81.6 1.1 %reduce-precision_convert_fusion.1 = (bf16[1,40,1024]{2,1,0:T(8,128)(2,1)S(1)}, f32[5,8,1024]{2,1,0:T(8,128)S(1)}) fusion(f32[5,8,1024]{2,1,0:T(8,128)} %copy-done.1, f32[8,1024]{1,0:T(8,128)S(1)} %fusion.75, f32[1,8,1024]{2,1,0:T(8,128)S(1)} %broadcast.492, f32[3,8,1024]{2,1,0:T(8,128)S(1)} %get-tuple-element.184, f32[1,8,1024]{2,1,0:T(8,128)S(1)} %get-tuple-element.186, ...), kind=kLoop, calls=%fused_computation.50 | loop fusion | flops 778240 | bytes 1425408 | tf_op jit(solution)/shard_map/convert
  82.8 2.2 %convolution_bitcast_fusion = f32[3,3,40,1024]{3,2,1,0:T(8,128)S(1)} fusion(bf16[1,1024,1024]{2,1,0:T(8,128)(2,1)S(1)} %copy-done.7, bf16[1,1024,1024]{2,1,0:T(8,128)(2,1)S(1)} %copy-done.9, bf16[1,1024,1024]{2,1,0:T(8,128)(2,1)S(1)} %copy-done.5, bf16[1,40,1024]{2,1,0:T(8,128)(2,1)S(1)} %get-tuple-element.136, ...), kind=kOutput, calls=%fused_computation.14 | convolution fusion | flops 774586368 | bytes 8011776 | tf_op jit(solution)/shard_map/pra,kba->kprb/dot_general | solution.py:110
  85.2 20.2 %instance_coupling_2.1 = (f32[5,8,1024]{2,1,0:T(8,128)}, f32[5,1,1024]{2,1,0:T(1,128)}, f32[5,1,1024]{2,1,0:T(1,128)}) custom-call(f32[5,8,1024]{2,1,0:T(8,128)} %copy-done, f32[8]{0:T(128)} %compare_select_fusion.table_ref), custom_call_target="tpu_custom_call" | custom-call | tf_op jit(solution)/shard_map/instance_coupling_2/pallas_call | solution.py:250
  105.3 0.8 subtract_multiply_fusion.2
  106.4 1.8 %fusion.35 = f32[5,1,8,1024]{3,2,1,0:T(8,128)} fusion(f32[5,8,1024]{2,1,0:T(8,128)} %copy-done, f32[5,8,1024]{2,1,0:T(8,128)} %get-tuple-element.36, f32[3,1,40,1024]{3,2,1,0:T(8,128)S(1)} %slice_add_fusion, f32[1,8,1024]{2,1,0:T(8,128)S(1)} %negate_bitcast_fusion, f32[3,8,1024]{2,1,0:T(8,128)S(1)} %get-tuple-element.44, ...), kind=kLoop, calls=%fused_computation.71 | loop fusion | flops 696320 | bytes 1343488 | tf_op jit(solution)/shard_map/broadcast_in_dim | solution.py:427
  (87 shorter events, 2.2 us)
Async XLA Ops:
  4.2 2.8 %copy-start.2 = (f32[5,1,8,1024]{3,2,1,0:T(8,128)S(1)}, f32[5,1,8,1024]{3,2,1,0:T(8,128)}, u32[]{:S(2)}) copy-start(f32[5,1,8,1024]{3,2,1,0:T(8,128)} %param.14) | copy-start | bytes 491524
  7.0 2.4 %copy-start.4 = (bf16[1,1024,1024]{2,1,0:T(8,128)(2,1)}, bf16[1,1024,1024]{2,1,0:T(8,128)(2,1)S(1)}, u32[]{:S(2)}) copy-start(bf16[1,1024,1024]{2,1,0:T(8,128)(2,1)S(1)} %get-tuple-element.62) | copy-start | bytes 6291460
  7.0 2.4 %copy-start.6 = (bf16[1,1024,1024]{2,1,0:T(8,128)(2,1)}, bf16[1,1024,1024]{2,1,0:T(8,128)(2,1)S(1)}, u32[]{:S(2)}) copy-start(bf16[1,1024,1024]{2,1,0:T(8,128)(2,1)S(1)} %get-tuple-element.63) | copy-start | bytes 6291460
  7.0 2.6 %copy-start.8 = (bf16[1,1024,1024]{2,1,0:T(8,128)(2,1)}, bf16[1,1024,1024]{2,1,0:T(8,128)(2,1)S(1)}, u32[]{:S(2)}) copy-start(bf16[1,1024,1024]{2,1,0:T(8,128)(2,1)S(1)} %get-tuple-element.64) | copy-start | bytes 6291460
  7.1 2.6 %copy-start.10 = (f32[1,8,1024]{2,1,0:T(8,128)S(1)}, f32[1,8,1024]{2,1,0:T(8,128)}, u32[]{:S(2)}) copy-start(f32[1,8,1024]{2,1,0:T(8,128)} %param.15) | copy-start | bytes 98308
  7.1 2.6 %copy-start.16 = (f32[1,8,1024]{2,1,0:T(8,128)S(1)}, f32[1,8,1024]{2,1,0:T(8,128)}, u32[]{:S(2)}) copy-start(f32[1,8,1024]{2,1,0:T(8,128)} %param.17) | copy-start | bytes 98308
  7.1 3.3 %copy-start.22 = (s32[16]{0:T(128)S(1)}, s32[16]{0:T(128)}, u32[]{:S(2)}) copy-start(s32[16]{0:T(128)} %param.20) | copy-start | bytes 196
  7.1 3.3 %copy-start.19 = (f32[3,16]{1,0:T(4,128)S(1)}, f32[3,16]{1,0:T(4,128)}, u32[]{:S(2)}) copy-start(f32[3,16]{1,0:T(4,128)} %param.18) | copy-start | bytes 580
  7.1 3.3 %copy-start.20 = (f32[2,16]{1,0:T(2,128)S(1)}, f32[2,16]{1,0:T(2,128)}, u32[]{:S(2)}) copy-start(f32[2,16]{1,0:T(2,128)} %param.19) | copy-start | bytes 388
  7.1 30.9 %copy-start.3 = (f32[5,1,8,1024]{3,2,1,0:T(8,128)S(1)}, f32[5,1,8,1024]{3,2,1,0:T(8,128)}, u32[]{:S(2)}) copy-start(f32[5,1,8,1024]{3,2,1,0:T(8,128)} %param.14) | copy-start | bytes 491524
  9.6 30.1 %copy-start.18 = (pred[3]{0:T(512)(128)(4,1)S(1)}, pred[3]{0:T(512)(128)(4,1)}, u32[]{:S(2)}) copy-start(pred[3]{0:T(512)(128)(4,1)} %constant.102.clone.1) | copy-start | bytes 13
  9.7 32.7 %copy-start.12 = (f32[8,1024]{1,0:T(8,128)}, f32[8,1024]{1,0:T(8,128)S(1)}, u32[]{:S(2)}) copy-start(f32[8,1024]{1,0:T(8,128)S(1)} %get-tuple-element.185) | copy-start | bytes 98308
  11.0 34.0 %copy-start.21 = (f32[8]{0:T(128)S(1)}, f32[8]{0:T(128)}, u32[]{:S(2)}) copy-start(f32[8]{0:T(128)} %constant.121.clone) | copy-start | bytes 100
  38.0 3.7 %copy-start.15 = (f32[32,8,128]{2,1,0:T(8,128)S(1)}, f32[32,8,128]{2,1,0:T(8,128)}, u32[]{:S(2)}) copy-start(f32[32,8,128]{2,1,0:T(8,128)} %get-tuple-element.30) | copy-start | bytes 393220
  38.9 15.1 %copy-start.17 = (s32[2048]{0:T(1024)S(1)}, s32[2048]{0:T(1024)}, u32[]{:S(2)}) copy-start(s32[2048]{0:T(1024)} %param.23) | copy-start | bytes 24580
  44.8 11.6 %copy-start.14 = (f32[3,8,1024]{2,1,0:T(8,128)S(1)}, f32[3,8,1024]{2,1,0:T(8,128)}, u32[]{:S(2)}) copy-start(f32[3,8,1024]{2,1,0:T(8,128)} %get-tuple-element.56) | copy-start | bytes 294916
  57.5 5.4 %copy-start.1 = (f32[5,8,1024]{2,1,0:T(8,128)}, f32[5,8,1024]{2,1,0:T(8,128)S(1)}, u32[]{:S(2)}) copy-start(f32[5,8,1024]{2,1,0:T(8,128)S(1)} %get-tuple-element.53.psi_ref) | copy-start | bytes 491524
  62.1 20.6 %copy-start.5 = (bf16[1,1024,1024]{2,1,0:T(8,128)(2,1)S(1)}, bf16[1,1024,1024]{2,1,0:T(8,128)(2,1)}, u32[]{:S(2)}) copy-start(bf16[1,1024,1024]{2,1,0:T(8,128)(2,1)} %copy-done.4) | copy-start | bytes 6291460
  62.1 0.8 copy-start.11
  77.6 5.1 %copy-start.7 = (bf16[1,1024,1024]{2,1,0:T(8,128)(2,1)S(1)}, bf16[1,1024,1024]{2,1,0:T(8,128)(2,1)}, u32[]{:S(2)}) copy-start(bf16[1,1024,1024]{2,1,0:T(8,128)(2,1)} %copy-done.6) | copy-start | bytes 6291460
  77.6 5.1 %copy-start.9 = (bf16[1,1024,1024]{2,1,0:T(8,128)(2,1)S(1)}, bf16[1,1024,1024]{2,1,0:T(8,128)(2,1)}, u32[]{:S(2)}) copy-start(bf16[1,1024,1024]{2,1,0:T(8,128)(2,1)} %copy-done.8) | copy-start | bytes 6291460
  82.7 2.4 %copy-start = (f32[5,8,1024]{2,1,0:T(8,128)}, f32[5,8,1024]{2,1,0:T(8,128)S(1)}, u32[]{:S(2)}) copy-start(f32[5,8,1024]{2,1,0:T(8,128)S(1)} %get-tuple-element.47.psi_ref) | copy-start | bytes 491524
  85.0 21.4 %copy-start.13 = (f32[8,1024]{1,0:T(8,128)S(1)}, f32[8,1024]{1,0:T(8,128)}, u32[]{:S(2)}) copy-start(f32[8,1024]{1,0:T(8,128)} %copy-done.12) | copy-start | bytes 98308

commit v9 on v6

--- a/solution.py
+++ b/solution.py
@@ -154,13 +154,13 @@
     here = lax.axis_index("space")
     up, down = (here + 1) % slabs, (here + slabs - 1) % slabs
     if gather:
-        others = [(here + d) % slabs for d in range(1, slabs)]
-        greet_all([{"inst": p} for p in ring + partners] + [{"space": s} for s in others])
+        everyone = [(me + d) % count for d in range(1, count)]
+        greet_all([{"inst": p} for p in everyone] + [{"space": up}, {"space": down}])
         gathered = []
-        for slot, peer in enumerate(others):
+        for slot, peer in enumerate(everyone):
             copy = pltpu.make_async_remote_copy(
-                src_ref=block_ref, dst_ref=gheld.at[here], send_sem=gsend.at[slot],
-                recv_sem=grecv.at[slot], device_id={"space": peer},
+                src_ref=block_ref.at[peer], dst_ref=gheld.at[me], send_sem=gsend.at[slot],
+                recv_sem=grecv.at[slot], device_id={"inst": peer},
                 device_id_type=pl.DeviceIdType.MESH)
             copy.start()
             gathered.append(copy)
@@ -225,7 +225,7 @@
     if gather:
         for copy in gathered:
             copy.wait()
-        gheld[here] = block_ref[...]
+        gheld[me] = block_ref[me]
         stacked_ref[...] = gheld[...]
 
 
@@ -240,11 +240,11 @@
     edge = jax.ShapeDtypeStruct((comps, 1, plane), psi.dtype)
     extra_out, extra_scratch, operands = (), [], (psi, table)
     if gather:
-        extra_out = (jax.ShapeDtypeStruct((slabs, *block.shape), block.dtype),)
+        extra_out = (jax.ShapeDtypeStruct(block.shape, block.dtype),)
         extra_scratch = [
-            pltpu.VMEM((slabs, *block.shape), block.dtype),
-            pltpu.SemaphoreType.DMA((slabs - 1,)),
-            pltpu.SemaphoreType.DMA((slabs - 1,)),
+            pltpu.VMEM(block.shape, block.dtype),
+            pltpu.SemaphoreType.DMA((count - 1,)),
+            pltpu.SemaphoreType.DMA((count - 1,)),
         ]
         operands = (psi, table, block)
     return pl.pallas_call(
@@ -370,8 +370,7 @@
     row_entry = spectral_coeff(
         jnp.arange(inst_count, dtype=jnp.int32).astype(jnp.float32), float(inst_count)
     )
-    first = instance_coupling(psi, row_entry, 0, packed)
-    stacked = first[3]
+    stacked = space_gather(packed, ITERS)
     observers = stacked[:, :rows, :per].transpose(1, 0, 2).reshape(rows, -1)
     owned_count = panel_normal.shape[1]
     piece = owned_count // inst_count
@@ -394,7 +393,8 @@
         [real * cos_beat + imag * sin_beat, real * sin_beat - imag * cos_beat], axis=1
     )
     partial = jnp.dot(mixes, pairs, precision=lax.Precision.HIGHEST)
-    routed = inst_route(partial.reshape(inst_count, piece // 128, 128), ITERS + 1)
+    first = instance_coupling(psi, row_entry, 0, partial.reshape(inst_count, piece // 128, 128))
+    routed = first[3]
     weight = routed.reshape(owned_count)
     layers = psi_start.shape[2]
     plane = psi_start.shape[3]

time: 101 us -> 96.5 us (0.955)
  other arithmetic: 13.5 us -> 10.6 us
  Pallas kernels: 69.7 us -> 68 us
    pallas_call x3, Pallas kernels: 61.9 us -> 52.3 us  [instance_coupling(): pl.pallas_call(functools.partial(coupling_kernel, count, inner, gather),...]
    pallas_call x1, Pallas kernels: 7.78 us -> 15.8 us  [space_gather(): pl.pallas_call(functools.partial(gather_kernel, count), out_shape=jax.Sha...]
    another operation x6, other arithmetic: 2.08 us -> 0.47 us
    mul x2 -> x3, other arithmetic: 1.73 us -> 2.56 us  [shards(): 0.5 * (minus_a - plus_a)]
where the time goes in v9:
time: 96.5 us; the launch traced here: 95.7 us
  Pallas kernels  68 us (70%)
  matrix products  13 us (13%)
  other arithmetic  10.6 us (11%)
  local copies, waits for them, and re-layouts  3.45 us (4%)
    pallas_call x3, Pallas kernels, instance_coupling(): pl.pallas_call(functools.partial(coupling_kernel, count, inner, gather),...  52.3 us
    pallas_call x1, Pallas kernels, space_gather(): pl.pallas_call(functools.partial(gather_kernel, count), out_shape=jax.Sha...  15.8 us
    dot_general x3, matrix products, plane_gather(): jnp.einsum('pra,kba->kprb', parts, onehot, preferred_element_type=jnp.flo...  10.8 us
    mul x3, other arithmetic, shards(): 0.5 * (minus_a - plus_a)  2.56 us
    mul x1, other arithmetic, shards(): along * jnp.cos(lag)  2.39 us

profile of v9, /device:TPU:1, one launch (start us, length us, event | category | flops | bytes accessed | tf_op | source)
XLA Modules:
  0.0 95.7 jit_solution(17005834695740204080)
XLA Ops:
  0.0 0.7 constant_dynamic-slice_fusion
  0.7 0.7 convert_bitcast_fusion
  1.4 1.3 %select_maximum_fusion.block_ref = f32[8,128]{1,0:T(8,128)} fusion(f32[1,16]{1,0:T(1,128)S(1)} %convert_bitcast_fusion, f32[2,16]{1,0:T(2,128)} %param.19, f32[3,16]{1,0:T(4,128)} %param.18), kind=kLoop, calls=%fused_computation.248 | loop fusion | flops 11264 | bytes 4480 | tf_op jit(solution)/shard_map/concatenate | solution.py:363
  2.7 15.8 %space_gather.1 = f32[32,8,128]{2,1,0:T(8,128)} custom-call(f32[8,128]{1,0:T(8,128)} %select_maximum_fusion.block_ref), custom_call_target="tpu_custom_call" | custom-call | tf_op jit(solution)/shard_map/space_gather/pallas_call | solution.py:296
  18.5 0.9 slice_bitcast_fusion.12
  19.5 0.3 fusion.23
  19.8 0.1 slice_reduce_fusion.2
  20.1 2.4 %cosine_multiply_fusion = (f32[512,256]{1,0:T(8,128)S(1)}, f32[512,256]{1,0:T(8,128)S(1)}) fusion(f32[512,256]{1,0:T(8,128)S(1)} %get-tuple-element.41, f32[512]{0:T(512)S(1)} %broadcast_multiply_fusion, f32[512,256]{1,0:T(8,128)S(1)} %get-tuple-element.40), kind=kLoop, calls=%fused_computation.33 | loop fusion | flops 786432 | bytes 2099200 | tf_op jit(solution)/shard_map/mul | solution.py:388
  22.7 0.1 fusion.73
  22.8 0.5 fusion.25
  23.3 0.6 reshape.481.refs_0_
  24.0 0.6 compare_select_fusion.table_ref
  24.5 17.0 %instance_coupling_0.1 = (f32[5,8,1024]{2,1,0:T(8,128)}, f32[5,1,1024]{2,1,0:T(1,128)}, f32[5,1,1024]{2,1,0:T(1,128)}, f32[8,2,128]{2,1,0:T(2,128)}) custom-call(f32[5,8,1024]{2,1,0:T(8,128)} %bitcast.183, f32[8]{0:T(128)} %compare_select_fusion.table_ref, f32[8,2,128]{2,1,0:T(2,128)} %reshape.481.refs_0_), custom_call_target="tpu_custom_call" | custom-call | tf_op jit(solution)/shard_map/instance_coupling_0/pallas_call | solution.py:250
  41.6 0.8 subtract_multiply_fusion.8
  42.6 3.6 %fusion.14 = f32[4,3,40,1024]{3,2,1,0:T(8,128)S(1)} fusion(s32[4,1024]{1,0:T(4,128)S(1)} %copy-done.21, bf16[1,40,1024]{2,1,0:T(8,128)(2,1)S(1)} %get-tuple-element.160, bf16[1,40,1024]{2,1,0:T(8,128)(2,1)S(1)} %get-tuple-element.161, bf16[1,40,1024]{2,1,0:T(8,128)(2,1)S(1)} %get-tuple-element.159), kind=kOutput, calls=%fused_computation.14 | convolution fusion | flops 1011564544 | bytes 2228224 | tf_op jit(solution)/shard_map/pra,kba->kprb/dot_general | solution.py:110
  46.2 0.1 slice_add_fusion.4
  46.4 0.5 copy-done.16
  47.1 0.1 fusion.53
  47.3 1.6 %fusion.11 = f32[3,8,1024]{2,1,0:T(8,128)S(1)} fusion(s32[2048]{0:T(1024)S(1)} %get-tuple-element.188, bf16[1,8,2048]{2,1,0:T(8,128)(2,1)S(1)} %get-tuple-element.186, bf16[1,8,2048]{2,1,0:T(8,128)(2,1)S(1)} %get-tuple-element.185, bf16[1,8,2048]{2,1,0:T(8,128)(2,1)S(1)} %get-tuple-element.184), kind=kOutput, calls=%fused_computation.10 | convolution fusion | flops 102858752 | bytes 204800 | tf_op jit(solution)/shard_map/plq,qb->plb/dot_general | solution.py:123
  49.0 0.2 reduce-precision_convert_fusion.3
  49.2 3.6 %fusion.17 = f32[4,3,40,1024]{3,2,1,0:T(8,128)S(1)} fusion(s32[4,1024]{1,0:T(4,128)S(1)} %copy-done.21, bf16[1,40,1024]{2,1,0:T(8,128)(2,1)S(1)} %get-tuple-element.146, bf16[1,40,1024]{2,1,0:T(8,128)(2,1)S(1)} %get-tuple-element.145, bf16[1,40,1024]{2,1,0:T(8,128)(2,1)S(1)} %get-tuple-element.52), kind=kOutput, calls=%fused_computation.15 | convolution fusion | flops 1011564544 | bytes 2228224 | tf_op jit(solution)/shard_map/pra,kba->kprb/dot_general | solution.py:110
  52.8 0.1 slice_add_fusion.2
  53.0 19.9 %instance_coupling_1.1 = (f32[5,8,1024]{2,1,0:T(8,128)}, f32[5,1,1024]{2,1,0:T(1,128)}, f32[5,1,1024]{2,1,0:T(1,128)}) custom-call(f32[5,8,1024]{2,1,0:T(8,128)} %copy-done.2, f32[8]{0:T(128)} %compare_select_fusion.table_ref), custom_call_target="tpu_custom_call" | custom-call | tf_op jit(solution)/shard_map/instance_coupling_1/pallas_call | solution.py:250
  73.0 0.9 subtract_multiply_fusion.5
  74.0 0.1 fusion.50
  74.1 0.2 reduce-precision_convert_fusion.1
  74.4 3.7 %fusion.20 = f32[4,3,40,1024]{3,2,1,0:T(8,128)S(1)} fusion(s32[4,1024]{1,0:T(4,128)S(1)} %copy-done.21, bf16[1,40,1024]{2,1,0:T(8,128)(2,1)S(1)} %get-tuple-element.131, bf16[1,40,1024]{2,1,0:T(8,128)(2,1)S(1)} %get-tuple-element.130, bf16[1,40,1024]{2,1,0:T(8,128)(2,1)S(1)} %get-tuple-element.46), kind=kOutput, calls=%fused_computation.16 | convolution fusion | flops 1011564544 | bytes 2228224 | tf_op jit(solution)/shard_map/pra,kba->kprb/dot_general | solution.py:110
  78.1 0.1 slice_add_fusion
  78.4 15.3 %instance_coupling_2.1 = (f32[5,8,1024]{2,1,0:T(8,128)}, f32[5,1,1024]{2,1,0:T(1,128)}, f32[5,1,1024]{2,1,0:T(1,128)}) custom-call(f32[5,8,1024]{2,1,0:T(8,128)} %copy-done, f32[8]{0:T(128)} %compare_select_fusion.table_ref), custom_call_target="tpu_custom_call" | custom-call | tf_op jit(solution)/shard_map/instance_coupling_2/pallas_call | solution.py:250
  93.7 0.9 subtract_multiply_fusion.2
  94.7 0.1 fusion.47
  94.9 0.8 subtract_bitcast_fusion
  (83 shorter events, 1.3 us)
Async XLA Ops:
  18.4 4.2 %copy-start.20 = (f32[8]{0:T(128)S(1)}, f32[8]{0:T(128)}, u32[]{:S(2)}) copy-start(f32[8]{0:T(128)} %constant.121.clone) | copy-start | bytes 100
  19.8 21.8 %copy-start.4 = (f32[5,1,8,1024]{3,2,1,0:T(8,128)S(1)}, f32[5,1,8,1024]{3,2,1,0:T(8,128)}, u32[]{:S(2)}) copy-start(f32[5,1,8,1024]{3,2,1,0:T(8,128)} %param.14) | copy-start | bytes 491524
  20.1 22.4 %copy-start.5 = (f32[1,8,1024]{2,1,0:T(8,128)S(1)}, f32[1,8,1024]{2,1,0:T(8,128)}, u32[]{:S(2)}) copy-start(f32[1,8,1024]{2,1,0:T(8,128)} %param.15) | copy-start | bytes 98308
  20.1 22.4 %copy-start.9 = (f32[3,1,8,1024]{3,2,1,0:T(8,128)S(1)}, f32[3,1,8,1024]{3,2,1,0:T(8,128)}, u32[]{:S(2)}) copy-start(f32[3,1,8,1024]{3,2,1,0:T(8,128)} %param.16) | copy-start | bytes 294916
  22.5 20.1 %copy-start.21 = (s32[4,1024]{1,0:T(4,128)S(1)}, s32[4,1024]{1,0:T(4,128)}, u32[]{:S(2)}) copy-start(s32[4,1024]{1,0:T(4,128)} %param.24) | copy-start | bytes 49156
  46.2 0.8 copy-start.16
  46.3 0.8 copy-start.19
  46.4 0.9 copy-start.18
  46.4 0.9 copy-start.17
  47.1 1.9 %copy-start.7 = (f32[5,8,1024]{2,1,0:T(8,128)S(1)}, f32[5,8,1024]{2,1,0:T(8,128)}, u32[]{:S(2)}) copy-start(f32[5,8,1024]{2,1,0:T(8,128)} %get-tuple-element.29) | copy-start | bytes 491524
  47.1 1.9 %copy-start.10 = (f32[5,1,1024]{2,1,0:T(1,128)S(1)}, f32[5,1,1024]{2,1,0:T(1,128)}, u32[]{:S(2)}) copy-start(f32[5,1,1024]{2,1,0:T(1,128)} %get-tuple-element.27) | copy-start | bytes 61444
  47.1 1.9 %copy-start.11 = (f32[5,1,1024]{2,1,0:T(1,128)S(1)}, f32[5,1,1024]{2,1,0:T(1,128)}, u32[]{:S(2)}) copy-start(f32[5,1,1024]{2,1,0:T(1,128)} %get-tuple-element.28) | copy-start | bytes 61444
  49.1 3.8 %copy-start.2 = (f32[5,8,1024]{2,1,0:T(8,128)}, f32[5,8,1024]{2,1,0:T(8,128)S(1)}, u32[]{:S(2)}) copy-start(f32[5,8,1024]{2,1,0:T(8,128)S(1)} %get-tuple-element.53.psi_ref) | copy-start | bytes 491524
  53.0 21.1 %copy-start.3 = (f32[5,8,1024]{2,1,0:T(8,128)S(1)}, f32[5,8,1024]{2,1,0:T(8,128)}, u32[]{:S(2)}) copy-start(f32[5,8,1024]{2,1,0:T(8,128)} %copy-done.2) | copy-start | bytes 491524
  73.0 1.2 %copy-start.8 = (f32[5,8,1024]{2,1,0:T(8,128)S(1)}, f32[5,8,1024]{2,1,0:T(8,128)}, u32[]{:S(2)}) copy-start(f32[5,8,1024]{2,1,0:T(8,128)} %get-tuple-element.33) | copy-start | bytes 491524
  73.0 1.2 %copy-start.14 = (f32[5,1,1024]{2,1,0:T(1,128)S(1)}, f32[5,1,1024]{2,1,0:T(1,128)}, u32[]{:S(2)}) copy-start(f32[5,1,1024]{2,1,0:T(1,128)} %get-tuple-element.31) | copy-start | bytes 61444
  73.0 1.2 %copy-start.15 = (f32[5,1,1024]{2,1,0:T(1,128)S(1)}, f32[5,1,1024]{2,1,0:T(1,128)}, u32[]{:S(2)}) copy-start(f32[5,1,1024]{2,1,0:T(1,128)} %get-tuple-element.32) | copy-start | bytes 61444
  74.3 4.0 %copy-start = (f32[5,8,1024]{2,1,0:T(8,128)}, f32[5,8,1024]{2,1,0:T(8,128)S(1)}, u32[]{:S(2)}) copy-start(f32[5,8,1024]{2,1,0:T(8,128)S(1)} %get-tuple-element.47.psi_ref) | copy-start | bytes 491524
  78.4 16.5 %copy-start.1 = (f32[5,8,1024]{2,1,0:T(8,128)S(1)}, f32[5,8,1024]{2,1,0:T(8,128)}, u32[]{:S(2)}) copy-start(f32[5,8,1024]{2,1,0:T(8,128)} %copy-done) | copy-start | bytes 491524
  93.7 1.2 %copy-start.6 = (f32[5,8,1024]{2,1,0:T(8,128)S(1)}, f32[5,8,1024]{2,1,0:T(8,128)}, u32[]{:S(2)}) copy-start(f32[5,8,1024]{2,1,0:T(8,128)} %get-tuple-element.36) | copy-start | bytes 491524
  93.7 1.2 %copy-start.12 = (f32[5,1,1024]{2,1,0:T(1,128)S(1)}, f32[5,1,1024]{2,1,0:T(1,128)}, u32[]{:S(2)}) copy-start(f32[5,1,1024]{2,1,0:T(1,128)} %get-tuple-element.34) | copy-start | bytes 61444
  93.7 1.2 %copy-start.13 = (f32[5,1,1024]{2,1,0:T(1,128)S(1)}, f32[5,1,1024]{2,1,0:T(1,128)}, u32[]{:S(2)}) copy-start(f32[5,1,1024]{2,1,0:T(1,128)} %get-tuple-element.35) | copy-start | bytes 61444

commit v10 on v9

--- a/solution.py
+++ b/solution.py
@@ -147,8 +147,9 @@
     outer = count // inner
     me = lax.axis_index("inst")
     me_hi, me_lo = me // inner, me % inner
-    ring = [me_hi * inner + (me_lo + d) % inner for d in range(1, inner)]
-    ring_from = [me_hi * inner + (me_lo - d) % inner for d in range(1, inner)]
+    steps = sorted(range(1, inner), key=lambda d: -min(d, inner - d))
+    ring = [me_hi * inner + (me_lo + d) % inner for d in steps]
+    ring_from = [me_hi * inner + (me_lo - d) % inner for d in steps]
     partners = [((me_hi + h) % outer) * inner + me_lo for h in range(1, outer)]
     slabs = lax.axis_size("space")
     here = lax.axis_index("space")

time: 96.5 us -> 96.1 us (level)
  no operation moved by 1% of the time
where the time goes in v10:
time: 96.1 us; the launch traced here: 95.3 us
  Pallas kernels  67.7 us (70%)
  matrix products  13 us (14%)
  other arithmetic  10.6 us (11%)
  local copies, waits for them, and re-layouts  3.45 us (4%)
    pallas_call x3, Pallas kernels, instance_coupling(): pl.pallas_call(functools.partial(coupling_kernel, count, inner, gather),...  51.9 us
    pallas_call x1, Pallas kernels, space_gather(): pl.pallas_call(functools.partial(gather_kernel, count), out_shape=jax.Sha...  15.8 us
    dot_general x3, matrix products, plane_gather(): jnp.einsum('pra,kba->kprb', parts, onehot, preferred_element_type=jnp.flo...  10.8 us
    mul x3, other arithmetic, shards(): 0.5 * (minus_a - plus_a)  2.56 us
    mul x1, other arithmetic, shards(): along * jnp.cos(lag)  2.39 us

profile of v10, /device:TPU:1, one launch (start us, length us, event | category | flops | bytes accessed | tf_op | source)
XLA Modules:
  0.0 95.3 jit_solution(16284167644965444113)
XLA Ops:
  0.0 0.7 constant_dynamic-slice_fusion
  0.7 0.7 convert_bitcast_fusion
  1.4 1.3 %select_maximum_fusion.block_ref = f32[8,128]{1,0:T(8,128)} fusion(f32[1,16]{1,0:T(1,128)S(1)} %convert_bitcast_fusion, f32[2,16]{1,0:T(2,128)} %param.19, f32[3,16]{1,0:T(4,128)} %param.18), kind=kLoop, calls=%fused_computation.248 | loop fusion | flops 11264 | bytes 4480 | tf_op jit(solution)/shard_map/concatenate | solution.py:364
  2.7 15.8 %space_gather.1 = f32[32,8,128]{2,1,0:T(8,128)} custom-call(f32[8,128]{1,0:T(8,128)} %select_maximum_fusion.block_ref), custom_call_target="tpu_custom_call" | custom-call | tf_op jit(solution)/shard_map/space_gather/pallas_call | solution.py:297
  18.5 0.9 slice_bitcast_fusion.12
  19.5 0.3 fusion.23
  19.8 0.1 slice_reduce_fusion.2
  20.1 2.4 %cosine_multiply_fusion = (f32[512,256]{1,0:T(8,128)S(1)}, f32[512,256]{1,0:T(8,128)S(1)}) fusion(f32[512,256]{1,0:T(8,128)S(1)} %get-tuple-element.41, f32[512]{0:T(512)S(1)} %broadcast_multiply_fusion, f32[512,256]{1,0:T(8,128)S(1)} %get-tuple-element.40), kind=kLoop, calls=%fused_computation.33 | loop fusion | flops 786432 | bytes 2099200 | tf_op jit(solution)/shard_map/mul | solution.py:389
  22.7 0.1 fusion.73
  22.8 0.5 fusion.25
  23.3 0.6 reshape.481.refs_0_
  24.0 0.6 compare_select_fusion.table_ref
  24.5 17.0 %instance_coupling_0.1 = (f32[5,8,1024]{2,1,0:T(8,128)}, f32[5,1,1024]{2,1,0:T(1,128)}, f32[5,1,1024]{2,1,0:T(1,128)}, f32[8,2,128]{2,1,0:T(2,128)}) custom-call(f32[5,8,1024]{2,1,0:T(8,128)} %bitcast.183, f32[8]{0:T(128)} %compare_select_fusion.table_ref, f32[8,2,128]{2,1,0:T(2,128)} %reshape.481.refs_0_), custom_call_target="tpu_custom_call" | custom-call | tf_op jit(solution)/shard_map/instance_coupling_0/pallas_call | solution.py:251
  41.6 0.8 subtract_multiply_fusion.8
  42.6 3.6 %fusion.14 = f32[4,3,40,1024]{3,2,1,0:T(8,128)S(1)} fusion(s32[4,1024]{1,0:T(4,128)S(1)} %copy-done.21, bf16[1,40,1024]{2,1,0:T(8,128)(2,1)S(1)} %get-tuple-element.160, bf16[1,40,1024]{2,1,0:T(8,128)(2,1)S(1)} %get-tuple-element.161, bf16[1,40,1024]{2,1,0:T(8,128)(2,1)S(1)} %get-tuple-element.159), kind=kOutput, calls=%fused_computation.14 | convolution fusion | flops 1011564544 | bytes 2228224 | tf_op jit(solution)/shard_map/pra,kba->kprb/dot_general | solution.py:110
  46.1 0.1 slice_add_fusion.4
  46.3 0.5 copy-done.16
  47.1 0.1 fusion.53
  47.3 1.6 %fusion.11 = f32[3,8,1024]{2,1,0:T(8,128)S(1)} fusion(s32[2048]{0:T(1024)S(1)} %get-tuple-element.188, bf16[1,8,2048]{2,1,0:T(8,128)(2,1)S(1)} %get-tuple-element.186, bf16[1,8,2048]{2,1,0:T(8,128)(2,1)S(1)} %get-tuple-element.185, bf16[1,8,2048]{2,1,0:T(8,128)(2,1)S(1)} %get-tuple-element.184), kind=kOutput, calls=%fused_computation.10 | convolution fusion | flops 102858752 | bytes 204800 | tf_op jit(solution)/shard_map/plq,qb->plb/dot_general | solution.py:123
  48.9 0.2 reduce-precision_convert_fusion.3
  49.2 3.6 %fusion.17 = f32[4,3,40,1024]{3,2,1,0:T(8,128)S(1)} fusion(s32[4,1024]{1,0:T(4,128)S(1)} %copy-done.21, bf16[1,40,1024]{2,1,0:T(8,128)(2,1)S(1)} %get-tuple-element.146, bf16[1,40,1024]{2,1,0:T(8,128)(2,1)S(1)} %get-tuple-element.145, bf16[1,40,1024]{2,1,0:T(8,128)(2,1)S(1)} %get-tuple-element.52), kind=kOutput, calls=%fused_computation.15 | convolution fusion | flops 1011564544 | bytes 2228224 | tf_op jit(solution)/shard_map/pra,kba->kprb/dot_general | solution.py:110
  52.7 0.1 slice_add_fusion.2
  53.0 19.1 %instance_coupling_1.1 = (f32[5,8,1024]{2,1,0:T(8,128)}, f32[5,1,1024]{2,1,0:T(1,128)}, f32[5,1,1024]{2,1,0:T(1,128)}) custom-call(f32[5,8,1024]{2,1,0:T(8,128)} %copy-done.2, f32[8]{0:T(128)} %compare_select_fusion.table_ref), custom_call_target="tpu_custom_call" | custom-call | tf_op jit(solution)/shard_map/instance_coupling_1/pallas_call | solution.py:251
  72.2 0.9 subtract_multiply_fusion.5
  73.1 0.1 fusion.50
  73.3 0.2 reduce-precision_convert_fusion.1
  73.5 3.7 %fusion.20 = f32[4,3,40,1024]{3,2,1,0:T(8,128)S(1)} fusion(s32[4,1024]{1,0:T(4,128)S(1)} %copy-done.21, bf16[1,40,1024]{2,1,0:T(8,128)(2,1)S(1)} %get-tuple-element.131, bf16[1,40,1024]{2,1,0:T(8,128)(2,1)S(1)} %get-tuple-element.130, bf16[1,40,1024]{2,1,0:T(8,128)(2,1)S(1)} %get-tuple-element.46), kind=kOutput, calls=%fused_computation.16 | convolution fusion | flops 1011564544 | bytes 2228224 | tf_op jit(solution)/shard_map/pra,kba->kprb/dot_general | solution.py:110
  77.3 0.1 slice_add_fusion
  77.5 15.8 %instance_coupling_2.1 = (f32[5,8,1024]{2,1,0:T(8,128)}, f32[5,1,1024]{2,1,0:T(1,128)}, f32[5,1,1024]{2,1,0:T(1,128)}) custom-call(f32[5,8,1024]{2,1,0:T(8,128)} %copy-done, f32[8]{0:T(128)} %compare_select_fusion.table_ref), custom_call_target="tpu_custom_call" | custom-call | tf_op jit(solution)/shard_map/instance_coupling_2/pallas_call | solution.py:251
  93.4 0.9 subtract_multiply_fusion.2
  94.3 0.1 fusion.47
  94.5 0.8 subtract_bitcast_fusion
  (83 shorter events, 1.3 us)
Async XLA Ops:
  18.4 4.2 %copy-start.20 = (f32[8]{0:T(128)S(1)}, f32[8]{0:T(128)}, u32[]{:S(2)}) copy-start(f32[8]{0:T(128)} %constant.121.clone) | copy-start | bytes 100
  19.8 21.7 %copy-start.4 = (f32[5,1,8,1024]{3,2,1,0:T(8,128)S(1)}, f32[5,1,8,1024]{3,2,1,0:T(8,128)}, u32[]{:S(2)}) copy-start(f32[5,1,8,1024]{3,2,1,0:T(8,128)} %param.14) | copy-start | bytes 491524
  20.1 22.3 %copy-start.5 = (f32[1,8,1024]{2,1,0:T(8,128)S(1)}, f32[1,8,1024]{2,1,0:T(8,128)}, u32[]{:S(2)}) copy-start(f32[1,8,1024]{2,1,0:T(8,128)} %param.15) | copy-start | bytes 98308
  20.1 22.4 %copy-start.9 = (f32[3,1,8,1024]{3,2,1,0:T(8,128)S(1)}, f32[3,1,8,1024]{3,2,1,0:T(8,128)}, u32[]{:S(2)}) copy-start(f32[3,1,8,1024]{3,2,1,0:T(8,128)} %param.16) | copy-start | bytes 294916
  22.5 20.1 %copy-start.21 = (s32[4,1024]{1,0:T(4,128)S(1)}, s32[4,1024]{1,0:T(4,128)}, u32[]{:S(2)}) copy-start(s32[4,1024]{1,0:T(4,128)} %param.24) | copy-start | bytes 49156
  46.1 0.8 copy-start.16
  46.3 0.8 copy-start.19
  46.3 0.9 copy-start.18
  46.3 0.9 copy-start.17
  47.0 1.9 %copy-start.7 = (f32[5,8,1024]{2,1,0:T(8,128)S(1)}, f32[5,8,1024]{2,1,0:T(8,128)}, u32[]{:S(2)}) copy-start(f32[5,8,1024]{2,1,0:T(8,128)} %get-tuple-element.29) | copy-start | bytes 491524
  47.0 1.9 %copy-start.10 = (f32[5,1,1024]{2,1,0:T(1,128)S(1)}, f32[5,1,1024]{2,1,0:T(1,128)}, u32[]{:S(2)}) copy-start(f32[5,1,1024]{2,1,0:T(1,128)} %get-tuple-element.27) | copy-start | bytes 61444
  47.0 1.9 %copy-start.11 = (f32[5,1,1024]{2,1,0:T(1,128)S(1)}, f32[5,1,1024]{2,1,0:T(1,128)}, u32[]{:S(2)}) copy-start(f32[5,1,1024]{2,1,0:T(1,128)} %get-tuple-element.28) | copy-start | bytes 61444
  49.1 3.8 %copy-start.2 = (f32[5,8,1024]{2,1,0:T(8,128)}, f32[5,8,1024]{2,1,0:T(8,128)S(1)}, u32[]{:S(2)}) copy-start(f32[5,8,1024]{2,1,0:T(8,128)S(1)} %get-tuple-element.53.psi_ref) | copy-start | bytes 491524
  53.0 20.3 %copy-start.3 = (f32[5,8,1024]{2,1,0:T(8,128)S(1)}, f32[5,8,1024]{2,1,0:T(8,128)}, u32[]{:S(2)}) copy-start(f32[5,8,1024]{2,1,0:T(8,128)} %copy-done.2) | copy-start | bytes 491524
  72.1 1.2 %copy-start.8 = (f32[5,8,1024]{2,1,0:T(8,128)S(1)}, f32[5,8,1024]{2,1,0:T(8,128)}, u32[]{:S(2)}) copy-start(f32[5,8,1024]{2,1,0:T(8,128)} %get-tuple-element.33) | copy-start | bytes 491524
  72.1 1.2 %copy-start.14 = (f32[5,1,1024]{2,1,0:T(1,128)S(1)}, f32[5,1,1024]{2,1,0:T(1,128)}, u32[]{:S(2)}) copy-start(f32[5,1,1024]{2,1,0:T(1,128)} %get-tuple-element.31) | copy-start | bytes 61444
  72.2 1.2 %copy-start.15 = (f32[5,1,1024]{2,1,0:T(1,128)S(1)}, f32[5,1,1024]{2,1,0:T(1,128)}, u32[]{:S(2)}) copy-start(f32[5,1,1024]{2,1,0:T(1,128)} %get-tuple-element.32) | copy-start | bytes 61444
  73.5 4.0 %copy-start = (f32[5,8,1024]{2,1,0:T(8,128)}, f32[5,8,1024]{2,1,0:T(8,128)S(1)}, u32[]{:S(2)}) copy-start(f32[5,8,1024]{2,1,0:T(8,128)S(1)} %get-tuple-element.47.psi_ref) | copy-start | bytes 491524
  77.5 16.9 %copy-start.1 = (f32[5,8,1024]{2,1,0:T(8,128)S(1)}, f32[5,8,1024]{2,1,0:T(8,128)}, u32[]{:S(2)}) copy-start(f32[5,8,1024]{2,1,0:T(8,128)} %copy-done) | copy-start | bytes 491524
  93.3 1.2 %copy-start.6 = (f32[5,8,1024]{2,1,0:T(8,128)S(1)}, f32[5,8,1024]{2,1,0:T(8,128)}, u32[]{:S(2)}) copy-start(f32[5,8,1024]{2,1,0:T(8,128)} %get-tuple-element.36) | copy-start | bytes 491524
  93.3 1.2 %copy-start.12 = (f32[5,1,1024]{2,1,0:T(1,128)S(1)}, f32[5,1,1024]{2,1,0:T(1,128)}, u32[]{:S(2)}) copy-start(f32[5,1,1024]{2,1,0:T(1,128)} %get-tuple-element.34) | copy-start | bytes 61444
  93.3 1.2 %copy-start.13 = (f32[5,1,1024]{2,1,0:T(1,128)S(1)}, f32[5,1,1024]{2,1,0:T(1,128)}, u32[]{:S(2)}) copy-start(f32[5,1,1024]{2,1,0:T(1,128)} %get-tuple-element.35) | copy-start | bytes 61444

commit v11 on v10

--- a/solution.py
+++ b/solution.py
@@ -276,7 +276,8 @@
 
 def gather_kernel(count, block_ref, out_ref, held, send_sem, recv_sem):
     me = lax.axis_index("space")
-    peers = [(me + d) % count for d in range(1, count)]
+    steps = sorted(range(1, count), key=lambda d: -min(d, count - d))
+    peers = [(me + d) % count for d in steps]
     greet("space", peers)
     copies = []
     for slot, peer in enumerate(peers):

time: 96.1 us -> 96.3 us (level)
  no operation moved by 1% of the time
where the time goes in v11:
time: 96.3 us; the launch traced here: 95.4 us
  Pallas kernels  67.7 us (70%)
  matrix products  13 us (13%)
  other arithmetic  10.6 us (11%)
  local copies, waits for them, and re-layouts  3.45 us (4%)
    pallas_call x3, Pallas kernels, instance_coupling(): pl.pallas_call(functools.partial(coupling_kernel, count, inner, gather),...  51.9 us
    pallas_call x1, Pallas kernels, space_gather(): pl.pallas_call(functools.partial(gather_kernel, count), out_shape=jax.Sha...  15.8 us
    dot_general x3, matrix products, plane_gather(): jnp.einsum('pra,kba->kprb', parts, onehot, preferred_element_type=jnp.flo...  10.8 us
    mul x3, other arithmetic, shards(): 0.5 * (minus_a - plus_a)  2.56 us
    mul x1, other arithmetic, shards(): along * jnp.cos(lag)  2.39 us

profile of v11, /device:TPU:1, one launch (start us, length us, event | category | flops | bytes accessed | tf_op | source)
XLA Modules:
  0.0 95.4 jit_solution(5298932449550983772)
XLA Ops:
  0.0 0.7 constant_dynamic-slice_fusion
  0.7 0.7 convert_bitcast_fusion
  1.4 1.3 %select_maximum_fusion.block_ref = f32[8,128]{1,0:T(8,128)} fusion(f32[1,16]{1,0:T(1,128)S(1)} %convert_bitcast_fusion, f32[2,16]{1,0:T(2,128)} %param.19, f32[3,16]{1,0:T(4,128)} %param.18), kind=kLoop, calls=%fused_computation.248 | loop fusion | flops 11264 | bytes 4480 | tf_op jit(solution)/shard_map/concatenate | solution.py:365
  2.7 15.8 %space_gather.1 = f32[32,8,128]{2,1,0:T(8,128)} custom-call(f32[8,128]{1,0:T(8,128)} %select_maximum_fusion.block_ref), custom_call_target="tpu_custom_call" | custom-call | tf_op jit(solution)/shard_map/space_gather/pallas_call | solution.py:298
  18.5 0.9 slice_bitcast_fusion.12
  19.5 0.3 fusion.23
  19.8 0.1 slice_reduce_fusion.2
  20.1 2.4 %cosine_multiply_fusion = (f32[512,256]{1,0:T(8,128)S(1)}, f32[512,256]{1,0:T(8,128)S(1)}) fusion(f32[512,256]{1,0:T(8,128)S(1)} %get-tuple-element.41, f32[512]{0:T(512)S(1)} %broadcast_multiply_fusion, f32[512,256]{1,0:T(8,128)S(1)} %get-tuple-element.40), kind=kLoop, calls=%fused_computation.33 | loop fusion | flops 786432 | bytes 2099200 | tf_op jit(solution)/shard_map/mul | solution.py:390
  22.7 0.1 fusion.73
  22.8 0.5 fusion.25
  23.3 0.6 reshape.481.refs_0_
  24.0 0.6 compare_select_fusion.table_ref
  24.5 16.9 %instance_coupling_0.1 = (f32[5,8,1024]{2,1,0:T(8,128)}, f32[5,1,1024]{2,1,0:T(1,128)}, f32[5,1,1024]{2,1,0:T(1,128)}, f32[8,2,128]{2,1,0:T(2,128)}) custom-call(f32[5,8,1024]{2,1,0:T(8,128)} %bitcast.183, f32[8]{0:T(128)} %compare_select_fusion.table_ref, f32[8,2,128]{2,1,0:T(2,128)} %reshape.481.refs_0_), custom_call_target="tpu_custom_call" | custom-call | tf_op jit(solution)/shard_map/instance_coupling_0/pallas_call | solution.py:251
  41.5 0.8 subtract_multiply_fusion.8
  42.5 3.6 %fusion.14 = f32[4,3,40,1024]{3,2,1,0:T(8,128)S(1)} fusion(s32[4,1024]{1,0:T(4,128)S(1)} %copy-done.21, bf16[1,40,1024]{2,1,0:T(8,128)(2,1)S(1)} %get-tuple-element.160, bf16[1,40,1024]{2,1,0:T(8,128)(2,1)S(1)} %get-tuple-element.161, bf16[1,40,1024]{2,1,0:T(8,128)(2,1)S(1)} %get-tuple-element.159), kind=kOutput, calls=%fused_computation.14 | convolution fusion | flops 1011564544 | bytes 2228224 | tf_op jit(solution)/shard_map/pra,kba->kprb/dot_general | solution.py:110
  46.0 0.1 slice_add_fusion.4
  46.2 0.5 copy-done.16
  47.0 0.1 fusion.53
  47.2 1.6 %fusion.11 = f32[3,8,1024]{2,1,0:T(8,128)S(1)} fusion(s32[2048]{0:T(1024)S(1)} %get-tuple-element.188, bf16[1,8,2048]{2,1,0:T(8,128)(2,1)S(1)} %get-tuple-element.186, bf16[1,8,2048]{2,1,0:T(8,128)(2,1)S(1)} %get-tuple-element.185, bf16[1,8,2048]{2,1,0:T(8,128)(2,1)S(1)} %get-tuple-element.184), kind=kOutput, calls=%fused_computation.10 | convolution fusion | flops 102858752 | bytes 204800 | tf_op jit(solution)/shard_map/plq,qb->plb/dot_general | solution.py:123
  48.8 0.2 reduce-precision_convert_fusion.3
  49.1 3.6 %fusion.17 = f32[4,3,40,1024]{3,2,1,0:T(8,128)S(1)} fusion(s32[4,1024]{1,0:T(4,128)S(1)} %copy-done.21, bf16[1,40,1024]{2,1,0:T(8,128)(2,1)S(1)} %get-tuple-element.146, bf16[1,40,1024]{2,1,0:T(8,128)(2,1)S(1)} %get-tuple-element.145, bf16[1,40,1024]{2,1,0:T(8,128)(2,1)S(1)} %get-tuple-element.52), kind=kOutput, calls=%fused_computation.15 | convolution fusion | flops 1011564544 | bytes 2228224 | tf_op jit(solution)/shard_map/pra,kba->kprb/dot_general | solution.py:110
  52.6 0.1 slice_add_fusion.2
  52.9 19.3 %instance_coupling_1.1 = (f32[5,8,1024]{2,1,0:T(8,128)}, f32[5,1,1024]{2,1,0:T(1,128)}, f32[5,1,1024]{2,1,0:T(1,128)}) custom-call(f32[5,8,1024]{2,1,0:T(8,128)} %copy-done.2, f32[8]{0:T(128)} %compare_select_fusion.table_ref), custom_call_target="tpu_custom_call" | custom-call | tf_op jit(solution)/shard_map/instance_coupling_1/pallas_call | solution.py:251
  72.3 0.9 subtract_multiply_fusion.5
  73.2 0.1 fusion.50
  73.4 0.2 reduce-precision_convert_fusion.1
  73.6 3.7 %fusion.20 = f32[4,3,40,1024]{3,2,1,0:T(8,128)S(1)} fusion(s32[4,1024]{1,0:T(4,128)S(1)} %copy-done.21, bf16[1,40,1024]{2,1,0:T(8,128)(2,1)S(1)} %get-tuple-element.131, bf16[1,40,1024]{2,1,0:T(8,128)(2,1)S(1)} %get-tuple-element.130, bf16[1,40,1024]{2,1,0:T(8,128)(2,1)S(1)} %get-tuple-element.46), kind=kOutput, calls=%fused_computation.16 | convolution fusion | flops 1011564544 | bytes 2228224 | tf_op jit(solution)/shard_map/pra,kba->kprb/dot_general | solution.py:110
  77.4 0.1 slice_add_fusion
  77.6 15.7 %instance_coupling_2.1 = (f32[5,8,1024]{2,1,0:T(8,128)}, f32[5,1,1024]{2,1,0:T(1,128)}, f32[5,1,1024]{2,1,0:T(1,128)}) custom-call(f32[5,8,1024]{2,1,0:T(8,128)} %copy-done, f32[8]{0:T(128)} %compare_select_fusion.table_ref), custom_call_target="tpu_custom_call" | custom-call | tf_op jit(solution)/shard_map/instance_coupling_2/pallas_call | solution.py:251
  93.4 0.9 subtract_multiply_fusion.2
  94.3 0.1 fusion.47
  94.5 0.8 subtract_bitcast_fusion
  (83 shorter events, 1.3 us)
Async XLA Ops:
  18.4 4.2 %copy-start.20 = (f32[8]{0:T(128)S(1)}, f32[8]{0:T(128)}, u32[]{:S(2)}) copy-start(f32[8]{0:T(128)} %constant.121.clone) | copy-start | bytes 100
  19.8 21.6 %copy-start.4 = (f32[5,1,8,1024]{3,2,1,0:T(8,128)S(1)}, f32[5,1,8,1024]{3,2,1,0:T(8,128)}, u32[]{:S(2)}) copy-start(f32[5,1,8,1024]{3,2,1,0:T(8,128)} %param.14) | copy-start | bytes 491524
  20.1 22.2 %copy-start.5 = (f32[1,8,1024]{2,1,0:T(8,128)S(1)}, f32[1,8,1024]{2,1,0:T(8,128)}, u32[]{:S(2)}) copy-start(f32[1,8,1024]{2,1,0:T(8,128)} %param.15) | copy-start | bytes 98308
  20.1 22.3 %copy-start.9 = (f32[3,1,8,1024]{3,2,1,0:T(8,128)S(1)}, f32[3,1,8,1024]{3,2,1,0:T(8,128)}, u32[]{:S(2)}) copy-start(f32[3,1,8,1024]{3,2,1,0:T(8,128)} %param.16) | copy-start | bytes 294916
  22.5 20.0 %copy-start.21 = (s32[4,1024]{1,0:T(4,128)S(1)}, s32[4,1024]{1,0:T(4,128)}, u32[]{:S(2)}) copy-start(s32[4,1024]{1,0:T(4,128)} %param.24) | copy-start | bytes 49156
  46.0 0.8 copy-start.16
  46.2 0.8 copy-start.19
  46.2 0.9 copy-start.18
  46.2 0.9 copy-start.17
  46.9 1.9 %copy-start.7 = (f32[5,8,1024]{2,1,0:T(8,128)S(1)}, f32[5,8,1024]{2,1,0:T(8,128)}, u32[]{:S(2)}) copy-start(f32[5,8,1024]{2,1,0:T(8,128)} %get-tuple-element.29) | copy-start | bytes 491524
  46.9 1.9 %copy-start.10 = (f32[5,1,1024]{2,1,0:T(1,128)S(1)}, f32[5,1,1024]{2,1,0:T(1,128)}, u32[]{:S(2)}) copy-start(f32[5,1,1024]{2,1,0:T(1,128)} %get-tuple-element.27) | copy-start | bytes 61444
  46.9 1.9 %copy-start.11 = (f32[5,1,1024]{2,1,0:T(1,128)S(1)}, f32[5,1,1024]{2,1,0:T(1,128)}, u32[]{:S(2)}) copy-start(f32[5,1,1024]{2,1,0:T(1,128)} %get-tuple-element.28) | copy-start | bytes 61444
  49.0 3.8 %copy-start.2 = (f32[5,8,1024]{2,1,0:T(8,128)}, f32[5,8,1024]{2,1,0:T(8,128)S(1)}, u32[]{:S(2)}) copy-start(f32[5,8,1024]{2,1,0:T(8,128)S(1)} %get-tuple-element.53.psi_ref) | copy-start | bytes 491524
  52.9 20.5 %copy-start.3 = (f32[5,8,1024]{2,1,0:T(8,128)S(1)}, f32[5,8,1024]{2,1,0:T(8,128)}, u32[]{:S(2)}) copy-start(f32[5,8,1024]{2,1,0:T(8,128)} %copy-done.2) | copy-start | bytes 491524
  72.2 1.2 %copy-start.8 = (f32[5,8,1024]{2,1,0:T(8,128)S(1)}, f32[5,8,1024]{2,1,0:T(8,128)}, u32[]{:S(2)}) copy-start(f32[5,8,1024]{2,1,0:T(8,128)} %get-tuple-element.33) | copy-start | bytes 491524
  72.2 1.2 %copy-start.14 = (f32[5,1,1024]{2,1,0:T(1,128)S(1)}, f32[5,1,1024]{2,1,0:T(1,128)}, u32[]{:S(2)}) copy-start(f32[5,1,1024]{2,1,0:T(1,128)} %get-tuple-element.31) | copy-start | bytes 61444
  72.2 1.2 %copy-start.15 = (f32[5,1,1024]{2,1,0:T(1,128)S(1)}, f32[5,1,1024]{2,1,0:T(1,128)}, u32[]{:S(2)}) copy-start(f32[5,1,1024]{2,1,0:T(1,128)} %get-tuple-element.32) | copy-start | bytes 61444
  73.6 4.0 %copy-start = (f32[5,8,1024]{2,1,0:T(8,128)}, f32[5,8,1024]{2,1,0:T(8,128)S(1)}, u32[]{:S(2)}) copy-start(f32[5,8,1024]{2,1,0:T(8,128)S(1)} %get-tuple-element.47.psi_ref) | copy-start | bytes 491524
  77.6 16.9 %copy-start.1 = (f32[5,8,1024]{2,1,0:T(8,128)S(1)}, f32[5,8,1024]{2,1,0:T(8,128)}, u32[]{:S(2)}) copy-start(f32[5,8,1024]{2,1,0:T(8,128)} %copy-done) | copy-start | bytes 491524
  93.3 1.2 %copy-start.6 = (f32[5,8,1024]{2,1,0:T(8,128)S(1)}, f32[5,8,1024]{2,1,0:T(8,128)}, u32[]{:S(2)}) copy-start(f32[5,8,1024]{2,1,0:T(8,128)} %get-tuple-element.36) | copy-start | bytes 491524
  93.4 1.2 %copy-start.12 = (f32[5,1,1024]{2,1,0:T(1,128)S(1)}, f32[5,1,1024]{2,1,0:T(1,128)}, u32[]{:S(2)}) copy-start(f32[5,1,1024]{2,1,0:T(1,128)} %get-tuple-element.34) | copy-start | bytes 61444
  93.4 1.2 %copy-start.13 = (f32[5,1,1024]{2,1,0:T(1,128)S(1)}, f32[5,1,1024]{2,1,0:T(1,128)}, u32[]{:S(2)}) copy-start(f32[5,1,1024]{2,1,0:T(1,128)} %get-tuple-element.35) | copy-start | bytes 61444
